TPU v7x, 32 devices: a whole 2x2x4 slice. The times are simulated.
32 devices in a mesh: grp: 4 (over z), mem: 8 (over y, x, core).
Axes of the slice: x: 2, y: 2, z: 4, core: 2. Of those that a mesh axis runs over, the one named last changes fastest.
Arguments:
- bin_sketch: bfloat16 [256, 1024], P(('grp', 'mem')), may hold values from -6 to 6
- rep_sketch: bfloat16 [8192, 1024], P(('grp', 'mem')), may hold values from -6 to 6
- bin_profile: bfloat16 [256, 32768], P('grp', 'mem'), may hold values from -6 to 6
- member_profile: bfloat16 [12, 256, 32768], P('grp', None, 'mem'), may hold values from -6 to 6
- bin_routes: int32 [256, 2], P('grp'), may hold values from 0 to 11, all different within a row; in each aligned block of 64 rows (0 to 63, 64 to 127, ...) at most 16 rows name the same one
- owner_slot: int32 [12], replicated, may hold values from 0 to 11, each once
- cluster_sizes: int32 [12], replicated, may hold values from 128 to 256, as said below
Outputs:
- coarse_scores: bfloat16 [256, 8192], P(None, ('grp', 'mem'))
- fine_scores: float32 [256, 2, 256], P('grp', None, 'mem')
Inputs may be any that keep to these rules, and one draw needn't show every extreme that they name: `bin_routes`: within the bins of one index of grp (64 consecutive bins), no cluster is named by more than 16 routes, a bound that some block reaches; the two clusters of a bin differ. `owner_slot`: A permutation. `cluster_sizes`: each a multiple of 128.
All inputs are finite; a program needn't handle non-finite values.
Results may differ from a plain program's by a relative error of at most 0.001.
Values may be sent and summed in bfloat16 or wider, within the bound.
No kernel may reach another device: no remote copies, remote signals or barrier semaphores. Data moves between devices by JAX's collectives and lax.ppermute only.
A program may use at most 128 MiB of HBM per device.

v0:
```python
import jax
import jax.numpy as jnp
from jax import lax
from jax.sharding import PartitionSpec as P

FW = 32768
MOST = 16


def local(
    bin_sketch, rep_sketch, bin_profile, member_profile, bin_routes, owner_slot, cluster_sizes
):
    coarse_scale = bin_sketch.shape[1] ** (-0.5)
    group_rows = lax.all_gather(bin_sketch, "mem", axis=0, tiled=True)
    product = lax.dot_general(
        lax.all_gather(group_rows, "grp", axis=0, tiled=True),
        rep_sketch,
        (((1,), (1,)), ((), ())),
        preferred_element_type=jnp.float32,
    )
    coarse_scores = (product * coarse_scale).astype(jnp.bfloat16)
    rows_here, width_here = bin_profile.shape
    slot_count, members, _ = member_profile.shape
    groups = lax.axis_size("grp")
    cluster_total = owner_slot.shape[0]
    capacity = groups * slot_count * MOST
    route_flat = bin_routes.reshape(-1)
    cluster_ids = jnp.arange(cluster_total, dtype=jnp.int32)
    route_hit = (route_flat[:, None] == cluster_ids[None, :]).astype(jnp.int32)
    storage = jnp.sum(route_hit * owner_slot[None, :], axis=1)
    route_size = jnp.sum(route_hit * cluster_sizes[None, :], axis=1)
    route_rank = jnp.sum((jnp.cumsum(route_hit, axis=0) - route_hit) * route_hit, axis=1)
    slot_index = storage * MOST + route_rank
    source = bin_profile[jnp.arange(route_flat.shape[0], dtype=jnp.int32) // 2]
    outgoing = jnp.zeros((capacity, width_here), jnp.bfloat16).at[slot_index].set(source)
    outgoing = outgoing.reshape(groups, slot_count * MOST, width_here)
    incoming = lax.all_to_all(outgoing, "grp", split_axis=0, concat_axis=0, tiled=True)
    incoming = incoming.reshape(groups, slot_count, MOST, width_here)
    partial_value = jnp.einsum(
        "gsmc,sjc->gsmj", incoming, member_profile, preferred_element_type=jnp.float32
    )
    summed = lax.psum_scatter(partial_value, "mem", scatter_dimension=3, tiled=True)
    returned = lax.all_to_all(summed, "grp", split_axis=0, concat_axis=0, tiled=True)
    member_local = returned.shape[3]
    route_scores = returned.reshape(capacity, member_local)[slot_index] * FW ** (-0.5)
    column = lax.axis_index("mem") * member_local + jnp.arange(member_local, dtype=jnp.int32)
    member_live = column[None, :] < route_size[:, None]
    fine_scores = jnp.where(member_live, route_scores, 0.0).reshape(rows_here, 2, member_local)
    return (coarse_scores, fine_scores)


def solution(mesh):
    return jax.shard_map(
        local,
        mesh=mesh,
        in_specs=(
            P(("grp", "mem"), None),
            P(("grp", "mem"), None),
            P("grp", "mem"),
            P("grp", None, "mem"),
            P("grp", None),
            P(),
            P(),
        ),
        out_specs=(P(None, ("grp", "mem")), P("grp", None, "mem")),
        check_vma=False,
    )
```

profile of v0, /device:TPU:0, one launch (start us, length us, event | category | flops | bytes accessed | tf_op | source)
XLA Modules:
  0.0 133.0 jit_solution(8496143700417119367)
XLA Ops:
  7.2 0.8 copy.17
  8.0 0.1 eq.15
  8.3 0.2 reduce_window_sum.11
  8.4 0.9 select_reduce_fusion.2
  9.3 6.4 %scatter_custom_fusion = bf16[192,4096]{1,0:T(8,128)(2,1)} fusion(s32[128]{0:T(128)S(1)} %fusion.14, bf16[64,4096]{1,0:T(8,128)(2,1)S(1)} %copy-done, s32[1024]{0:T(1024)S(1)} %pad_clamp_fusion.1, bf16[]{:T(256)} %constant.36.clone.1), kind=kCustom, calls=%fused_computation.9 | custom fusion | bytes 1572866 | tf_op jit(solution)/shard_map/scatter | solution.py:35
  15.7 6.5 %all-to-all-start = ((bf16[4,48,4096]{2,1,0:T(8,128)(2,1)}), bf16[4,48,4096]{2,1,0:T(8,128)(2,1)S(1)}, u32[]{:S(2)}, u32[]{:S(2)}) async-start(bf16[4,48,4096]{2,1,0:T(8,128)(2,1)} %bitcast.3), calls=%async_computation | async-start | bytes 3145728 | tf_op jit(solution)/shard_map/all_to_all | solution.py:37
  22.2 9.2 %all_gather.6 = bf16[64,1024]{1,0:T(8,128)(2,1)S(1)} all-gather(bf16[8,1024]{1,0:T(8,128)(2,1)S(1)} %copy-done.2), channel_id=1, replica_groups=mesh['grp'=4,'mem'=8] {'mem'}, dimensions={0}, use_global_device_ids=true | all-gather | bytes 147456 | tf_op jit(solution)/shard_map/all_gather | solution.py:14
  31.4 38.1 %all_gather.7 = bf16[256,1024]{1,0:T(8,128)(2,1)S(1)} all-gather(bf16[64,1024]{1,0:T(8,128)(2,1)S(1)} %all_gather.6), channel_id=1, replica_groups=mesh['grp'=4,'mem'=8] {'grp'}, dimensions={0}, use_global_device_ids=true | all-gather | bytes 655360 | tf_op jit(solution)/shard_map/all_gather | solution.py:16
  69.5 4.8 %fusion.4 = f32[4,3,16,256]{3,2,0,1:T(8,128)S(1)} fusion(bf16[3,256,4096]{2,1,0:T(8,128)(2,1)} %param.10, bf16[4,3,16,4096]{3,2,1,0:T(8,128)(2,1)S(1)} %bitcast.25), kind=kOutput, calls=%fused_computation.8 | convolution fusion | flops 402653184 | bytes 8060928 | tf_op jit(solution)/shard_map/gsmc,sjc->gsmj/dot_general | solution.py:39
  74.4 0.7 copy.23
  75.1 1.5 %reshape.132 = f32[256,192]{1,0:T(8,128)} reshape(f32[256,3,4,16]{3,2,1,0:T(4,128)S(1)} %bitcast.24) | data formatting | bytes 393216
  76.6 1.0 fusion.3
  77.6 33.7 %reduce-scatter.4.cloned.1.call-done = f32[32,192]{1,0:T(8,128)} async-done(((f32[256,192]{1,0:T(8,128)}), f32[32,192]{1,0:T(8,128)}) %reduce-scatter.4.cloned.1.call-update) | async-done | bytes 24592
  111.4 0.9 reshape.133
  112.3 0.1 copy.20
  112.4 0.7 reshape.140
  113.1 4.6 %all-to-all-start.1 = ((f32[4,1,1536]{2,1,0:T(1,128)}), f32[4,1,1536]{2,1,0:T(1,128)S(1)}, u32[]{:S(2)}, u32[]{:S(2)}) async-start(f32[4,1,1536]{2,1,0:T(1,128)} %reshape.140), calls=%async_computation.1 | async-start | bytes 49152 | tf_op jit(solution)/shard_map/all_to_all | solution.py:43
  117.7 0.1 lt.38
  117.9 5.4 %all-to-all-done.1 = f32[4,1,1536]{2,1,0:T(1,128)S(1)} async-done(((f32[4,1,1536]{2,1,0:T(1,128)}), f32[4,1,1536]{2,1,0:T(1,128)S(1)}, u32[]{:S(2)}, u32[]{:S(2)}) %all-to-all-start.1) | async-done | bytes 24608 | tf_op jit(solution)/shard_map/all_to_all | solution.py:43
  123.4 0.5 broadcast.125
  123.9 0.7 reduce
  124.6 0.1 reshape.141
  124.7 0.6 gather_fusion
  125.4 0.7 compare_select_fusion
  (18 shorter events, 0.3 us)
Async XLA Ops:
  7.2 2.2 %copy-start = (bf16[64,4096]{1,0:T(8,128)(2,1)S(1)}, bf16[64,4096]{1,0:T(8,128)(2,1)}, u32[]{:S(2)}) copy-start(bf16[64,4096]{1,0:T(8,128)(2,1)} %param.9) | copy-start | bytes 1572868
  15.7 6.5 %copy-start.2 = (bf16[8,1024]{1,0:T(8,128)(2,1)S(1)}, bf16[8,1024]{1,0:T(8,128)(2,1)}, u32[]{:S(2)}) copy-start(bf16[8,1024]{1,0:T(8,128)(2,1)} %param.7) | copy-start | bytes 49156
  15.7 53.8 %all-to-all-start = ((bf16[4,48,4096]{2,1,0:T(8,128)(2,1)}), bf16[4,48,4096]{2,1,0:T(8,128)(2,1)S(1)}, u32[]{:S(2)}, u32[]{:S(2)}) async-start(bf16[4,48,4096]{2,1,0:T(8,128)(2,1)} %bitcast.3), calls=%async_computation | async-start | bytes 3145728 | tf_op jit(solution)/shard_map/all_to_all | solution.py:37
  22.2 89.2 %reduce-scatter.4.cloned.1.call-start = ((), (), s32[]{:S(2)}) async-start(), calls=%async_computation.3 | async-start | bytes 294912
  74.4 2.3 %copy-start.1 = (bf16[256,1024]{1,0:T(8,128)(2,1)S(1)}, bf16[256,1024]{1,0:T(8,128)(2,1)}, u32[]{:S(2)}) copy-start(bf16[256,1024]{1,0:T(8,128)(2,1)} %param.8) | copy-start | bytes 1572868
  113.1 10.2 %all-to-all-start.1 = ((f32[4,1,1536]{2,1,0:T(1,128)}), f32[4,1,1536]{2,1,0:T(1,128)S(1)}, u32[]{:S(2)}, u32[]{:S(2)}) async-start(f32[4,1,1536]{2,1,0:T(1,128)} %reshape.140), calls=%async_computation.1 | async-start | bytes 49152 | tf_op jit(solution)/shard_map/all_to_all | solution.py:43
Sparse Core Ops, SparseCore 0:
  76.7 34.6 reduce-scatter.3
where the time goes:
time: 133 us
  blocking collectives  47.3 us (36%)
  waiting for transfers between devices  39.2 us (29%)
  between operations  14.1 us (11%)
  local copies, waits for them, and re-layouts  12.8 us (10%)
  starting transfers between devices  11.1 us (8%)
  matrix products  5.81 us (4%)
  other arithmetic  2.59 us (2%)
    all_gather x1, blocking collectives, local(): lax.all_gather(group_rows, 'grp', axis=0, tiled=True)  38.1 us
    unnamed x2, waiting for transfers between devices  33.8 us
    all_gather x1, blocking collectives, local(): group_rows = lax.all_gather(bin_sketch, 'mem', axis=0, tiled=True)  9.22 us
    all_to_all x1, starting transfers between devices, local(): lax.all_to_all(outgoing, 'grp', split_axis=0, concat_axis=0, tiled=True)  6.48 us
    scatter x1, local copies, waits for them, and re-layouts, local(): jnp.zeros((capacity, width_here), jnp.bfloat16).at[slot_index].set(source)  6.38 us
    all_to_all x1, waiting for transfers between devices, local(): lax.all_to_all(summed, 'grp', split_axis=0, concat_axis=0, tiled=True)  5.43 us
    dot_general x1, matrix products, local(): jnp.einsum('gsmc,sjc->gsmj', incoming, member_profile, preferred_element_...  4.81 us
    unnamed x12, local copies, waits for them, and re-layouts  4.76 us
  transfers between devices with their start and end apart: 3, of which 2 were waited for; matrix products, arithmetic and copies ran while one was open for 1% of the time, Pallas kernels for 0%

commit v1 on v0

v1 whole, which is shorter than its diff:
```python
import jax
import jax.numpy as jnp
from jax import lax
from jax.sharding import PartitionSpec as P

FW = 32768
MOST = 16


def pick(hit, rows):
    return lax.dot_general(
        hit.astype(jnp.bfloat16),
        rows,
        (((1,), (0,)), ((), ())),
        preferred_element_type=jnp.float32,
    ).astype(jnp.bfloat16)


def make_local(groups, mems):
    last = groups - 1
    half = groups // 2
    middle = (half - 1, half) if groups > 1 else ()

    def swap(value, key):
        return lax.ppermute(value, "grp", [(i, i ^ key) for i in range(groups)])

    def local(
        bin_sketch, rep_sketch, bin_profile, member_profile, bin_routes, owner_slot, cluster_sizes
    ):
        rows_here, width_here = bin_profile.shape
        slot_count, members, _ = member_profile.shape
        per_group = slot_count * MOST
        me = lax.axis_index("grp")
        mine = lax.axis_index("mem")
        inner = (me == half - 1) | (me == half)

        whole = lax.ppermute(
            bin_profile, "grp", [(i, i ^ last) for i in range(groups) if i in middle]
        )

        cluster_ids = jnp.arange(owner_slot.shape[0], dtype=jnp.int32)
        route_flat = bin_routes.T.reshape(-1)
        route_hit = (route_flat[None, :] == cluster_ids[:, None]).astype(jnp.int32)
        storage = jnp.sum(route_hit * owner_slot[:, None], axis=0)
        route_size = jnp.sum(route_hit * cluster_sizes[:, None], axis=0)
        route_rank = jnp.sum((jnp.cumsum(route_hit, axis=1) - route_hit) * route_hit, axis=0)
        place = (storage * MOST + route_rank).reshape(2, rows_here)
        place_other = swap(place, last)

        local_place = jnp.arange(per_group, dtype=jnp.int32)[:, None]

        def chosen(where, group, rows):
            wanted = local_place + group * per_group
            return pick((where[0][None] == wanted) | (where[1][None] == wanted), rows)

        def scores(rows):
            split = rows.reshape(slot_count, MOST, width_here)
            out = lax.dot_general(
                member_profile,
                split,
                (((2,), (2,)), ((0,), (0,))),
                preferred_element_type=jnp.float32,
            )
            return out.transpose(1, 0, 2).reshape(members, per_group)

        def reduce_mem(value):
            step = 1
            block = members // mems
            value = value.reshape(mems, block, value.shape[1])
            while step < mems:
                bit = (mine // step) % 2
                pairs = value.reshape(value.shape[0] // 2, 2, block, value.shape[2])
                keep = lax.dynamic_index_in_dim(pairs, bit, 1, keepdims=False)
                send = lax.dynamic_index_in_dim(pairs, 1 - bit, 1, keepdims=False)
                got = lax.ppermute(send, "mem", [(i, i ^ step) for i in range(mems)])
                value = keep + got
                step *= 2
            return value.reshape(block, -1)

        sent = {}
        for key in range(1, half):
            sent[key] = swap(chosen(place, me ^ key, bin_profile), key)
        if groups > 1:
            outer = [(i, i ^ last) for i in range(groups) if i not in middle]
            direct = lax.ppermute(chosen(place, me ^ last, bin_profile), "grp", outer)
            sent[last] = jnp.where(inner, chosen(place_other, me, whole), direct)
        for key in range(half, last):
            there = jnp.where(inner, me ^ last ^ key, me ^ key)
            block = jnp.where(inner, whole, bin_profile)
            where = jnp.where(inner, place_other, place)
            route = [(i, i ^ last ^ key if i in middle else i ^ key) for i in range(groups)]
            sent[key] = lax.ppermute(chosen(where, there, block), "grp", route)
        sent[0] = chosen(place, me, bin_profile)

        sketches = lax.all_gather(bin_sketch, "grp", axis=0)
        sketches = lax.all_gather(sketches, "mem", axis=0)
        product = lax.dot_general(
            sketches.transpose(1, 0, 2, 3).reshape(-1, sketches.shape[3]),
            rep_sketch,
            (((1,), (1,)), ((), ())),
            preferred_element_type=jnp.float32,
        )
        coarse_scores = (product * bin_sketch.shape[1] ** (-0.5)).astype(jnp.bfloat16)

        early = [k for k in range(groups) if k < half]
        late = [k for k in range(groups) if k >= half]
        back = {}
        for keys in (early, late):
            if keys:
                summed = reduce_mem(jnp.concatenate([scores(sent[k]) for k in keys], axis=1))
                for at, k in enumerate(keys):
                    part = summed[:, at * per_group : (at + 1) * per_group]
                    back[k] = swap(part, k) if k else part
        table = jnp.concatenate([back[k] for k in range(groups)], axis=1)

        owner = place // per_group
        column = (owner ^ me) * per_group + place % per_group
        ids = jnp.arange(groups * per_group, dtype=jnp.int32)[:, None]
        found = (column.reshape(-1)[None, :] == ids).astype(jnp.float32)
        raw = lax.dot_general(
            table,
            found,
            (((1,), (0,)), ((), ())),
            precision=lax.Precision.HIGHEST,
            preferred_element_type=jnp.float32,
        )
        member_local = table.shape[0]
        member = mine * member_local + jnp.arange(member_local, dtype=jnp.int32)
        live = member[:, None] < route_size[None, :]
        fine = jnp.where(live, raw * FW ** (-0.5), 0.0)
        fine_scores = fine.reshape(member_local, 2, rows_here).transpose(2, 1, 0)
        return (coarse_scores, fine_scores)

    return local


def solution(mesh):
    return jax.shard_map(
        make_local(mesh.shape["grp"], mesh.shape["mem"]),
        mesh=mesh,
        in_specs=(
            P(("grp", "mem"), None),
            P(("grp", "mem"), None),
            P("grp", "mem"),
            P("grp", None, "mem"),
            P("grp", None),
            P(),
            P(),
        ),
        out_specs=(P(None, ("grp", "mem")), P("grp", None, "mem")),
        check_vma=False,
    )
```

time: 133 us -> 93.3 us (0.70)
  waiting for transfers between devices: 39.2 us -> 13.8 us
  matrix products: 5.81 us -> 26.4 us
  blocking collectives: 47.3 us -> 29.4 us
  between operations: 14.1 us -> 0.96 us
  local copies, waits for them, and re-layouts: 12.8 us -> 3.87 us
  starting transfers between devices: 11.1 us -> 17.1 us
  other arithmetic: 2.59 us -> 1.15 us
    unnamed x2 -> x0, waiting for transfers between devices: 33.8 us -> none
    dot_general x2 -> x11, matrix products: 5.81 us -> 26.4 us  [the longest x4 18 us: scores(): lax.dot_general(member_profile, split, (((2,), (2,)), ((0,), (0,))), pref...]
    all_gather x2, blocking collectives: 47.3 us -> 29.4 us  [the longest x1 19.6 us: local(): sketches = lax.all_gather(bin_sketch, 'grp', axis=0)]
    ppermute x0 -> x14, starting transfers between devices: none -> 17.1 us  [the longest x5 8.47 us: swap(): return lax.ppermute(value, 'grp', [(i, i ^ key) for i in range(groups)])]
    ppermute x0 -> x14, waiting for transfers between devices: none -> 13.8 us  [the longest x6 4.77 us: reduce_mem(): got = lax.ppermute(send, 'mem', [(i, i ^ step) for i in range(mems)])]
    all_to_all x2 -> x0, starting transfers between devices: 11.1 us -> none  [the longest x1 6.48 us: local(): lax.all_to_all(outgoing, 'grp', split_axis=0, concat_axis=0, tiled=True)]
    scatter x1 -> x0, local copies, waits for them, and re-layouts: 6.38 us -> none  [local(): jnp.zeros((capacity, width_here), jnp.bfloat16).at[slot_index].set(source)]
    all_to_all x2 -> x0, waiting for transfers between devices: 5.43 us -> none  [the longest x1 5.43 us: local(): lax.all_to_all(summed, 'grp', split_axis=0, concat_axis=0, tiled=True)]
  transfers between devices with their start and end apart: 3 -> 14, of which waited for: 2 -> 6; matrix products, arithmetic and copies ran while one was open for 1% -> 25% of each run, Pallas kernels for 0% -> 0%
where the time goes in v1:
time: 93.3 us; the launch traced here: 92.8 us
  blocking collectives  29.4 us (32%)
  matrix products  26.4 us (28%)
  starting transfers between devices  17.1 us (18%)
  waiting for transfers between devices  13.8 us (15%)
  local copies, waits for them, and re-layouts  3.87 us (4%)
  other arithmetic  1.15 us (1%)
  between operations  0.96 us (1%)
    all_gather x1, blocking collectives, local(): sketches = lax.all_gather(bin_sketch, 'grp', axis=0)  19.6 us
    dot_general x4, matrix products, scores(): lax.dot_general(member_profile, split, (((2,), (2,)), ((0,), (0,))), pref...  18 us
    all_gather x1, blocking collectives, local(): sketches = lax.all_gather(sketches, 'mem', axis=0)  9.84 us
    ppermute x5, starting transfers between devices, swap(): return lax.ppermute(value, 'grp', [(i, i ^ key) for i in range(groups)])  8.47 us
    dot_general x5, matrix products, pick(): lax.dot_general(hit.astype(jnp.bfloat16), rows, (((1,), (0,)), ((), ())),...  7.13 us
    ppermute x6, starting transfers between devices, reduce_mem(): got = lax.ppermute(send, 'mem', [(i, i ^ step) for i in range(mems)])  5.23 us
    ppermute x6, waiting for transfers between devices, reduce_mem(): got = lax.ppermute(send, 'mem', [(i, i ^ step) for i in range(mems)])  4.77 us
    ppermute x1, waiting for transfers between devices, local(): sent[key] = lax.ppermute(chosen(where, there, block), 'grp', route)  4.76 us
  transfers between devices with their start and end apart: 14, of which 6 were waited for; matrix products, arithmetic and copies ran while one was open for 25% of the time, Pallas kernels for 0%

profile of v1, /device:TPU:0, one launch (start us, length us, event | category | flops | bytes accessed | tf_op | source)
XLA Modules:
  0.0 92.8 jit_solution(1475851250506103937)
XLA Ops:
  2.6 5.1 %collective-permute-start.5 = (s32[2,64]{1,0:T(2,128)S(1)}, s32[2,64]{1,0:T(2,128)S(1)}, u32[]{:S(2)}, u32[]{:S(2)}) collective-permute-start(s32[2,64]{1,0:T(2,128)S(1)} %add.172), channel_id=1, source_target_pairs={{0,24},{8,16},{16,8},{24,0},{1,25},{9,17},{17,9},{25,1},{2,26},{10... | collective-permute-start | bytes 1544 | tf_op jit(solution)/shard_map/ppermute | solution.py:25
  8.5 2.1 %convolution_convert_fusion = bf16[48,4096]{1,0:T(8,128)(2,1)} fusion(bf16[64,4096]{1,0:T(8,128)(2,1)} %param.9, s32[64]{0:T(128)S(1)} %get-tuple-element.20, s32[64]{0:T(128)S(1)} %get-tuple-element.19, s32[48]{0:T(128)S(1)} %iota_add_fusion), kind=kOutput, calls=%fused_computation | convolution fusion | flops 25371648 | bytes 918208 | tf_op jit(solution)/shard_map/dot_general | solution.py:11
  10.6 1.9 %collective-permute-start.8 = (bf16[48,4096]{1,0:T(8,128)(2,1)}, bf16[48,4096]{1,0:T(8,128)(2,1)}, u32[]{:S(2)}, u32[]{:S(2)}) collective-permute-start(bf16[48,4096]{1,0:T(8,128)(2,1)} %convolution_convert_fusion), channel_id=1, source_target_pairs={{0,24},{24,0},{1,25},{25,1},{2,26},{26,2},{3,27},{27,3},{4,28},{28... | collective-permute-start | bytes 1179656 | tf_op jit(solution)/shard_map/ppermute | solution.py:85
  12.5 2.1 %convolution_convert_fusion.3 = bf16[48,4096]{1,0:T(8,128)(2,1)} fusion(bf16[64,4096]{1,0:T(8,128)(2,1)} %param.9, s32[64]{0:T(128)S(1)} %get-tuple-element.20, s32[64]{0:T(128)S(1)} %get-tuple-element.19, s32[48]{0:T(128)S(1)} %iota_add_fusion.2), kind=kOutput, calls=%fused_computation.3 | convolution fusion | flops 25371648 | bytes 918208 | tf_op jit(solution)/shard_map/dot_general | solution.py:11
  15.3 1.3 %convolution_convert_fusion.4 = bf16[48,4096]{1,0:T(8,128)(2,1)S(1)} fusion(bf16[64,4096]{1,0:T(8,128)(2,1)} %param.9, s32[64]{0:T(128)S(1)} %get-tuple-element.20, s32[64]{0:T(128)S(1)} %get-tuple-element.19, s32[48]{0:T(128)S(1)} %iota_add_fusion.3), kind=kOutput, calls=%fused_computation.4 | convolution fusion | flops 25371648 | bytes 918208 | tf_op jit(solution)/shard_map/dot_general | solution.py:11
  16.6 4.5 %convolution_bitcast_fusion.3 = f32[256,3,16]{0,2,1:T(8,128)S(1)} fusion(bf16[3,16,4096]{2,1,0:T(8,128)(2,1)S(1)} %bitcast.74, bf16[3,256,4096]{2,1,0:T(8,128)(2,1)} %param.10), kind=kOutput, calls=%fused_computation.11 | convolution fusion | flops 100663296 | bytes 6733824 | tf_op jit(solution)/shard_map/dot_general | solution.py:58
  21.4 19.6 %all-gather = bf16[32,1024]{1,0:T(8,128)(2,1)S(1)} all-gather(bf16[8,1024]{1,0:T(8,128)(2,1)S(1)} %copy-done.2), channel_id=2, replica_groups=mesh['grp'=4,'mem'=8] {'grp'}, dimensions={0}, use_global_device_ids=true | all-gather | bytes 81920 | tf_op jit(solution)/shard_map/all_gather | solution.py:95
  41.0 9.8 %all-gather.1 = bf16[32,8,1024]{2,1,0:T(8,128)(2,1)S(1)} all-gather(bf16[4,8,1024]{2,1,0:T(8,128)(2,1)S(1)} %bitcast.81), channel_id=3, replica_groups=mesh['grp'=4,'mem'=8] {'mem'}, dimensions={0}, use_global_device_ids=true | all-gather | bytes 589824 | tf_op jit(solution)/shard_map/all_gather | solution.py:96
  51.0 4.5 %convolution_bitcast_fusion.2 = f32[256,3,16]{0,2,1:T(8,128)S(1)} fusion(bf16[3,16,4096]{2,1,0:T(8,128)(2,1)S(1)} %bitcast.75, bf16[3,256,4096]{2,1,0:T(8,128)(2,1)} %param.10), kind=kOutput, calls=%fused_computation.10 | convolution fusion | flops 100663296 | bytes 6733824 | tf_op jit(solution)/shard_map/dot_general | solution.py:58
  56.0 0.8 collective-permute-start.7
  56.9 1.3 %fusion = bf16[48,4096]{1,0:T(8,128)(2,1)S(1)} fusion(bf16[48,4096]{1,0:T(8,128)(2,1)} %collective-permute-done.8, bf16[64,4096]{1,0:T(8,128)(2,1)S(1)} %collective-permute-done.6, pred[]{:T(512)S(6)} %or.20, s32[64]{0:T(128)S(1)} %get-tuple-element.16, s32[64]{0:T(128)S(1)} %get-tuple-element.15, s32[48]{0:T(128)S(1)} %iota_add_fusion.3), kind=kOutput, calls=%fused_computation.5 | convolution fusion | flops 25568256 | bytes 1311425 | tf_op jit(solution)/shard_map/dot_general | solution.py:11
  58.2 4.5 %convolution_bitcast_fusion = f32[256,3,16]{0,2,1:T(8,128)S(1)} fusion(bf16[3,16,4096]{2,1,0:T(8,128)(2,1)S(1)} %bitcast.73, bf16[3,256,4096]{2,1,0:T(8,128)(2,1)} %param.10), kind=kOutput, calls=%fused_computation.8 | convolution fusion | flops 100663296 | bytes 6733824 | tf_op jit(solution)/shard_map/dot_general | solution.py:58
  62.9 4.8 %collective-permute-done.7 = bf16[48,4096]{1,0:T(8,128)(2,1)S(1)} collective-permute-done((bf16[48,4096]{1,0:T(8,128)(2,1)S(1)}, bf16[48,4096]{1,0:T(8,128)(2,1)S(1)}, u32[]{:S(2)}, u32[]{:S(2)}) %collective-permute-start.7) | collective-permute-done | bytes 393248 | tf_op jit(solution)/shard_map/ppermute | solution.py:92
  67.7 4.5 %convolution_bitcast_fusion.1 = f32[256,3,16]{0,2,1:T(8,128)S(1)} fusion(bf16[3,16,4096]{2,1,0:T(8,128)(2,1)S(1)} %bitcast.76, bf16[3,256,4096]{2,1,0:T(8,128)(2,1)} %param.10), kind=kOutput, calls=%fused_computation.9 | convolution fusion | flops 100663296 | bytes 6733824 | tf_op jit(solution)/shard_map/dot_general | solution.py:58
  73.3 1.0 %fusion.1 = bf16[256,256]{1,0:T(8,128)(2,1)} fusion(bf16[256,1024]{1,0:T(8,128)(2,1)S(1)} %bitcast.71, bf16[256,1024]{1,0:T(8,128)(2,1)S(1)} %copy-done), kind=kOutput, calls=%fused_computation.7 | convolution fusion | flops 134348800 | bytes 1179648 | tf_op jit(solution)/shard_map/dot_general | solution.py:97
  75.2 1.6 %collective-permute-start.2 = (f32[2,32,96]{2,1,0:T(8,128)S(1)}, f32[2,32,96]{2,1,0:T(8,128)S(1)}, u32[]{:S(2)}, u32[]{:S(2)}) collective-permute-start(f32[2,32,96]{2,1,0:T(8,128)S(1)} %dynamic-slice_bitcast_fusion.1), channel_id=1, source_target_pairs={{0,2},{1,3},{2,0},{3,1},{4,6},{5,7},{6,4},{7,5},{8,10},{9,11},{10,... | collective-permute-start | bytes 73736 | tf_op jit(solution)/shard_map/ppermute | solution.py:75
  77.5 1.6 %collective-permute-done.2 = f32[2,32,96]{2,1,0:T(8,128)S(1)} collective-permute-done((f32[2,32,96]{2,1,0:T(8,128)S(1)}, f32[2,32,96]{2,1,0:T(8,128)S(1)}, u32[]{:S(2)}, u32[]{:S(2)}) %collective-permute-start.2) | collective-permute-done | bytes 24608 | tf_op jit(solution)/shard_map/ppermute | solution.py:75
  79.2 1.7 %collective-permute-start.3 = (f32[1,32,96]{2,1,0:T(8,128)S(1)}, f32[1,32,96]{2,1,0:T(8,128)S(1)}, u32[]{:S(2)}, u32[]{:S(2)}) collective-permute-start(f32[1,32,96]{2,1,0:T(8,128)S(1)} %constant_dynamic-slice_fusion.3), channel_id=1, source_target_pairs={{0,4},{1,5},{2,6},{3,7},{4,0},{5,1},{6,2},{7,3},{8,12},{9,13},{10,... | collective-permute-start | bytes 36872 | tf_op jit(solution)/shard_map/ppermute | solution.py:75
  81.5 1.5 %collective-permute-done.3 = f32[1,32,96]{2,1,0:T(8,128)S(1)} collective-permute-done((f32[1,32,96]{2,1,0:T(8,128)S(1)}, f32[1,32,96]{2,1,0:T(8,128)S(1)}, u32[]{:S(2)}, u32[]{:S(2)}) %collective-permute-start.3) | collective-permute-done | bytes 12320 | tf_op jit(solution)/shard_map/ppermute | solution.py:75
  83.1 1.7 %collective-permute-done.11 = f32[1,32,96]{2,1,0:T(8,128)S(1)} collective-permute-done((f32[1,32,96]{2,1,0:T(8,128)S(1)}, f32[1,32,96]{2,1,0:T(8,128)S(1)}, u32[]{:S(2)}, u32[]{:S(2)}) %collective-permute-start.11) | collective-permute-done | bytes 12320 | tf_op jit(solution)/shard_map/ppermute | solution.py:75
  84.8 1.5 %collective-permute-start.12 = (f32[32,48]{1,0:T(8,128)S(1)}, f32[32,48]{1,0:T(8,128)S(1)}, u32[]{:S(2)}, u32[]{:S(2)}) collective-permute-start(f32[32,48]{1,0:T(8,128)S(1)} %get-tuple-element.13), channel_id=1, source_target_pairs={{0,16},{8,24},{16,0},{24,8},{1,17},{9,25},{17,1},{25,9},{2,18},{10... | collective-permute-start | bytes 18440 | tf_op jit(solution)/shard_map/ppermute | solution.py:25
  86.3 1.2 %collective-permute-start.13 = (f32[32,48]{1,0:T(8,128)S(1)}, f32[32,48]{1,0:T(8,128)S(1)}, u32[]{:S(2)}, u32[]{:S(2)}) collective-permute-start(f32[32,48]{1,0:T(8,128)S(1)} %get-tuple-element.14), channel_id=1, source_target_pairs={{0,24},{8,16},{16,8},{24,0},{1,25},{9,17},{17,9},{25,1},{2,26},{10... | collective-permute-start | bytes 18440 | tf_op jit(solution)/shard_map/ppermute | solution.py:25
  87.5 1.9 %collective-permute-done.12 = f32[32,48]{1,0:T(8,128)S(1)} collective-permute-done((f32[32,48]{1,0:T(8,128)S(1)}, f32[32,48]{1,0:T(8,128)S(1)}, u32[]{:S(2)}, u32[]{:S(2)}) %collective-permute-start.12) | collective-permute-done | bytes 6176 | tf_op jit(solution)/shard_map/ppermute | solution.py:25
  89.5 2.4 %collective-permute-done.13 = f32[32,48]{1,0:T(8,128)S(1)} collective-permute-done((f32[32,48]{1,0:T(8,128)S(1)}, f32[32,48]{1,0:T(8,128)S(1)}, u32[]{:S(2)}, u32[]{:S(2)}) %collective-permute-start.13) | collective-permute-done | bytes 6176 | tf_op jit(solution)/shard_map/ppermute | solution.py:25
  (66 shorter events, 8.9 us)
Async XLA Ops:
  0.6 72.6 %copy-start = (bf16[256,1024]{1,0:T(8,128)(2,1)S(1)}, bf16[256,1024]{1,0:T(8,128)(2,1)}, u32[]{:S(2)}) copy-start(bf16[256,1024]{1,0:T(8,128)(2,1)} %param.8) | copy-start | bytes 1572868
  0.6 20.7 %copy-start.2 = (bf16[8,1024]{1,0:T(8,128)(2,1)S(1)}, bf16[8,1024]{1,0:T(8,128)(2,1)}, u32[]{:S(2)}) copy-start(bf16[8,1024]{1,0:T(8,128)(2,1)} %param.7) | copy-start | bytes 49156
  2.6 48.3 %collective-permute-start.5 = (s32[2,64]{1,0:T(2,128)S(1)}, s32[2,64]{1,0:T(2,128)S(1)}, u32[]{:S(2)}, u32[]{:S(2)}) collective-permute-start(s32[2,64]{1,0:T(2,128)S(1)} %add.172), channel_id=1, source_target_pairs={{0,24},{8,16},{16,8},{24,0},{1,25},{9,17},{17,9},{25,1},{2,26},{10... | collective-permute-start | bytes 1544 | tf_op jit(solution)/shard_map/ppermute | solution.py:25
  7.7 48.0 %collective-permute-start.6 = (bf16[64,4096]{1,0:T(8,128)(2,1)}, bf16[64,4096]{1,0:T(8,128)(2,1)S(1)}, u32[]{:S(2)}, u32[]{:S(2)}) collective-permute-start(bf16[64,4096]{1,0:T(8,128)(2,1)} %param.9), channel_id=1, source_target_pairs={{8,16},{16,8},{9,17},{17,9},{10,18},{18,10},{11,19},{19,11},{12,20... | collective-permute-start | bytes 1572872 | tf_op jit(solution)/shard_map/ppermute | solution.py:37
  10.6 46.3 %collective-permute-start.8 = (bf16[48,4096]{1,0:T(8,128)(2,1)}, bf16[48,4096]{1,0:T(8,128)(2,1)}, u32[]{:S(2)}, u32[]{:S(2)}) collective-permute-start(bf16[48,4096]{1,0:T(8,128)(2,1)} %convolution_convert_fusion), channel_id=1, source_target_pairs={{0,24},{24,0},{1,25},{25,1},{2,26},{26,2},{3,27},{27,3},{4,28},{28... | collective-permute-start | bytes 1179656 | tf_op jit(solution)/shard_map/ppermute | solution.py:85
  14.6 36.3 %collective-permute-start = (bf16[48,4096]{1,0:T(8,128)(2,1)}, bf16[48,4096]{1,0:T(8,128)(2,1)S(1)}, u32[]{:S(2)}, u32[]{:S(2)}) collective-permute-start(bf16[48,4096]{1,0:T(8,128)(2,1)} %convolution_convert_fusion.3), channel_id=1, source_target_pairs={{0,8},{8,0},{16,24},{24,16},{1,9},{9,1},{17,25},{25,17},{2,10},{10... | collective-permute-start | bytes 1179656 | tf_op jit(solution)/shard_map/ppermute | solution.py:25
  21.2 34.6 %copy-start.1 = (bf16[64,4096]{1,0:T(8,128)(2,1)S(1)}, bf16[64,4096]{1,0:T(8,128)(2,1)}, u32[]{:S(2)}) copy-start(bf16[64,4096]{1,0:T(8,128)(2,1)} %param.9) | copy-start | bytes 1572868
  56.0 11.6 %collective-permute-start.7 = (bf16[48,4096]{1,0:T(8,128)(2,1)S(1)}, bf16[48,4096]{1,0:T(8,128)(2,1)S(1)}, u32[]{:S(2)}, u32[]{:S(2)}) collective-permute-start(bf16[48,4096]{1,0:T(8,128)(2,1)S(1)} %convolution_convert_fusion.2), channel_id=1, source_target_pairs={{0,16},{8,0},{16,24},{24,8},{1,17},{9,1},{17,25},{25,9},{2,18},{10... | collective-permute-start | bytes 1179656 | tf_op jit(solution)/shard_map/ppermute | solution.py:92
  73.2 1.9 %collective-permute-start.1 = (f32[4,32,96]{2,1,0:T(8,128)S(1)}, f32[4,32,96]{2,1,0:T(8,128)S(1)}, u32[]{:S(2)}, u32[]{:S(2)}) collective-permute-start(f32[4,32,96]{2,1,0:T(8,128)S(1)} %bitcast.82), channel_id=1, source_target_pairs={{0,1},{1,0},{2,3},{3,2},{4,5},{5,4},{6,7},{7,6},{8,9},{9,8},{10,11... | collective-permute-start | bytes 147464 | tf_op jit(solution)/shard_map/ppermute | solution.py:75
  74.5 2.3 %collective-permute-start.9 = (f32[4,32,96]{2,1,0:T(8,128)S(1)}, f32[4,32,96]{2,1,0:T(8,128)S(1)}, u32[]{:S(2)}, u32[]{:S(2)}) collective-permute-start(f32[4,32,96]{2,1,0:T(8,128)S(1)} %bitcast.83), channel_id=1, source_target_pairs={{0,1},{1,0},{2,3},{3,2},{4,5},{5,4},{6,7},{7,6},{8,9},{9,8},{10,11... | collective-permute-start | bytes 147464 | tf_op jit(solution)/shard_map/ppermute | solution.py:75
  75.2 4.0 %collective-permute-start.2 = (f32[2,32,96]{2,1,0:T(8,128)S(1)}, f32[2,32,96]{2,1,0:T(8,128)S(1)}, u32[]{:S(2)}, u32[]{:S(2)}) collective-permute-start(f32[2,32,96]{2,1,0:T(8,128)S(1)} %dynamic-slice_bitcast_fusion.1), channel_id=1, source_target_pairs={{0,2},{1,3},{2,0},{3,1},{4,6},{5,7},{6,4},{7,5},{8,10},{9,11},{10,... | collective-permute-start | bytes 73736 | tf_op jit(solution)/shard_map/ppermute | solution.py:75
  76.8 4.1 %collective-permute-start.10 = (f32[2,32,96]{2,1,0:T(8,128)S(1)}, f32[2,32,96]{2,1,0:T(8,128)S(1)}, u32[]{:S(2)}, u32[]{:S(2)}) collective-permute-start(f32[2,32,96]{2,1,0:T(8,128)S(1)} %dynamic-slice_bitcast_fusion), channel_id=1, source_target_pairs={{0,2},{1,3},{2,0},{3,1},{4,6},{5,7},{6,4},{7,5},{8,10},{9,11},{10,... | collective-permute-start | bytes 73736 | tf_op jit(solution)/shard_map/ppermute | solution.py:75
  79.2 3.8 %collective-permute-start.3 = (f32[1,32,96]{2,1,0:T(8,128)S(1)}, f32[1,32,96]{2,1,0:T(8,128)S(1)}, u32[]{:S(2)}, u32[]{:S(2)}) collective-permute-start(f32[1,32,96]{2,1,0:T(8,128)S(1)} %constant_dynamic-slice_fusion.3), channel_id=1, source_target_pairs={{0,4},{1,5},{2,6},{3,7},{4,0},{5,1},{6,2},{7,3},{8,12},{9,13},{10,... | collective-permute-start | bytes 36872 | tf_op jit(solution)/shard_map/ppermute | solution.py:75
  80.9 3.8 %collective-permute-start.11 = (f32[1,32,96]{2,1,0:T(8,128)S(1)}, f32[1,32,96]{2,1,0:T(8,128)S(1)}, u32[]{:S(2)}, u32[]{:S(2)}) collective-permute-start(f32[1,32,96]{2,1,0:T(8,128)S(1)} %constant_dynamic-slice_fusion), channel_id=1, source_target_pairs={{0,4},{1,5},{2,6},{3,7},{4,0},{5,1},{6,2},{7,3},{8,12},{9,13},{10,... | collective-permute-start | bytes 36872 | tf_op jit(solution)/shard_map/ppermute | solution.py:75
  83.0 4.5 %collective-permute-start.4 = (f32[32,48]{1,0:T(8,128)S(1)}, f32[32,48]{1,0:T(8,128)S(1)}, u32[]{:S(2)}, u32[]{:S(2)}) collective-permute-start(f32[32,48]{1,0:T(8,128)S(1)} %get-tuple-element.12), channel_id=1, source_target_pairs={{0,8},{8,0},{16,24},{24,16},{1,9},{9,1},{17,25},{25,17},{2,10},{10... | collective-permute-start | bytes 18440 | tf_op jit(solution)/shard_map/ppermute | solution.py:25
  84.8 4.6 %collective-permute-start.12 = (f32[32,48]{1,0:T(8,128)S(1)}, f32[32,48]{1,0:T(8,128)S(1)}, u32[]{:S(2)}, u32[]{:S(2)}) collective-permute-start(f32[32,48]{1,0:T(8,128)S(1)} %get-tuple-element.13), channel_id=1, source_target_pairs={{0,16},{8,24},{16,0},{24,8},{1,17},{9,25},{17,1},{25,9},{2,18},{10... | collective-permute-start | bytes 18440 | tf_op jit(solution)/shard_map/ppermute | solution.py:25
  86.3 5.5 %collective-permute-start.13 = (f32[32,48]{1,0:T(8,128)S(1)}, f32[32,48]{1,0:T(8,128)S(1)}, u32[]{:S(2)}, u32[]{:S(2)}) collective-permute-start(f32[32,48]{1,0:T(8,128)S(1)} %get-tuple-element.14), channel_id=1, source_target_pairs={{0,24},{8,16},{16,8},{24,0},{1,25},{9,17},{17,9},{25,1},{2,26},{10... | collective-permute-start | bytes 18440 | tf_op jit(solution)/shard_map/ppermute | solution.py:25

commit v2 on v0

v2 whole, which is shorter than its diff:
```python
import functools

import jax
import jax.numpy as jnp
from jax import lax
from jax.experimental import pallas as pl
from jax.experimental.pallas import tpu as pltpu
from jax.sharding import PartitionSpec as P

FW = 32768
MOST = 16
VM = pl.BlockSpec(memory_space=pltpu.VMEM)
SM = pl.BlockSpec(memory_space=pltpu.SMEM)
NT = (((1,), (1,)), ((), ()))
NN = (((1,), (0,)), ((), ()))


def iota(shape, axis):
    return lax.broadcasted_iota(jnp.int32, shape, axis)


def hits(where, group, count):
    wanted = iota((count, where.shape[1]), 0) + group * count
    return (where[0:1] == wanted) | (where[1:2] == wanted)


def pick(hit, rows):
    one = hit.astype(jnp.float32).astype(jnp.bfloat16)
    return lax.dot_general(one, rows, NN, preferred_element_type=jnp.float32).astype(jnp.bfloat16)


def index_kernel(count, who, slots, sizes, routes, places, lives):
    total = slots.shape[0]
    rows = routes.shape[1]
    cluster = iota((total, rows), 0)
    slot_of = jnp.zeros((total, rows), jnp.int32)
    size_of = jnp.zeros((total, rows), jnp.int32)
    for c in range(total):
        slot_of = jnp.where(cluster == c, slots[c], slot_of)
        size_of = jnp.where(cluster == c, sizes[c], size_of)
    before = (iota((rows, rows), 0) < iota((rows, rows), 1)).astype(jnp.float32).astype(jnp.bfloat16)
    seen = jnp.zeros((total, 1), jnp.float32)
    for r in range(2):
        hit = routes[r : r + 1] == cluster
        one = hit.astype(jnp.float32)
        earlier = lax.dot_general(
            one.astype(jnp.bfloat16), before, NN, preferred_element_type=jnp.float32
        )
        rank = jnp.sum(jnp.where(hit, earlier + seen, 0.0), axis=0, keepdims=True)
        seen = seen + jnp.sum(one, axis=1, keepdims=True)
        slot = jnp.sum(jnp.where(hit, slot_of, 0), axis=0, keepdims=True)
        places[r : r + 1] = slot * MOST + rank.astype(jnp.int32)
        lives[r : r + 1] = jnp.sum(jnp.where(hit, size_of, 0), axis=0, keepdims=True)


def pick_kernel(count, groups, who, places, rows, *outs):
    where = places[...]
    for group, out in zip(groups, outs, strict=True):
        out[...] = pick(hits(where, who[group], count), rows[...])


def forward_kernel(count, keys, who, places, places_other, rows, whole, *outs):
    @pl.when(who[0] == 1)
    def _():
        where = places_other[...]
        for at in range(keys):
            outs[at][...] = pick(hits(where, who[1 + at], count), whole[...])
        outs[keys][...] = pick(hits(where, who[1 + keys], count), whole[...])

    @pl.when(who[0] == 0)
    def _():
        where = places[...]
        for at in range(keys):
            outs[at][...] = pick(hits(where, who[1 + at], count), rows[...])


def score_kernel(n_in, choose, mems, who, members, *refs):
    ins, (keep, send, acc) = refs[:n_in], refs[n_in:]
    slot_count, total, _ = members.shape
    count = slot_count * MOST
    block = total // mems

    def put(src, lane):
        for s in range(slot_count):
            acc[:, lane + s * MOST : lane + (s + 1) * MOST] = lax.dot_general(
                members[s], src[s * MOST : (s + 1) * MOST, :], NT, preferred_element_type=jnp.float32
            )

    lane = 0
    for at in range(n_in - (1 if choose else 0)):
        if choose and at == n_in - 2:
            @pl.when(who[0] == 1)
            def _(lane=lane, at=at):
                put(ins[at], lane)

            @pl.when(who[0] == 0)
            def _(lane=lane, at=at):
                put(ins[at + 1], lane)
        else:
            put(ins[at], lane)
        lane += count
    for p in range(mems // 2):
        for core, out in ((0, keep), (1, send)):
            at = (who[1] ^ (p * 2 + core)) * block
            out[p] = acc[pl.ds(pl.multiple_of(at, block), block), :]


def final_kernel(count, scale, keys, who, places, lives, *refs):
    tables, out = refs[:-1], refs[-1]
    block, rows = out.shape[1], out.shape[2]
    member = iota((block, rows), 0) + who[0]
    for r in range(2):
        total = jnp.zeros((block, rows), jnp.float32)
        where = places[r : r + 1]
        for at in range(len(keys)):
            wanted = iota((count, rows), 0) + who[1 + at] * count
            one = (where == wanted).astype(jnp.float32)
            total = total + lax.dot_general(
                tables[at][...], one, NN,
                precision=lax.Precision.HIGHEST, preferred_element_type=jnp.float32,
            )
        out[r] = jnp.where(member < lives[r : r + 1], total * scale, 0.0)


def call(kernel, shapes, n_smem, n_vmem, scratch=(), name=None, flops=0):
    return pl.pallas_call(
        kernel,
        out_shape=[jax.ShapeDtypeStruct(s, d) for s, d in shapes],
        in_specs=[SM] * n_smem + [VM] * n_vmem,
        out_specs=[VM] * len(shapes),
        scratch_shapes=scratch,
        name=name,
        cost_estimate=pl.CostEstimate(flops=flops, bytes_accessed=1 << 18, transcendentals=0),
    )


def make_local(groups, mems):
    last = groups - 1
    half = groups // 2
    middle = (half - 1, half)

    def swap(value, key):
        return lax.ppermute(value, "grp", [(i, i ^ key) for i in range(groups)])

    def swap_mem(value, key):
        return lax.ppermute(value, "mem", [(i, i ^ key) for i in range(mems)])

    def local(
        bin_sketch, rep_sketch, bin_profile, member_profile, bin_routes, owner_slot, cluster_sizes
    ):
        rows_here, width_here = bin_profile.shape
        slot_count, members, _ = member_profile.shape
        count = slot_count * MOST
        block = members // mems
        me = lax.axis_index("grp")
        mine = lax.axis_index("mem")
        inner = ((me == half - 1) | (me == half)).astype(jnp.int32)
        bf, f32, i32 = jnp.bfloat16, jnp.float32, jnp.int32
        rows_out = ((count, width_here), bf)

        with jax.named_scope("whole"):
            whole = lax.ppermute(bin_profile, "grp", [(i, i ^ last) for i in middle])

        near = list(range(1, half))
        far = list(range(half, last))
        with jax.named_scope("index"):
            places, lives = call(
                functools.partial(index_kernel, count),
                [((2, rows_here), i32)] * 2, 3, 1, name="index",
            )(me.reshape(1), owner_slot, cluster_sizes, bin_routes.T)
        with jax.named_scope("place"):
            places_other = swap(places, last)
        with jax.named_scope("picks"):
            who = jnp.stack([me ^ k for k in near + [last, 0]])
            *sends, own = call(
                functools.partial(pick_kernel, count, range(len(near) + 2)),
                [rows_out] * (len(near) + 2), 1, 2, name="picks",
            )(who, places, bin_profile)

        sketches = bin_sketch[None]
        with jax.named_scope("sketch_grp"):
            sketches = jnp.stack([bin_sketch] + [swap(bin_sketch, k) for k in range(1, groups)])

        got = {0: own}
        with jax.named_scope("near"):
            for k in near:
                got[k] = swap(sends[k - 1], k)
        with jax.named_scope("direct"):
            outer = [(i, i ^ last) for i in range(groups) if i not in middle]
            direct = lax.ppermute(sends[-1], "grp", outer) if outer else sends[-1]
        with jax.named_scope("forward"):
            who = jnp.stack([inner] + [jnp.where(inner == 1, me ^ last ^ k, me ^ k) for k in far] + [me])
            *onward, through = call(
                functools.partial(forward_kernel, count, len(far)),
                [rows_out] * (len(far) + 1), 1, 4, name="forward",
            )(who, places, places_other, bin_profile, whole)
        with jax.named_scope("far"):
            for at, k in enumerate(far):
                way = [(i, i ^ last ^ k if i in middle else i ^ k) for i in range(groups)]
                got[k] = lax.ppermute(onward[at], "grp", way)

        step = 1
        while step < mems:
            with jax.named_scope("sketch_mem"):
                sketches = jnp.stack([sketches, swap_mem(sketches, step)])
            step *= 2
        sketches = sketches.reshape(-1, bin_sketch.shape[1])

        def scores(arrays, choose):
            lanes = count * (len(arrays) - choose)
            return call(
                functools.partial(score_kernel, len(arrays), choose, mems),
                [((mems // 2, block, lanes), f32)] * 2, 1, 1 + len(arrays),
                scratch=[pltpu.VMEM((members, lanes), f32)], name="scores",
                flops=2 * members * width_here * lanes * 8,
            )(jnp.stack([inner, mine]), member_profile, *arrays)

        def reduce_mem(keep, send):
            value = keep + swap_mem(send, 1)
            while value.shape[0] > 1:
                n = value.shape[0] // 2
                value = value[:n] + swap_mem(value[n:], n * 2)
            return value[0]

        back = {}
        early = [0] + near + [last]
        with jax.named_scope("early"):
            summed = reduce_mem(*scores([got[k] for k in [0] + near] + [through, direct], True))
            for at, k in enumerate(early):
                part = summed[:, at * count : (at + 1) * count]
                back[k] = swap(part, k) if k else part
        with jax.named_scope("late"):
            if far:
                summed = reduce_mem(*scores([got[k] for k in far], False))
                for at, k in enumerate(far):
                    back[k] = swap(summed[:, at * count : (at + 1) * count], k)

        with jax.named_scope("coarse"):
            product = lax.dot_general(sketches, rep_sketch, NT, preferred_element_type=f32)
            product = (product * bin_sketch.shape[1] ** (-0.5)).astype(bf)
            each = bin_sketch.shape[0]
            row = iota((product.shape[0], 1), 0) // each
            source = (row % mems ^ mine) * groups + (row // mems ^ me)
            within = iota((product.shape[0], 1), 0) % each
            perm = source * each + within == iota((1, product.shape[0]), 1)
            coarse_scores = pick(perm, product)

        keys = sorted(back)
        with jax.named_scope("final"):
            who = jnp.stack([mine * block] + [me ^ k for k in keys])
            (fine,) = call(
                functools.partial(final_kernel, count, FW ** (-0.5), keys),
                [((2, block, rows_here), f32)], 1, 2 + len(keys), name="final",
            )(who, places, lives, *[back[k] for k in keys])
        return (coarse_scores, fine.transpose(2, 0, 1))

    return local


def solution(mesh):
    return jax.shard_map(
        make_local(mesh.shape["grp"], mesh.shape["mem"]),
        mesh=mesh,
        in_specs=(
            P(("grp", "mem"), None),
            P(("grp", "mem"), None),
            P("grp", "mem"),
            P("grp", None, "mem"),
            P("grp", None),
            P(),
            P(),
        ),
        out_specs=(P(None, ("grp", "mem")), P("grp", None, "mem")),
        check_vma=False,
    )
```

time: 133 us -> 80.7 us (0.61)
  blocking collectives: 47.3 us -> 0 us
  Pallas kernels: 0 us -> 22.3 us
  waiting for transfers between devices: 39.2 us -> 17.2 us
  starting transfers between devices: 11.1 us -> 29.5 us
  between operations: 14.1 us -> 0.79 us
  local copies, waits for them, and re-layouts: 12.8 us -> 4.82 us
  matrix products: 5.81 us -> 1.23 us
  other arithmetic: 2.59 us -> 4.49 us
    all_gather x2 -> x0, blocking collectives: 47.3 us -> none  [the longest x1 38.1 us: local(): lax.all_gather(group_rows, 'grp', axis=0, tiled=True)]
    unnamed x2 -> x0, waiting for transfers between devices: 33.8 us -> none
    ppermute x0 -> x20, starting transfers between devices: none -> 29.5 us  [the longest x8 17.5 us: swap(): return lax.ppermute(value, 'grp', [(i, i ^ key) for i in range(groups)])]
    pallas_call x0 -> x6, Pallas kernels: none -> 22.3 us  [the longest x2 14.4 us: scores(): call(functools.partial(score_kernel, len(arrays), choose, mems), [((mems...]
    ppermute x0 -> x20, waiting for transfers between devices: none -> 17.2 us  [the longest x8 10.1 us: swap(): return lax.ppermute(value, 'grp', [(i, i ^ key) for i in range(groups)])]
    all_to_all x2 -> x0, starting transfers between devices: 11.1 us -> none  [the longest x1 6.48 us: local(): lax.all_to_all(outgoing, 'grp', split_axis=0, concat_axis=0, tiled=True)]
    scatter x1 -> x0, local copies, waits for them, and re-layouts: 6.38 us -> none  [local(): jnp.zeros((capacity, width_here), jnp.bfloat16).at[slot_index].set(source)]
    all_to_all x2 -> x0, waiting for transfers between devices: 5.43 us -> none  [the longest x1 5.43 us: local(): lax.all_to_all(summed, 'grp', split_axis=0, concat_axis=0, tiled=True)]
  transfers between devices with their start and end apart: 3 -> 20, of which waited for: 2 -> 8; matrix products, arithmetic and copies ran while one was open for 1% -> 9% of each run, Pallas kernels for 0% -> 26%
where the time goes in v2:
time: 80.7 us; the launch traced here: 80.3 us
  starting transfers between devices  29.5 us (37%)
  Pallas kernels  22.3 us (28%)
  waiting for transfers between devices  17.2 us (21%)
  local copies, waits for them, and re-layouts  4.82 us (6%)
  other arithmetic  4.49 us (6%)
  matrix products  1.23 us (2%)
    ppermute x8, starting transfers between devices, swap(): return lax.ppermute(value, 'grp', [(i, i ^ key) for i in range(groups)])  17.5 us
    pallas_call x2, Pallas kernels, scores(): call(functools.partial(score_kernel, len(arrays), choose, mems), [((mems...  14.4 us
    ppermute x8, waiting for transfers between devices, swap(): return lax.ppermute(value, 'grp', [(i, i ^ key) for i in range(groups)])  10.1 us
    ppermute x9, starting transfers between devices, swap_mem(): return lax.ppermute(value, 'mem', [(i, i ^ key) for i in range(mems)])  8.04 us
    ppermute x9, waiting for transfers between devices, swap_mem(): return lax.ppermute(value, 'mem', [(i, i ^ key) for i in range(mems)])  7.16 us
    unnamed x18, local copies, waits for them, and re-layouts  3.57 us
    ppermute x1, starting transfers between devices, local(): direct = lax.ppermute(sends[-1], 'grp', outer) if outer else sends[-1]  3.24 us
    pallas_call x1, Pallas kernels, local(): call(functools.partial(forward_kernel, count, len(far)), [rows_out] * (le...  2.41 us
  transfers between devices with their start and end apart: 20, of which 8 were waited for; matrix products, arithmetic and copies ran while one was open for 9% of the time, Pallas kernels for 26%

profile of v2, /device:TPU:0, one launch (start us, length us, event | category | flops | bytes accessed | tf_op | source)
XLA Modules:
  0.0 80.3 jit_solution(14010770502752284993)
XLA Ops:
  0.6 3.1 %collective-permute-start = (bf16[8,1024]{1,0:T(8,128)(2,1)}, bf16[8,1024]{1,0:T(8,128)(2,1)S(1)}, u32[]{:S(2)}, u32[]{:S(2)}) collective-permute-start(bf16[8,1024]{1,0:T(8,128)(2,1)} %param.7), channel_id=1, source_target_pairs={{0,8},{8,0},{16,24},{24,16},{1,9},{9,1},{17,25},{25,17},{2,10},{10... | collective-permute-start | bytes 49160 | tf_op jit(solution)/shard_map/sketch_grp/ppermute | solution.py:143
  3.8 2.6 %collective-permute-start.1 = (bf16[8,1024]{1,0:T(8,128)(2,1)}, bf16[8,1024]{1,0:T(8,128)(2,1)S(1)}, u32[]{:S(2)}, u32[]{:S(2)}) collective-permute-start(bf16[8,1024]{1,0:T(8,128)(2,1)} %param.7), channel_id=1, source_target_pairs={{0,16},{8,24},{16,0},{24,8},{1,17},{9,25},{17,1},{25,9},{2,18},{10... | collective-permute-start | bytes 49160 | tf_op jit(solution)/shard_map/sketch_grp/ppermute | solution.py:143
  7.6 1.4 %index.1 = (s32[2,64]{1,0:T(2,128)}, s32[2,64]{1,0:T(2,128)}) custom-call(s32[1]{0:T(128)} %bitcast.12.who, s32[12]{0:T(128)} %slots.1, s32[12]{0:T(128)} %sizes.1, s32[2,64]{1,0:T(2,128)} %bitcast.39), custom_call_target="tpu_custom_call" | custom-call | bytes 262144 | tf_op jit(solution)/shard_map/index/index/pallas_call | solution.py:167
  9.1 2.3 %picks.1 = (bf16[48,4096]{1,0:T(8,128)(2,1)}, bf16[48,4096]{1,0:T(8,128)(2,1)}, bf16[48,4096]{1,0:T(8,128)(2,1)}) custom-call(s32[3]{0:T(128)} %add_add_fusion.who, s32[2,64]{1,0:T(2,128)} %get-tuple-element.13.places, bf16[64,4096]{1,0:T(8,128)(2,1)} %rows.3), custom_call_target="tpu_custom_call" | custom-call | bytes 262144 | tf_op jit(solution)/shard_map/picks/picks/pallas_call | solution.py:175
  11.4 3.7 %collective-permute-start.6 = (bf16[48,4096]{1,0:T(8,128)(2,1)}, bf16[48,4096]{1,0:T(8,128)(2,1)S(1)}, u32[]{:S(2)}, u32[]{:S(2)}) collective-permute-start(bf16[48,4096]{1,0:T(8,128)(2,1)} %get-tuple-element.16), channel_id=1, source_target_pairs={{0,8},{8,0},{16,24},{24,16},{1,9},{9,1},{17,25},{25,17},{2,10},{10... | collective-permute-start | bytes 1179656 | tf_op jit(solution)/shard_map/near/ppermute | solution.py:143
  15.1 3.2 %collective-permute-start.9 = (bf16[48,4096]{1,0:T(8,128)(2,1)}, bf16[48,4096]{1,0:T(8,128)(2,1)S(1)}, u32[]{:S(2)}, u32[]{:S(2)}) collective-permute-start(bf16[48,4096]{1,0:T(8,128)(2,1)} %get-tuple-element.18), channel_id=1, source_target_pairs={{0,24},{24,0},{1,25},{25,1},{2,26},{26,2},{3,27},{27,3},{4,28},{28... | collective-permute-start | bytes 1179656 | tf_op jit(solution)/shard_map/direct/ppermute | solution.py:190
  19.0 2.5 %collective-permute-start.7 = (s32[2,64]{1,0:T(2,128)}, s32[2,64]{1,0:T(2,128)S(1)}, u32[]{:S(2)}, u32[]{:S(2)}) collective-permute-start(s32[2,64]{1,0:T(2,128)} %get-tuple-element.13.places), channel_id=1, source_target_pairs={{0,24},{8,16},{16,8},{24,0},{1,25},{9,17},{17,9},{25,1},{2,26},{10... | collective-permute-start | bytes 1544 | tf_op jit(solution)/shard_map/place/ppermute | solution.py:143
  23.5 1.6 %collective-permute-start.4 = (bf16[2,4,8,1024]{3,2,1,0:T(8,128)(2,1)S(1)}, bf16[2,4,8,1024]{3,2,1,0:T(8,128)(2,1)S(1)}, u32[]{:S(2)}, u32[]{:S(2)}) collective-permute-start(bf16[2,4,8,1024]{3,2,1,0:T(8,128)(2,1)S(1)} %get-tuple-element.27), channel_id=1, source_target_pairs={{0,2},{1,3},{2,0},{3,1},{4,6},{5,7},{6,4},{7,5},{8,10},{9,11},{10,... | collective-permute-start | bytes 393224 | tf_op jit(solution)/shard_map/sketch_mem/ppermute | solution.py:146
  25.1 7.7 %collective-permute-done.7.places_other = s32[2,64]{1,0:T(2,128)S(1)} collective-permute-done((s32[2,64]{1,0:T(2,128)}, s32[2,64]{1,0:T(2,128)S(1)}, u32[]{:S(2)}, u32[]{:S(2)}) %collective-permute-start.7) | collective-permute-done | bytes 544 | tf_op jit(solution)/shard_map/place/ppermute | solution.py:143
  34.2 2.4 %forward.1 = (bf16[48,4096]{1,0:T(8,128)(2,1)}, bf16[48,4096]{1,0:T(8,128)(2,1)}) custom-call(s32[3]{0:T(128)} %add_add_fusion.1.who, s32[2,64]{1,0:T(2,128)} %get-tuple-element.13.places, s32[2,64]{1,0:T(2,128)} %copy-done.6, bf16[64,4096]{1,0:T(8,128)(2,1)} %rows.3, bf16[64,4096]{1,0:T(8,128)(2,1)} %copy-done.1), custom_call_target="tpu_custom_call" | custom-call | bytes 262144 | tf_op jit(solution)/shard_map/forward/forward/pallas_call | solution.py:193
  37.5 9.1 %scores.2 = (f32[4,32,144]{2,1,0:T(8,128)}, f32[4,32,144]{2,1,0:T(8,128)}) custom-call(s32[2]{0:T(128)} %pad_add_fusion.who, bf16[3,256,4096]{2,1,0:T(8,128)(2,1)} %members.3, bf16[48,4096]{1,0:T(8,128)(2,1)} %get-tuple-element.15.refs_0_, bf16[48,4096]{1,0:T(8,128)(2,1)} %copy-done.7, bf16[48,4096]{1,0:T(8,128)(2,1)} %get-tuple-element.17.refs_2_, ...), custom_call_target="tpu_custom_call" | custom-call | flops 2415919104 | bytes 262144 | tf_op jit(solution)/shard_map/early/scores/pallas_call | solution.py:211
  49.1 1.6 %collective-permute-start.11 = (f32[2,32,144]{2,1,0:T(8,128)S(1)}, f32[2,32,144]{2,1,0:T(8,128)S(1)}, u32[]{:S(2)}, u32[]{:S(2)}) collective-permute-start(f32[2,32,144]{2,1,0:T(8,128)S(1)} %slice.45), channel_id=1, source_target_pairs={{0,4},{1,5},{2,6},{3,7},{4,0},{5,1},{6,2},{7,3},{8,12},{9,13},{10,... | collective-permute-start | bytes 110600 | tf_op jit(solution)/shard_map/early/ppermute | solution.py:146
  51.3 2.3 %collective-permute-done.11 = f32[2,32,144]{2,1,0:T(8,128)S(1)} collective-permute-done((f32[2,32,144]{2,1,0:T(8,128)S(1)}, f32[2,32,144]{2,1,0:T(8,128)S(1)}, u32[]{:S(2)}, u32[]{:S(2)}) %collective-permute-start.11) | collective-permute-done | bytes 36896 | tf_op jit(solution)/shard_map/early/ppermute | solution.py:146
  53.7 1.5 %collective-permute-start.12 = (f32[1,32,144]{2,1,0:T(8,128)S(1)}, f32[1,32,144]{2,1,0:T(8,128)S(1)}, u32[]{:S(2)}, u32[]{:S(2)}) collective-permute-start(f32[1,32,144]{2,1,0:T(8,128)S(1)} %slice.47), channel_id=1, source_target_pairs={{0,2},{1,3},{2,0},{3,1},{4,6},{5,7},{6,4},{7,5},{8,10},{9,11},{10,... | collective-permute-start | bytes 55304 | tf_op jit(solution)/shard_map/early/ppermute | solution.py:146
  56.0 5.3 %scores.3 = (f32[4,32,48]{2,1,0:T(8,128)}, f32[4,32,48]{2,1,0:T(8,128)}) custom-call(s32[2]{0:T(128)} %pad_add_fusion.who, bf16[3,256,4096]{2,1,0:T(8,128)(2,1)} %members.3, bf16[48,4096]{1,0:T(8,128)(2,1)} %copy-done.2), custom_call_target="tpu_custom_call" | custom-call | flops 805306368 | bytes 262144 | tf_op jit(solution)/shard_map/late/scores/pallas_call | solution.py:211
  61.3 1.4 %collective-permute-done.15 = f32[4,32,48]{2,1,0:T(8,128)S(1)} collective-permute-done((f32[4,32,48]{2,1,0:T(8,128)}, f32[4,32,48]{2,1,0:T(8,128)S(1)}, u32[]{:S(2)}, u32[]{:S(2)}) %collective-permute-start.15) | collective-permute-done | bytes 24608 | tf_op jit(solution)/shard_map/late/ppermute | solution.py:146
  63.6 2.1 %collective-permute-start.16 = (f32[2,32,48]{2,1,0:T(8,128)S(1)}, f32[2,32,48]{2,1,0:T(8,128)S(1)}, u32[]{:S(2)}, u32[]{:S(2)}) collective-permute-start(f32[2,32,48]{2,1,0:T(8,128)S(1)} %slice.51), channel_id=1, source_target_pairs={{0,4},{1,5},{2,6},{3,7},{4,0},{5,1},{6,2},{7,3},{8,12},{9,13},{10,... | collective-permute-start | bytes 36872 | tf_op jit(solution)/shard_map/late/ppermute | solution.py:146
  65.7 1.9 %collective-permute-done.16 = f32[2,32,48]{2,1,0:T(8,128)S(1)} collective-permute-done((f32[2,32,48]{2,1,0:T(8,128)S(1)}, f32[2,32,48]{2,1,0:T(8,128)S(1)}, u32[]{:S(2)}, u32[]{:S(2)}) %collective-permute-start.16) | collective-permute-done | bytes 12320 | tf_op jit(solution)/shard_map/late/ppermute | solution.py:146
  68.8 2.0 %collective-permute-start.13 = (f32[32,48]{1,0:T(8,128)S(1)}, f32[32,48]{1,0:T(8,128)S(1)}, u32[]{:S(2)}, u32[]{:S(2)}) collective-permute-start(f32[32,48]{1,0:T(8,128)S(1)} %get-tuple-element.31), channel_id=1, source_target_pairs={{0,8},{8,0},{16,24},{24,16},{1,9},{9,1},{17,25},{25,17},{2,10},{10... | collective-permute-start | bytes 18440 | tf_op jit(solution)/shard_map/early/ppermute | solution.py:143
  70.8 2.5 %collective-permute-start.19 = (f32[32,48]{1,0:T(8,128)S(1)}, f32[32,48]{1,0:T(8,128)S(1)}, u32[]{:S(2)}, u32[]{:S(2)}) collective-permute-start(f32[32,48]{1,0:T(8,128)S(1)} %get-tuple-element.30), channel_id=1, source_target_pairs={{0,24},{8,16},{16,8},{24,0},{1,25},{9,17},{17,9},{25,1},{2,26},{10... | collective-permute-start | bytes 18440 | tf_op jit(solution)/shard_map/early/ppermute | solution.py:143
  73.3 1.1 %collective-permute-start.18 = (f32[32,48]{1,0:T(8,128)S(1)}, f32[32,48]{1,0:T(8,128)S(1)}, u32[]{:S(2)}, u32[]{:S(2)}) collective-permute-start(f32[32,48]{1,0:T(8,128)S(1)} %fusion.4), channel_id=1, source_target_pairs={{0,16},{8,24},{16,0},{24,8},{1,17},{9,25},{17,1},{25,9},{2,18},{10... | collective-permute-start | bytes 18440 | tf_op jit(solution)/shard_map/late/ppermute | solution.py:143
  74.4 1.2 %convolution_convert_fusion = bf16[256,256]{1,0:T(8,128)(2,1)} fusion(bf16[256,1024]{1,0:T(8,128)(2,1)S(1)} %bitcast.30, bf16[256,1024]{1,0:T(8,128)(2,1)S(1)} %copy-done, s32[256]{0:T(256)S(1)} %fusion.7), kind=kOutput, calls=%fused_computation.2 | convolution fusion | flops 168165376 | bytes 1180672 | tf_op jit(solution)/shard_map/coarse/dot_general | solution.py:29
  76.3 1.7 %collective-permute-done.18.refs_2_ = f32[32,48]{1,0:T(8,128)S(1)} collective-permute-done((f32[32,48]{1,0:T(8,128)S(1)}, f32[32,48]{1,0:T(8,128)S(1)}, u32[]{:S(2)}, u32[]{:S(2)}) %collective-permute-start.18) | collective-permute-done | bytes 6176 | tf_op jit(solution)/shard_map/late/ppermute | solution.py:143
  78.6 1.7 %final.1 = f32[2,32,64]{2,1,0:T(8,128)} custom-call(s32[5]{0:T(128)} %stack.105.who, s32[2,64]{1,0:T(2,128)} %get-tuple-element.13.places, s32[2,64]{1,0:T(2,128)} %get-tuple-element.14.lives, f32[32,48]{1,0:T(8,128)} %get-tuple-element.32.refs_0_, f32[32,48]{1,0:T(8,128)} %copy-done.3, f32[32,48]{1,0:T(8,128)} %copy-done.5, f32[32,48]{1,0:T(8,128)} %copy-done.4), custom_call_target="tpu_custom_call" | custom-call | bytes 262144 | tf_op jit(solution)/shard_map/final/final/pallas_call | solution.py:251
  (61 shorter events, 13.5 us)
Async XLA Ops:
  0.6 73.8 %copy-start = (bf16[256,1024]{1,0:T(8,128)(2,1)S(1)}, bf16[256,1024]{1,0:T(8,128)(2,1)}, u32[]{:S(2)}) copy-start(bf16[256,1024]{1,0:T(8,128)(2,1)} %param.8) | copy-start | bytes 1572868
  0.6 14.4 %collective-permute-start = (bf16[8,1024]{1,0:T(8,128)(2,1)}, bf16[8,1024]{1,0:T(8,128)(2,1)S(1)}, u32[]{:S(2)}, u32[]{:S(2)}) collective-permute-start(bf16[8,1024]{1,0:T(8,128)(2,1)} %param.7), channel_id=1, source_target_pairs={{0,8},{8,0},{16,24},{24,16},{1,9},{9,1},{17,25},{25,17},{2,10},{10... | collective-permute-start | bytes 49160 | tf_op jit(solution)/shard_map/sketch_grp/ppermute | solution.py:143
  3.8 15.2 %collective-permute-start.1 = (bf16[8,1024]{1,0:T(8,128)(2,1)}, bf16[8,1024]{1,0:T(8,128)(2,1)S(1)}, u32[]{:S(2)}, u32[]{:S(2)}) collective-permute-start(bf16[8,1024]{1,0:T(8,128)(2,1)} %param.7), channel_id=1, source_target_pairs={{0,16},{8,24},{16,0},{24,8},{1,17},{9,25},{17,1},{25,9},{2,18},{10... | collective-permute-start | bytes 49160 | tf_op jit(solution)/shard_map/sketch_grp/ppermute | solution.py:143
  6.4 15.1 %collective-permute-start.2 = (bf16[8,1024]{1,0:T(8,128)(2,1)}, bf16[8,1024]{1,0:T(8,128)(2,1)S(1)}, u32[]{:S(2)}, u32[]{:S(2)}) collective-permute-start(bf16[8,1024]{1,0:T(8,128)(2,1)} %param.7), channel_id=1, source_target_pairs={{0,24},{8,16},{16,8},{24,0},{1,25},{9,17},{17,9},{25,1},{2,26},{10... | collective-permute-start | bytes 49160 | tf_op jit(solution)/shard_map/sketch_grp/ppermute | solution.py:143
  6.4 26.5 %collective-permute-start.8 = (bf16[64,4096]{1,0:T(8,128)(2,1)}, bf16[64,4096]{1,0:T(8,128)(2,1)S(1)}, u32[]{:S(2)}, u32[]{:S(2)}) collective-permute-start(bf16[64,4096]{1,0:T(8,128)(2,1)} %rows.3), channel_id=1, source_target_pairs={{8,16},{16,8},{9,17},{17,9},{10,18},{18,10},{11,19},{19,11},{12,20... | collective-permute-start | bytes 1572872 | tf_op jit(solution)/shard_map/whole/ppermute | solution.py:162
  11.4 25.2 %collective-permute-start.6 = (bf16[48,4096]{1,0:T(8,128)(2,1)}, bf16[48,4096]{1,0:T(8,128)(2,1)S(1)}, u32[]{:S(2)}, u32[]{:S(2)}) collective-permute-start(bf16[48,4096]{1,0:T(8,128)(2,1)} %get-tuple-element.16), channel_id=1, source_target_pairs={{0,8},{8,0},{16,24},{24,16},{1,9},{9,1},{17,25},{25,17},{2,10},{10... | collective-permute-start | bytes 1179656 | tf_op jit(solution)/shard_map/near/ppermute | solution.py:143
  15.1 21.6 %collective-permute-start.9 = (bf16[48,4096]{1,0:T(8,128)(2,1)}, bf16[48,4096]{1,0:T(8,128)(2,1)S(1)}, u32[]{:S(2)}, u32[]{:S(2)}) collective-permute-start(bf16[48,4096]{1,0:T(8,128)(2,1)} %get-tuple-element.18), channel_id=1, source_target_pairs={{0,24},{24,0},{1,25},{25,1},{2,26},{26,2},{3,27},{27,3},{4,28},{28... | collective-permute-start | bytes 1179656 | tf_op jit(solution)/shard_map/direct/ppermute | solution.py:190
  19.0 13.8 %collective-permute-start.7 = (s32[2,64]{1,0:T(2,128)}, s32[2,64]{1,0:T(2,128)S(1)}, u32[]{:S(2)}, u32[]{:S(2)}) collective-permute-start(s32[2,64]{1,0:T(2,128)} %get-tuple-element.13.places), channel_id=1, source_target_pairs={{0,24},{8,16},{16,8},{24,0},{1,25},{9,17},{17,9},{25,1},{2,26},{10... | collective-permute-start | bytes 1544 | tf_op jit(solution)/shard_map/place/ppermute | solution.py:143
  22.2 1.3 %collective-permute-start.3 = (bf16[4,8,1024]{2,1,0:T(8,128)(2,1)S(1)}, bf16[4,8,1024]{2,1,0:T(8,128)(2,1)S(1)}, u32[]{:S(2)}, u32[]{:S(2)}) collective-permute-start(bf16[4,8,1024]{2,1,0:T(8,128)(2,1)S(1)} %get-tuple-element.29), channel_id=1, source_target_pairs={{0,1},{1,0},{2,3},{3,2},{4,5},{5,4},{6,7},{7,6},{8,9},{9,8},{10,11... | collective-permute-start | bytes 196616 | tf_op jit(solution)/shard_map/sketch_mem/ppermute | solution.py:146
  23.5 27.2 %collective-permute-start.4 = (bf16[2,4,8,1024]{3,2,1,0:T(8,128)(2,1)S(1)}, bf16[2,4,8,1024]{3,2,1,0:T(8,128)(2,1)S(1)}, u32[]{:S(2)}, u32[]{:S(2)}) collective-permute-start(bf16[2,4,8,1024]{3,2,1,0:T(8,128)(2,1)S(1)} %get-tuple-element.27), channel_id=1, source_target_pairs={{0,2},{1,3},{2,0},{3,1},{4,6},{5,7},{6,4},{7,5},{8,10},{9,11},{10,... | collective-permute-start | bytes 393224 | tf_op jit(solution)/shard_map/sketch_mem/ppermute | solution.py:146
  36.6 18.6 %collective-permute-start.14 = (bf16[48,4096]{1,0:T(8,128)(2,1)}, bf16[48,4096]{1,0:T(8,128)(2,1)S(1)}, u32[]{:S(2)}, u32[]{:S(2)}) collective-permute-start(bf16[48,4096]{1,0:T(8,128)(2,1)} %get-tuple-element.21), channel_id=1, source_target_pairs={{0,16},{8,0},{16,24},{24,8},{1,17},{9,1},{17,25},{25,9},{2,18},{10... | collective-permute-start | bytes 1179656 | tf_op jit(solution)/shard_map/far/ppermute | solution.py:200
  36.6 0.9 %copy-start.8 = (bf16[48,4096]{1,0:T(8,128)(2,1)}, bf16[48,4096]{1,0:T(8,128)(2,1)S(1)}, u32[]{:S(2)}) copy-start(bf16[48,4096]{1,0:T(8,128)(2,1)S(1)} %collective-permute-done.9.refs_3_) | copy-start | bytes 1179652
  46.6 1.6 %collective-permute-start.10 = (f32[4,32,144]{2,1,0:T(8,128)}, f32[4,32,144]{2,1,0:T(8,128)S(1)}, u32[]{:S(2)}, u32[]{:S(2)}) collective-permute-start(f32[4,32,144]{2,1,0:T(8,128)} %get-tuple-element.20), channel_id=1, source_target_pairs={{0,1},{1,0},{2,3},{3,2},{4,5},{5,4},{6,7},{7,6},{8,9},{9,8},{10,11... | collective-permute-start | bytes 221192 | tf_op jit(solution)/shard_map/early/ppermute | solution.py:146
  49.1 4.5 %collective-permute-start.11 = (f32[2,32,144]{2,1,0:T(8,128)S(1)}, f32[2,32,144]{2,1,0:T(8,128)S(1)}, u32[]{:S(2)}, u32[]{:S(2)}) collective-permute-start(f32[2,32,144]{2,1,0:T(8,128)S(1)} %slice.45), channel_id=1, source_target_pairs={{0,4},{1,5},{2,6},{3,7},{4,0},{5,1},{6,2},{7,3},{8,12},{9,13},{10,... | collective-permute-start | bytes 110600 | tf_op jit(solution)/shard_map/early/ppermute | solution.py:146
  50.7 10.5 %collective-permute-start.5 = (bf16[2,2,4,8,1024]{4,3,2,1,0:T(8,128)(2,1)S(1)}, bf16[2,2,4,8,1024]{4,3,2,1,0:T(8,128)(2,1)S(1)}, u32[]{:S(2)}, u32[]{:S(2)}) collective-permute-start(bf16[2,2,4,8,1024]{4,3,2,1,0:T(8,128)(2,1)S(1)} %get-tuple-element.25), channel_id=1, source_target_pairs={{0,4},{1,5},{2,6},{3,7},{4,0},{5,1},{6,2},{7,3},{8,12},{9,13},{10,... | collective-permute-start | bytes 786440 | tf_op jit(solution)/shard_map/sketch_mem/ppermute | solution.py:146
  53.7 12.0 %collective-permute-start.12 = (f32[1,32,144]{2,1,0:T(8,128)S(1)}, f32[1,32,144]{2,1,0:T(8,128)S(1)}, u32[]{:S(2)}, u32[]{:S(2)}) collective-permute-start(f32[1,32,144]{2,1,0:T(8,128)S(1)} %slice.47), channel_id=1, source_target_pairs={{0,2},{1,3},{2,0},{3,1},{4,6},{5,7},{6,4},{7,5},{8,10},{9,11},{10,... | collective-permute-start | bytes 55304 | tf_op jit(solution)/shard_map/early/ppermute | solution.py:146
  61.2 1.5 %collective-permute-start.15 = (f32[4,32,48]{2,1,0:T(8,128)}, f32[4,32,48]{2,1,0:T(8,128)S(1)}, u32[]{:S(2)}, u32[]{:S(2)}) collective-permute-start(f32[4,32,48]{2,1,0:T(8,128)} %get-tuple-element.23), channel_id=1, source_target_pairs={{0,1},{1,0},{2,3},{3,2},{4,5},{5,4},{6,7},{7,6},{8,9},{9,8},{10,11... | collective-permute-start | bytes 73736 | tf_op jit(solution)/shard_map/late/ppermute | solution.py:146
  63.6 4.0 %collective-permute-start.16 = (f32[2,32,48]{2,1,0:T(8,128)S(1)}, f32[2,32,48]{2,1,0:T(8,128)S(1)}, u32[]{:S(2)}, u32[]{:S(2)}) collective-permute-start(f32[2,32,48]{2,1,0:T(8,128)S(1)} %slice.51), channel_id=1, source_target_pairs={{0,4},{1,5},{2,6},{3,7},{4,0},{5,1},{6,2},{7,3},{8,12},{9,13},{10,... | collective-permute-start | bytes 36872 | tf_op jit(solution)/shard_map/late/ppermute | solution.py:146
  67.6 5.7 %collective-permute-start.17 = (f32[1,32,48]{2,1,0:T(8,128)S(1)}, f32[1,32,48]{2,1,0:T(8,128)S(1)}, u32[]{:S(2)}, u32[]{:S(2)}) collective-permute-start(f32[1,32,48]{2,1,0:T(8,128)S(1)} %slice.53), channel_id=1, source_target_pairs={{0,2},{1,3},{2,0},{3,1},{4,6},{5,7},{6,4},{7,5},{8,10},{9,11},{10,... | collective-permute-start | bytes 18440 | tf_op jit(solution)/shard_map/late/ppermute | solution.py:146
  68.8 6.9 %collective-permute-start.13 = (f32[32,48]{1,0:T(8,128)S(1)}, f32[32,48]{1,0:T(8,128)S(1)}, u32[]{:S(2)}, u32[]{:S(2)}) collective-permute-start(f32[32,48]{1,0:T(8,128)S(1)} %get-tuple-element.31), channel_id=1, source_target_pairs={{0,8},{8,0},{16,24},{24,16},{1,9},{9,1},{17,25},{25,17},{2,10},{10... | collective-permute-start | bytes 18440 | tf_op jit(solution)/shard_map/early/ppermute | solution.py:143
  70.8 5.5 %collective-permute-start.19 = (f32[32,48]{1,0:T(8,128)S(1)}, f32[32,48]{1,0:T(8,128)S(1)}, u32[]{:S(2)}, u32[]{:S(2)}) collective-permute-start(f32[32,48]{1,0:T(8,128)S(1)} %get-tuple-element.30), channel_id=1, source_target_pairs={{0,24},{8,16},{16,8},{24,0},{1,25},{9,17},{17,9},{25,1},{2,26},{10... | collective-permute-start | bytes 18440 | tf_op jit(solution)/shard_map/early/ppermute | solution.py:143
  73.3 4.7 %collective-permute-start.18 = (f32[32,48]{1,0:T(8,128)S(1)}, f32[32,48]{1,0:T(8,128)S(1)}, u32[]{:S(2)}, u32[]{:S(2)}) collective-permute-start(f32[32,48]{1,0:T(8,128)S(1)} %fusion.4), channel_id=1, source_target_pairs={{0,16},{8,24},{16,0},{24,8},{1,17},{9,25},{17,1},{25,9},{2,18},{10... | collective-permute-start | bytes 18440 | tf_op jit(solution)/shard_map/late/ppermute | solution.py:143
  75.6 2.3 %copy-start.3 = (f32[32,48]{1,0:T(8,128)}, f32[32,48]{1,0:T(8,128)S(1)}, u32[]{:S(2)}) copy-start(f32[32,48]{1,0:T(8,128)S(1)} %collective-permute-done.13.refs_1_) | copy-start | bytes 18436
  76.3 1.7 %copy-start.4 = (f32[32,48]{1,0:T(8,128)}, f32[32,48]{1,0:T(8,128)S(1)}, u32[]{:S(2)}) copy-start(f32[32,48]{1,0:T(8,128)S(1)} %collective-permute-done.19.refs_3_) | copy-start | bytes 18436
  (5 other events, 3.4 us)

commit v3 on v2

v3 whole, which is shorter than its diff:
```python
import functools

import jax
import jax.numpy as jnp
from jax import lax
from jax.experimental import pallas as pl
from jax.experimental.pallas import tpu as pltpu
from jax.sharding import PartitionSpec as P


FW = 32768
MOST = 16
VM = pl.BlockSpec(memory_space=pltpu.VMEM)
SM = pl.BlockSpec(memory_space=pltpu.SMEM)
FAR = pl.BlockSpec(memory_space=pltpu.HBM)
NT = (((1,), (1,)), ((), ()))
NN = (((1,), (0,)), ((), ()))


def iota(shape, axis):
    return lax.broadcasted_iota(jnp.int32, shape, axis)


def hits(where, group, count):
    wanted = iota((count, where.shape[1]), 0) + group * count
    return (where[0:1] == wanted) | (where[1:2] == wanted)


def pick(hit, rows):
    one = hit.astype(jnp.float32).astype(jnp.bfloat16)
    return lax.dot_general(one, rows, NN, preferred_element_type=jnp.float32).astype(jnp.bfloat16)


def head_kernel(
    keys, me, slots_far, sizes_far, routes_far, rows_far,
    places, lives, *refs,
):
    outs, (slots, sizes, routes, rows, sems) = refs[: len(keys)], refs[len(keys) :]
    pairs = ((slots_far, slots), (sizes_far, sizes), (routes_far, routes), (rows_far, rows))
    copies = [pltpu.make_async_copy(a, b, sems.at[i]) for i, (a, b) in enumerate(pairs)]
    for copy in copies:
        copy.start()
    total, count = slots.shape[0], outs[0].shape[0]
    width = routes.shape[1]
    before = (iota((width, width), 0) < iota((width, width), 1)).astype(jnp.float32)
    before = before.astype(jnp.bfloat16)
    cluster = iota((total, width), 0)
    slot_of = jnp.zeros((total, width), jnp.int32)
    size_of = jnp.zeros((total, width), jnp.int32)
    for copy in copies[:3]:
        copy.wait()
    for c in range(total):
        slot_of = jnp.where(cluster == c, slots[c], slot_of)
        size_of = jnp.where(cluster == c, sizes[c], size_of)
    seen = jnp.zeros((total, 1), jnp.float32)
    for r in range(2):
        hit = routes[r : r + 1] == cluster
        one = hit.astype(jnp.float32)
        earlier = lax.dot_general(
            one.astype(jnp.bfloat16), before, NN, preferred_element_type=jnp.float32
        )
        rank = jnp.sum(jnp.where(hit, earlier + seen, 0.0), axis=0, keepdims=True)
        seen = seen + jnp.sum(one, axis=1, keepdims=True)
        slot = jnp.sum(jnp.where(hit, slot_of, 0), axis=0, keepdims=True)
        places[r : r + 1] = slot * MOST + rank.astype(jnp.int32)
        lives[r : r + 1] = jnp.sum(jnp.where(hit, size_of, 0), axis=0, keepdims=True)
    where = places[...]
    copies[3].wait()
    for key, out in zip(keys, outs, strict=True):
        out[...] = pick(hits(where, me[0] ^ key, count), rows[...])


def is_inner(me, last):
    return (me[0] == last // 2) | (me[0] == last // 2 + 1)


def forward_kernel(keys, last, me, places_other, whole, *refs):
    outs = refs[len(keys) :]
    count = outs[0].shape[0]

    @pl.when(is_inner(me, last))
    def _():
        where = places_other[...]
        for key, out in zip(keys, outs):
            out[...] = pick(hits(where, me[0] ^ last ^ key, count), whole[...])
        outs[-1][...] = pick(hits(where, me[0], count), whole[...])


def score_kernel(sources, mems, last, lane, me, mine, members, *refs):
    ins, (keep, send, acc) = refs[:sources], refs[-3:]
    slot_count, total, _ = members.shape
    block = total // mems
    count = acc.shape[1]

    def put(src):
        for s in range(slot_count):
            acc[:, s * MOST : (s + 1) * MOST] = lax.dot_general(
                members[s], src[s * MOST : (s + 1) * MOST, :], NT, preferred_element_type=jnp.float32
            )

    if sources == 2:
        inner = is_inner(me, last)

        @pl.when(inner)
        def _():
            put(ins[0])

        @pl.when(jnp.logical_not(inner))
        def _():
            put(ins[1])
    else:
        put(ins[0])
    for p in range(mems // 2):
        for core, out in ((0, keep), (1, send)):
            at = (mine[0] ^ (p * 2 + core)) * block
            out[p, :, lane : lane + count] = acc[pl.ds(pl.multiple_of(at, block), block), :]


def final_kernel(count, scale, keys, me, mine, places, lives, *refs):
    tables, out = refs[:-1], refs[-1]
    block, rows = out.shape[1], out.shape[2]
    member = iota((block, rows), 0) + mine[0] * block
    for r in range(2):
        total = jnp.zeros((block, rows), jnp.float32)
        where = places[r : r + 1]
        for key, table in zip(keys, tables, strict=True):
            wanted = iota((count, rows), 0) + (me[0] ^ key) * count
            one = (where == wanted).astype(jnp.float32)
            total = total + lax.dot_general(
                table[...], one, NN,
                precision=lax.Precision.HIGHEST, preferred_element_type=jnp.float32,
            )
        out[r] = jnp.where(member < lives[r : r + 1], total * scale, 0.0)


def call(kernel, shapes, specs, scratch=(), flops=0, mib=4, alias=()):
    return pl.pallas_call(
        kernel,
        out_shape=[jax.ShapeDtypeStruct(s, d) for s, d in shapes],
        in_specs=specs,
        out_specs=[VM] * len(shapes),
        scratch_shapes=scratch,
        input_output_aliases=dict(alias),
        compiler_params=pltpu.CompilerParams(vmem_limit_bytes=mib << 20),
        cost_estimate=pl.CostEstimate(flops=flops, bytes_accessed=1 << 18, transcendentals=0),
    )


def stay(value):
    return pltpu.with_memory_space_constraint(value, pltpu.HBM)


def make_local(groups, mems):
    last = groups - 1
    half = groups // 2
    middle = (half - 1, half)

    def swap(value, key):
        return lax.ppermute(value, "grp", [(i, i ^ key) for i in range(groups)])

    def swap_mem(value, key):
        return lax.ppermute(value, "mem", [(i, i ^ key) for i in range(mems)])

    def local(
        bin_sketch, rep_sketch, bin_profile, member_profile, bin_routes, owner_slot, cluster_sizes
    ):
        rows_here, width_here = bin_profile.shape
        slot_count, members, _ = member_profile.shape
        count = slot_count * MOST
        block = members // mems
        me = lax.axis_index("grp")
        mine = lax.axis_index("mem")
        me1, mine1 = me.reshape(1), mine.reshape(1)
        member_profile = pltpu.with_memory_space_constraint(member_profile, pltpu.VMEM)
        bf, f32, i32 = jnp.bfloat16, jnp.float32, jnp.int32
        rows_out = ((count, width_here), bf)

        whole = lax.ppermute(bin_profile, "grp", [(i, i ^ last) for i in middle])

        near = list(range(1, half))
        far = list(range(half, last))
        keys = near + [last] + far + [0]
        total = owner_slot.shape[0]
        places, lives, *picked = call(
            functools.partial(head_kernel, keys),
            [((2, rows_here), i32)] * 2 + [rows_out] * len(keys),
            [SM] + [FAR] * 4,
            scratch=[
                pltpu.SMEM((total,), i32), pltpu.SMEM((total,), i32),
                pltpu.VMEM((2, rows_here), i32), pltpu.VMEM(bin_profile.shape, bf),
                pltpu.SemaphoreType.DMA((4,)),
            ],
        )(me1, *[stay(x) for x in (owner_slot, cluster_sizes, bin_routes.T, bin_profile)])
        picked = dict(zip(keys, picked, strict=True))
        places_other = lax.ppermute(places, "grp", [(i, i ^ last) for i in middle])

        sketches = bin_sketch[None]
        sketches = jnp.stack([bin_sketch] + [swap(bin_sketch, k) for k in range(1, groups)])

        got = {0: picked[0]}
        for k in near:
            got[k] = swap(picked[k], k)
        outer = [(i, i ^ last) for i in range(groups) if i not in middle]
        direct = lax.ppermute(picked[last], "grp", outer)
        *onward, through = call(
            functools.partial(forward_kernel, far, last),
            [rows_out] * (len(far) + 1), [SM] + [VM] * (2 + len(far)),
            alias=[(3 + i, i) for i in range(len(far))],
        )(me1, places_other, whole, *[picked[k] for k in far])
        for at, k in enumerate(far):
            way = [(i, i ^ last ^ k if i in middle else i ^ k) for i in range(groups)]
            got[k] = lax.ppermute(onward[at], "grp", way)

        step = 1
        while step < mems:
            sketches = jnp.stack([sketches, swap_mem(sketches, step)])
            step *= 2
        sketches = sketches.reshape(-1, bin_sketch.shape[1])

        def scores(keys):
            shape = ((mems // 2, block, count * len(keys)), f32)
            held = ()
            for at, k in enumerate(keys):
                rows = (through, direct) if k == last else (got[k],)
                held = call(
                    functools.partial(score_kernel, len(rows), mems, last, at * count),
                    [shape] * 2, [SM] * 2 + [VM] * (1 + len(rows) + len(held)),
                    scratch=[pltpu.VMEM((members, count), f32)], mib=2,
                    flops=2 * members * width_here * count * 8,
                    alias=[(3 + len(rows) + i, i) for i in range(len(held))],
                )(me1, mine1, member_profile, *rows, *held)
            return held

        def reduce_mem(keep, send):
            value = keep + swap_mem(send, 1)
            while value.shape[0] > 1:
                n = value.shape[0] // 2
                value = value[:n] + swap_mem(value[n:], n * 2)
            return value[0]

        back = {}
        early = [0] + near + [last]
        summed = reduce_mem(*scores(early))
        for at, k in enumerate(early):
            part = summed[:, at * count : (at + 1) * count]
            back[k] = swap(part, k) if k else part
        if far:
            summed = reduce_mem(*scores(far))
            for at, k in enumerate(far):
                back[k] = swap(summed[:, at * count : (at + 1) * count], k)

        product = lax.dot_general(sketches, rep_sketch, NT, preferred_element_type=f32)
        product = (product * bin_sketch.shape[1] ** (-0.5)).astype(bf)
        each = bin_sketch.shape[0]
        row = iota((product.shape[0], 1), 0) // each
        source = (row % mems ^ mine) * groups + (row // mems ^ me)
        within = iota((product.shape[0], 1), 0) % each
        perm = source * each + within == iota((1, product.shape[0]), 1)
        coarse_scores = pick(perm, product)

        keys = sorted(back)
        (fine,) = call(
            functools.partial(final_kernel, count, FW ** (-0.5), keys),
            [((2, block, rows_here), f32)], [SM] * 2 + [VM] * (2 + len(keys)),
        )(me1, mine1, places, lives, *[back[k] for k in keys])
        return (coarse_scores, fine.transpose(2, 0, 1))

    return local


def solution(mesh):
    local = make_local(mesh.shape["grp"], mesh.shape["mem"])

    return jax.shard_map(
        local,
        mesh=mesh,
        in_specs=(
            P(("grp", "mem"), None),
            P(("grp", "mem"), None),
            P("grp", "mem"),
            P("grp", None, "mem"),
            P("grp", None),
            P(),
            P(),
        ),
        out_specs=(P(None, ("grp", "mem")), P("grp", None, "mem")),
        check_vma=False,
    )
```

time: 80.7 us -> 62 us (0.77)
  Pallas kernels: 22.3 us -> 10.1 us
  other arithmetic: 4.49 us -> 0.91 us
  local copies, waits for them, and re-layouts: 4.82 us -> 2.89 us
  waiting for transfers between devices: 17.2 us -> 16.3 us
    pallas_call x5 -> x6, Pallas kernels: 20.6 us -> 9.16 us  [the longest x4 7.5 us: scores(): call(functools.partial(score_kernel, len(rows), mems, last, at * count),...]
    ppermute x1, starting transfers between devices: 0.01 us -> 2.62 us  [local(): got[k] = lax.ppermute(onward[at], 'grp', way)]
    ppermute x8 -> x7, waiting for transfers between devices: 10.1 us -> 7.47 us  [swap(): return lax.ppermute(value, 'grp', [(i, i ^ key) for i in range(groups)])]
    ppermute x8 -> x7, starting transfers between devices: 17.5 us -> 15 us  [swap(): return lax.ppermute(value, 'grp', [(i, i ^ key) for i in range(groups)])]
    another operation x3 -> x0, other arithmetic: 1.84 us -> none  [the longest x1 0.66 us: local(): jnp.stack([inner] + [jnp.where(inner == 1, me ^ last ^ k, me ^ k) for k i...]
    add x2, other arithmetic: 1.77 us -> 0.03 us  [reduce_mem(): value = keep + swap_mem(send, 1)]
    ppermute x9, waiting for transfers between devices: 7.16 us -> 8.46 us  [swap_mem(): return lax.ppermute(value, 'mem', [(i, i ^ key) for i in range(mems)])]
    ppermute x9, starting transfers between devices: 8.04 us -> 7.14 us  [swap_mem(): return lax.ppermute(value, 'mem', [(i, i ^ key) for i in range(mems)])]
  transfers between devices with their start and end apart: 20 -> 20, of which waited for: 8 -> 8; matrix products, arithmetic and copies ran while one was open for 9% -> 4% of each run, Pallas kernels for 26% -> 15%
where the time goes in v3:
time: 62 us; the launch traced here: 61.7 us
  starting transfers between devices  29.4 us (47%)
  waiting for transfers between devices  16.3 us (26%)
  Pallas kernels  10.1 us (16%)
  local copies, waits for them, and re-layouts  2.89 us (5%)
  matrix products  1.23 us (2%)
  other arithmetic  0.91 us (1%)
  between operations  0.88 us (1%)
    ppermute x7, starting transfers between devices, swap(): return lax.ppermute(value, 'grp', [(i, i ^ key) for i in range(groups)])  15 us
    ppermute x9, waiting for transfers between devices, swap_mem(): return lax.ppermute(value, 'mem', [(i, i ^ key) for i in range(mems)])  8.46 us
    pallas_call x4, Pallas kernels, scores(): call(functools.partial(score_kernel, len(rows), mems, last, at * count),...  7.5 us
    ppermute x7, waiting for transfers between devices, swap(): return lax.ppermute(value, 'grp', [(i, i ^ key) for i in range(groups)])  7.47 us
    ppermute x9, starting transfers between devices, swap_mem(): return lax.ppermute(value, 'mem', [(i, i ^ key) for i in range(mems)])  7.14 us
    ppermute x1, starting transfers between devices, local(): direct = lax.ppermute(picked[last], 'grp', outer)  3.14 us
    unnamed x6, local copies, waits for them, and re-layouts  2.79 us
    ppermute x1, starting transfers between devices, local(): got[k] = lax.ppermute(onward[at], 'grp', way)  2.62 us
  transfers between devices with their start and end apart: 20, of which 8 were waited for; matrix products, arithmetic and copies ran while one was open for 4% of the time, Pallas kernels for 15%

profile of v3, /device:TPU:0, one launch (start us, length us, event | category | flops | bytes accessed | tf_op | source)
XLA Modules:
  0.0 61.7 jit_solution(10270970173014151307)
XLA Ops:
  1.5 1.6 %shard_map.86 = (s32[2,64]{1,0:T(2,128)S(1)}, s32[2,64]{1,0:T(2,128)S(1)}, bf16[48,4096]{1,0:T(8,128)(2,1)S(1)}, bf16[48,4096]{1,0:T(8,128)(2,1)S(1)}, bf16[48,4...) custom-call(s32[1]{0:T(128)} %bitcast.11.me, s32[12]{0:T(128)} %slots_far.1, s32[12]{0:T(128)} %sizes_far.1, ...), custom_call_target="tpu_custom_call" | custom-call | bytes 262144 | tf_op jit(solution)/shard_map/pallas_call | solution.py:184
  3.1 5.9 %collective-permute-start.9 = (bf16[48,4096]{1,0:T(8,128)(2,1)S(1)}, bf16[48,4096]{1,0:T(8,128)(2,1)S(1)}, u32[]{:S(2)}, u32[]{:S(2)}) collective-permute-start(bf16[48,4096]{1,0:T(8,128)(2,1)S(1)} %get-tuple-element.23), channel_id=1, source_target_pairs={{0,8},{8,0},{16,24},{24,16},{1,9},{9,1},{17,25},{25,17},{2,10},{10... | collective-permute-start | bytes 1179656 | tf_op jit(solution)/shard_map/ppermute | solution.py:159
  9.1 1.8 %collective-permute-start.1 = (bf16[8,1024]{1,0:T(8,128)(2,1)}, bf16[8,1024]{1,0:T(8,128)(2,1)S(1)}, u32[]{:S(2)}, u32[]{:S(2)}) collective-permute-start(bf16[8,1024]{1,0:T(8,128)(2,1)} %param.7), channel_id=1, source_target_pairs={{0,16},{8,24},{16,0},{24,8},{1,17},{9,25},{17,1},{25,9},{2,18},{10... | collective-permute-start | bytes 49160 | tf_op jit(solution)/shard_map/ppermute | solution.py:159
  11.0 2.5 %collective-permute-start.2 = (bf16[8,1024]{1,0:T(8,128)(2,1)}, bf16[8,1024]{1,0:T(8,128)(2,1)S(1)}, u32[]{:S(2)}, u32[]{:S(2)}) collective-permute-start(bf16[8,1024]{1,0:T(8,128)(2,1)} %param.7), channel_id=1, source_target_pairs={{0,24},{8,16},{16,8},{24,0},{1,25},{9,17},{17,9},{25,1},{2,26},{10... | collective-permute-start | bytes 49160 | tf_op jit(solution)/shard_map/ppermute | solution.py:159
  13.5 4.9 %collective-permute-done = bf16[8,1024]{1,0:T(8,128)(2,1)S(1)} collective-permute-done((bf16[8,1024]{1,0:T(8,128)(2,1)}, bf16[8,1024]{1,0:T(8,128)(2,1)S(1)}, u32[]{:S(2)}, u32[]{:S(2)}) %collective-permute-start) | collective-permute-done | bytes 16416 | tf_op jit(solution)/shard_map/ppermute | solution.py:159
  18.4 3.1 %collective-permute-start.8 = (bf16[48,4096]{1,0:T(8,128)(2,1)S(1)}, bf16[48,4096]{1,0:T(8,128)(2,1)S(1)}, u32[]{:S(2)}, u32[]{:S(2)}) collective-permute-start(bf16[48,4096]{1,0:T(8,128)(2,1)S(1)} %get-tuple-element.22), channel_id=1, source_target_pairs={{0,24},{24,0},{1,25},{25,1},{2,26},{26,2},{3,27},{27,3},{4,28},{28... | collective-permute-start | bytes 1179656 | tf_op jit(solution)/shard_map/ppermute | solution.py:204
  23.0 2.8 %copy-done.1 = bf16[3,256,4096]{2,1,0:T(8,128)(2,1)S(1)} copy-done((bf16[3,256,4096]{2,1,0:T(8,128)(2,1)S(1)}, bf16[3,256,4096]{2,1,0:T(8,128)(2,1)}, u32[]{:S(2)}) %copy-start.1) | copy-done | bytes 6291480
  25.8 1.8 %shard_map.88 = (f32[4,32,144]{2,1,0:T(8,128)S(1)}, f32[4,32,144]{2,1,0:T(8,128)S(1)}) custom-call(s32[1]{0:T(128)} %bitcast.11.me, s32[1]{0:T(128)} %bitcast.12.mine, bf16[3,256,4096]{2,1,0:T(8,128)(2,1)S(1)} %copy-done.1, bf16[48,4096]{1,0:T(8,128)(2,1)S(1)} %get-tuple-element.24.refs_0_), custom_call_target="tpu_custom_call" | custom-call | flops 805306368 | bytes 262144 | tf_op jit(solution)/shard_map/pallas_call | solution.py:225
  27.7 1.6 %collective-permute-start.4 = (bf16[2,4,8,1024]{3,2,1,0:T(8,128)(2,1)S(1)}, bf16[2,4,8,1024]{3,2,1,0:T(8,128)(2,1)S(1)}, u32[]{:S(2)}, u32[]{:S(2)}) collective-permute-start(bf16[2,4,8,1024]{3,2,1,0:T(8,128)(2,1)S(1)} %get-tuple-element.37), channel_id=1, source_target_pairs={{0,2},{1,3},{2,0},{3,1},{4,6},{5,7},{6,4},{7,5},{8,10},{9,11},{10,... | collective-permute-start | bytes 393224 | tf_op jit(solution)/shard_map/ppermute | solution.py:162
  29.3 1.9 %shard_map.89 = (f32[4,32,144]{2,1,0:T(8,128)S(1)}, f32[4,32,144]{2,1,0:T(8,128)S(1)}) custom-call(s32[1]{0:T(128)} %bitcast.11.me, s32[1]{0:T(128)} %bitcast.12.mine, bf16[3,256,4096]{2,1,0:T(8,128)(2,1)S(1)} %copy-done.2, bf16[48,4096]{1,0:T(8,128)(2,1)S(1)} %collective-permute-done.9.refs_0_, ...), custom_call_target="tpu_custom_call", output_to_operand_aliasing={{0}: (4, {}), {1}: (5, {})} | custom-call | flops 805306368 | bytes 262144 | tf_op jit(solution)/shard_map/pallas_call | solution.py:225
  31.2 2.6 %collective-permute-start.14 = (bf16[48,4096]{1,0:T(8,128)(2,1)S(1)}, bf16[48,4096]{1,0:T(8,128)(2,1)S(1)}, u32[]{:S(2)}, u32[]{:S(2)}) collective-permute-start(bf16[48,4096]{1,0:T(8,128)(2,1)S(1)} %get-tuple-element.31), channel_id=1, source_target_pairs={{0,16},{8,0},{16,24},{24,8},{1,17},{9,1},{17,25},{25,9},{2,18},{10... | collective-permute-start | bytes 1179656 | tf_op jit(solution)/shard_map/ppermute | solution.py:212
  33.8 1.9 %shard_map.90 = (f32[4,32,144]{2,1,0:T(8,128)S(1)}, f32[4,32,144]{2,1,0:T(8,128)S(1)}) custom-call(s32[1]{0:T(128)} %bitcast.11.me, s32[1]{0:T(128)} %bitcast.12.mine, bf16[3,256,4096]{2,1,0:T(8,128)(2,1)S(1)} %copy-done.2, bf16[48,4096]{1,0:T(8,128)(2,1)S(1)} %get-tuple-element.21.refs_0_, ...), custom_call_target="tpu_custom_call", output_to_operand_aliasing={{0}: (5, {}), {1}: (6, {})} | custom-call | flops 805306368 | bytes 262144 | tf_op jit(solution)/shard_map/pallas_call | solution.py:225
  35.9 1.3 %collective-permute-done.10 = f32[4,32,144]{2,1,0:T(8,128)S(1)} collective-permute-done((f32[4,32,144]{2,1,0:T(8,128)S(1)}, f32[4,32,144]{2,1,0:T(8,128)S(1)}, u32[]{:S(2)}, u32[]{:S(2)}) %collective-permute-start.10) | collective-permute-done | bytes 73760 | tf_op jit(solution)/shard_map/ppermute | solution.py:162
  37.2 1.6 %collective-permute-start.11 = (f32[2,32,144]{2,1,0:T(8,128)S(1)}, f32[2,32,144]{2,1,0:T(8,128)S(1)}, u32[]{:S(2)}, u32[]{:S(2)}) collective-permute-start(f32[2,32,144]{2,1,0:T(8,128)S(1)} %slice.45), channel_id=1, source_target_pairs={{0,4},{1,5},{2,6},{3,7},{4,0},{5,1},{6,2},{7,3},{8,12},{9,13},{10,... | collective-permute-start | bytes 110600 | tf_op jit(solution)/shard_map/ppermute | solution.py:162
  39.4 2.3 %collective-permute-done.11 = f32[2,32,144]{2,1,0:T(8,128)S(1)} collective-permute-done((f32[2,32,144]{2,1,0:T(8,128)S(1)}, f32[2,32,144]{2,1,0:T(8,128)S(1)}, u32[]{:S(2)}, u32[]{:S(2)}) %collective-permute-start.11) | collective-permute-done | bytes 36896 | tf_op jit(solution)/shard_map/ppermute | solution.py:162
  42.9 1.8 %shard_map.91 = (f32[4,32,48]{2,1,0:T(8,128)S(1)}, f32[4,32,48]{2,1,0:T(8,128)S(1)}) custom-call(s32[1]{0:T(128)} %bitcast.11.me, s32[1]{0:T(128)} %bitcast.12.mine, bf16[3,256,4096]{2,1,0:T(8,128)(2,1)S(1)} %copy-done.2, bf16[48,4096]{1,0:T(8,128)(2,1)S(1)} %collective-permute-done.14.refs_0_), custom_call_target="tpu_custom_call" | custom-call | flops 805306368 | bytes 262144 | tf_op jit(solution)/shard_map/pallas_call | solution.py:225
  44.8 2.3 %collective-permute-done.5 = bf16[2,2,4,8,1024]{4,3,2,1,0:T(8,128)(2,1)S(1)} collective-permute-done((bf16[2,2,4,8,1024]{4,3,2,1,0:T(8,128)(2,1)S(1)}, bf16[2,2,4,8,1024]{4,3,2,1,0:T(8,128)(2,1)S(1)}, u32[]{:S(2)}, u32[]{:S(2)}) %collective-permute-start.5) | collective-permute-done | bytes 262176 | tf_op jit(solution)/shard_map/ppermute | solution.py:162
  47.3 1.5 %collective-permute-start.16 = (f32[2,32,48]{2,1,0:T(8,128)S(1)}, f32[2,32,48]{2,1,0:T(8,128)S(1)}, u32[]{:S(2)}, u32[]{:S(2)}) collective-permute-start(f32[2,32,48]{2,1,0:T(8,128)S(1)} %slice.51), channel_id=1, source_target_pairs={{0,4},{1,5},{2,6},{3,7},{4,0},{5,1},{6,2},{7,3},{8,12},{9,13},{10,... | collective-permute-start | bytes 36872 | tf_op jit(solution)/shard_map/ppermute | solution.py:162
  48.7 2.5 %collective-permute-done.16 = f32[2,32,48]{2,1,0:T(8,128)S(1)} collective-permute-done((f32[2,32,48]{2,1,0:T(8,128)S(1)}, f32[2,32,48]{2,1,0:T(8,128)S(1)}, u32[]{:S(2)}, u32[]{:S(2)}) %collective-permute-start.16) | collective-permute-done | bytes 12320 | tf_op jit(solution)/shard_map/ppermute | solution.py:162
  52.2 1.7 %collective-permute-start.13 = (f32[32,48]{1,0:T(8,128)S(1)}, f32[32,48]{1,0:T(8,128)S(1)}, u32[]{:S(2)}, u32[]{:S(2)}) collective-permute-start(f32[32,48]{1,0:T(8,128)S(1)} %get-tuple-element.41), channel_id=1, source_target_pairs={{0,8},{8,0},{16,24},{24,16},{1,9},{9,1},{17,25},{25,17},{2,10},{10... | collective-permute-start | bytes 18440 | tf_op jit(solution)/shard_map/ppermute | solution.py:159
  54.0 1.9 %collective-permute-start.19 = (f32[32,48]{1,0:T(8,128)S(1)}, f32[32,48]{1,0:T(8,128)S(1)}, u32[]{:S(2)}, u32[]{:S(2)}) collective-permute-start(f32[32,48]{1,0:T(8,128)S(1)} %get-tuple-element.40), channel_id=1, source_target_pairs={{0,24},{8,16},{16,8},{24,0},{1,25},{9,17},{17,9},{25,1},{2,26},{10... | collective-permute-start | bytes 18440 | tf_op jit(solution)/shard_map/ppermute | solution.py:159
  57.0 1.2 %convolution_convert_fusion = bf16[256,256]{1,0:T(8,128)(2,1)} fusion(bf16[256,1024]{1,0:T(8,128)(2,1)S(1)} %bitcast.24, bf16[256,1024]{1,0:T(8,128)(2,1)S(1)} %copy-done, s32[256]{0:T(256)S(1)} %fusion.7), kind=kOutput, calls=%fused_computation.2 | convolution fusion | flops 168165376 | bytes 1180672 | tf_op jit(solution)/shard_map/dot_general | solution.py:31
  58.2 1.3 %collective-permute-done.19.refs_3_ = f32[32,48]{1,0:T(8,128)S(1)} collective-permute-done((f32[32,48]{1,0:T(8,128)S(1)}, f32[32,48]{1,0:T(8,128)S(1)}, u32[]{:S(2)}, u32[]{:S(2)}) %collective-permute-start.19) | collective-permute-done | bytes 6176 | tf_op jit(solution)/shard_map/ppermute | solution.py:159
  59.5 1.2 %collective-permute-done.18.refs_2_ = f32[32,48]{1,0:T(8,128)S(1)} collective-permute-done((f32[32,48]{1,0:T(8,128)S(1)}, f32[32,48]{1,0:T(8,128)S(1)}, u32[]{:S(2)}, u32[]{:S(2)}) %collective-permute-start.18) | collective-permute-done | bytes 6176 | tf_op jit(solution)/shard_map/ppermute | solution.py:159
  (46 shorter events, 7.5 us)
Async XLA Ops:
  0.6 56.3 %copy-start = (bf16[256,1024]{1,0:T(8,128)(2,1)S(1)}, bf16[256,1024]{1,0:T(8,128)(2,1)}, u32[]{:S(2)}) copy-start(bf16[256,1024]{1,0:T(8,128)(2,1)} %param.8) | copy-start | bytes 1572868
  0.6 30.5 %collective-permute-start.7 = (bf16[64,4096]{1,0:T(8,128)(2,1)}, bf16[64,4096]{1,0:T(8,128)(2,1)S(1)}, u32[]{:S(2)}, u32[]{:S(2)}) collective-permute-start(bf16[64,4096]{1,0:T(8,128)(2,1)} %rows_far.1), channel_id=1, source_target_pairs={{8,16},{16,8},{9,17},{17,9},{10,18},{18,10},{11,19},{19,11},{12,20... | collective-permute-start | bytes 1572872 | tf_op jit(solution)/shard_map/ppermute | solution.py:178
  3.1 26.1 %collective-permute-start.9 = (bf16[48,4096]{1,0:T(8,128)(2,1)S(1)}, bf16[48,4096]{1,0:T(8,128)(2,1)S(1)}, u32[]{:S(2)}, u32[]{:S(2)}) collective-permute-start(bf16[48,4096]{1,0:T(8,128)(2,1)S(1)} %get-tuple-element.23), channel_id=1, source_target_pairs={{0,8},{8,0},{16,24},{24,16},{1,9},{9,1},{17,25},{25,17},{2,10},{10... | collective-permute-start | bytes 1179656 | tf_op jit(solution)/shard_map/ppermute | solution.py:159
  9.1 9.3 %collective-permute-start = (bf16[8,1024]{1,0:T(8,128)(2,1)}, bf16[8,1024]{1,0:T(8,128)(2,1)S(1)}, u32[]{:S(2)}, u32[]{:S(2)}) collective-permute-start(bf16[8,1024]{1,0:T(8,128)(2,1)} %param.7), channel_id=1, source_target_pairs={{0,8},{8,0},{16,24},{24,16},{1,9},{9,1},{17,25},{25,17},{2,10},{10... | collective-permute-start | bytes 49160 | tf_op jit(solution)/shard_map/ppermute | solution.py:159
  9.1 12.4 %collective-permute-start.1 = (bf16[8,1024]{1,0:T(8,128)(2,1)}, bf16[8,1024]{1,0:T(8,128)(2,1)S(1)}, u32[]{:S(2)}, u32[]{:S(2)}) collective-permute-start(bf16[8,1024]{1,0:T(8,128)(2,1)} %param.7), channel_id=1, source_target_pairs={{0,16},{8,24},{16,0},{24,8},{1,17},{9,25},{17,1},{25,9},{2,18},{10... | collective-permute-start | bytes 49160 | tf_op jit(solution)/shard_map/ppermute | solution.py:159
  11.0 11.2 %collective-permute-start.2 = (bf16[8,1024]{1,0:T(8,128)(2,1)}, bf16[8,1024]{1,0:T(8,128)(2,1)S(1)}, u32[]{:S(2)}, u32[]{:S(2)}) collective-permute-start(bf16[8,1024]{1,0:T(8,128)(2,1)} %param.7), channel_id=1, source_target_pairs={{0,24},{8,16},{16,8},{24,0},{1,25},{9,17},{17,9},{25,1},{2,26},{10... | collective-permute-start | bytes 49160 | tf_op jit(solution)/shard_map/ppermute | solution.py:159
  18.4 15.5 %collective-permute-start.8 = (bf16[48,4096]{1,0:T(8,128)(2,1)S(1)}, bf16[48,4096]{1,0:T(8,128)(2,1)S(1)}, u32[]{:S(2)}, u32[]{:S(2)}) collective-permute-start(bf16[48,4096]{1,0:T(8,128)(2,1)S(1)} %get-tuple-element.22), channel_id=1, source_target_pairs={{0,24},{24,0},{1,25},{25,1},{2,26},{26,2},{3,27},{27,3},{4,28},{28... | collective-permute-start | bytes 1179656 | tf_op jit(solution)/shard_map/ppermute | solution.py:204
  21.5 9.7 %collective-permute-start.6 = (s32[2,64]{1,0:T(2,128)S(1)}, s32[2,64]{1,0:T(2,128)S(1)}, u32[]{:S(2)}, u32[]{:S(2)}) collective-permute-start(s32[2,64]{1,0:T(2,128)S(1)} %get-tuple-element.18.places), channel_id=1, source_target_pairs={{8,16},{16,8},{9,17},{17,9},{10,18},{18,10},{11,19},{19,11},{12,20... | collective-permute-start | bytes 1544 | tf_op jit(solution)/shard_map/ppermute | solution.py:195
  22.9 4.7 %collective-permute-start.3 = (bf16[4,8,1024]{2,1,0:T(8,128)(2,1)S(1)}, bf16[4,8,1024]{2,1,0:T(8,128)(2,1)S(1)}, u32[]{:S(2)}, u32[]{:S(2)}) collective-permute-start(bf16[4,8,1024]{2,1,0:T(8,128)(2,1)S(1)} %get-tuple-element.39), channel_id=1, source_target_pairs={{0,1},{1,0},{2,3},{3,2},{4,5},{5,4},{6,7},{7,6},{8,9},{9,8},{10,11... | collective-permute-start | bytes 196616 | tf_op jit(solution)/shard_map/ppermute | solution.py:162
  23.0 2.8 %copy-start.1 = (bf16[3,256,4096]{2,1,0:T(8,128)(2,1)S(1)}, bf16[3,256,4096]{2,1,0:T(8,128)(2,1)}, u32[]{:S(2)}) copy-start(bf16[3,256,4096]{2,1,0:T(8,128)(2,1)} %members.7) | copy-start | bytes 18874372
  25.8 3.4 %copy-start.2 = (bf16[3,256,4096]{2,1,0:T(8,128)(2,1)S(1)}, bf16[3,256,4096]{2,1,0:T(8,128)(2,1)}, u32[]{:S(2)}) copy-start(bf16[3,256,4096]{2,1,0:T(8,128)(2,1)} %members.7) | copy-start | bytes 18874372
  27.7 11.1 %collective-permute-start.4 = (bf16[2,4,8,1024]{3,2,1,0:T(8,128)(2,1)S(1)}, bf16[2,4,8,1024]{3,2,1,0:T(8,128)(2,1)S(1)}, u32[]{:S(2)}, u32[]{:S(2)}) collective-permute-start(bf16[2,4,8,1024]{3,2,1,0:T(8,128)(2,1)S(1)} %get-tuple-element.37), channel_id=1, source_target_pairs={{0,2},{1,3},{2,0},{3,1},{4,6},{5,7},{6,4},{7,5},{8,10},{9,11},{10,... | collective-permute-start | bytes 393224 | tf_op jit(solution)/shard_map/ppermute | solution.py:162
  31.2 11.7 %collective-permute-start.14 = (bf16[48,4096]{1,0:T(8,128)(2,1)S(1)}, bf16[48,4096]{1,0:T(8,128)(2,1)S(1)}, u32[]{:S(2)}, u32[]{:S(2)}) collective-permute-start(bf16[48,4096]{1,0:T(8,128)(2,1)S(1)} %get-tuple-element.31), channel_id=1, source_target_pairs={{0,16},{8,0},{16,24},{24,8},{1,17},{9,1},{17,25},{25,9},{2,18},{10... | collective-permute-start | bytes 1179656 | tf_op jit(solution)/shard_map/ppermute | solution.py:212
  35.8 1.4 %collective-permute-start.10 = (f32[4,32,144]{2,1,0:T(8,128)S(1)}, f32[4,32,144]{2,1,0:T(8,128)S(1)}, u32[]{:S(2)}, u32[]{:S(2)}) collective-permute-start(f32[4,32,144]{2,1,0:T(8,128)S(1)} %get-tuple-element.30), channel_id=1, source_target_pairs={{0,1},{1,0},{2,3},{3,2},{4,5},{5,4},{6,7},{7,6},{8,9},{9,8},{10,11... | collective-permute-start | bytes 221192 | tf_op jit(solution)/shard_map/ppermute | solution.py:162
  37.2 4.5 %collective-permute-start.11 = (f32[2,32,144]{2,1,0:T(8,128)S(1)}, f32[2,32,144]{2,1,0:T(8,128)S(1)}, u32[]{:S(2)}, u32[]{:S(2)}) collective-permute-start(f32[2,32,144]{2,1,0:T(8,128)S(1)} %slice.45), channel_id=1, source_target_pairs={{0,4},{1,5},{2,6},{3,7},{4,0},{5,1},{6,2},{7,3},{8,12},{9,13},{10,... | collective-permute-start | bytes 110600 | tf_op jit(solution)/shard_map/ppermute | solution.py:162
  38.9 8.3 %collective-permute-start.5 = (bf16[2,2,4,8,1024]{4,3,2,1,0:T(8,128)(2,1)S(1)}, bf16[2,2,4,8,1024]{4,3,2,1,0:T(8,128)(2,1)S(1)}, u32[]{:S(2)}, u32[]{:S(2)}) collective-permute-start(bf16[2,2,4,8,1024]{4,3,2,1,0:T(8,128)(2,1)S(1)} %get-tuple-element.35), channel_id=1, source_target_pairs={{0,4},{1,5},{2,6},{3,7},{4,0},{5,1},{6,2},{7,3},{8,12},{9,13},{10,... | collective-permute-start | bytes 786440 | tf_op jit(solution)/shard_map/ppermute | solution.py:162
  41.8 7.0 %collective-permute-start.12 = (f32[1,32,144]{2,1,0:T(8,128)S(1)}, f32[1,32,144]{2,1,0:T(8,128)S(1)}, u32[]{:S(2)}, u32[]{:S(2)}) collective-permute-start(f32[1,32,144]{2,1,0:T(8,128)S(1)} %slice.47), channel_id=1, source_target_pairs={{0,2},{1,3},{2,0},{3,1},{4,6},{5,7},{6,4},{7,5},{8,10},{9,11},{10,... | collective-permute-start | bytes 55304 | tf_op jit(solution)/shard_map/ppermute | solution.py:162
  44.8 2.5 %collective-permute-start.15 = (f32[4,32,48]{2,1,0:T(8,128)S(1)}, f32[4,32,48]{2,1,0:T(8,128)S(1)}, u32[]{:S(2)}, u32[]{:S(2)}) collective-permute-start(f32[4,32,48]{2,1,0:T(8,128)S(1)} %get-tuple-element.33), channel_id=1, source_target_pairs={{0,1},{1,0},{2,3},{3,2},{4,5},{5,4},{6,7},{7,6},{8,9},{9,8},{10,11... | collective-permute-start | bytes 73736 | tf_op jit(solution)/shard_map/ppermute | solution.py:162
  47.3 4.0 %collective-permute-start.16 = (f32[2,32,48]{2,1,0:T(8,128)S(1)}, f32[2,32,48]{2,1,0:T(8,128)S(1)}, u32[]{:S(2)}, u32[]{:S(2)}) collective-permute-start(f32[2,32,48]{2,1,0:T(8,128)S(1)} %slice.51), channel_id=1, source_target_pairs={{0,4},{1,5},{2,6},{3,7},{4,0},{5,1},{6,2},{7,3},{8,12},{9,13},{10,... | collective-permute-start | bytes 36872 | tf_op jit(solution)/shard_map/ppermute | solution.py:162
  51.3 4.6 %collective-permute-start.17 = (f32[1,32,48]{2,1,0:T(8,128)S(1)}, f32[1,32,48]{2,1,0:T(8,128)S(1)}, u32[]{:S(2)}, u32[]{:S(2)}) collective-permute-start(f32[1,32,48]{2,1,0:T(8,128)S(1)} %slice.53), channel_id=1, source_target_pairs={{0,2},{1,3},{2,0},{3,1},{4,6},{5,7},{6,4},{7,5},{8,10},{9,11},{10,... | collective-permute-start | bytes 18440 | tf_op jit(solution)/shard_map/ppermute | solution.py:162
  52.2 6.0 %collective-permute-start.13 = (f32[32,48]{1,0:T(8,128)S(1)}, f32[32,48]{1,0:T(8,128)S(1)}, u32[]{:S(2)}, u32[]{:S(2)}) collective-permute-start(f32[32,48]{1,0:T(8,128)S(1)} %get-tuple-element.41), channel_id=1, source_target_pairs={{0,8},{8,0},{16,24},{24,16},{1,9},{9,1},{17,25},{25,17},{2,10},{10... | collective-permute-start | bytes 18440 | tf_op jit(solution)/shard_map/ppermute | solution.py:159
  54.0 5.5 %collective-permute-start.19 = (f32[32,48]{1,0:T(8,128)S(1)}, f32[32,48]{1,0:T(8,128)S(1)}, u32[]{:S(2)}, u32[]{:S(2)}) collective-permute-start(f32[32,48]{1,0:T(8,128)S(1)} %get-tuple-element.40), channel_id=1, source_target_pairs={{0,24},{8,16},{16,8},{24,0},{1,25},{9,17},{17,9},{25,1},{2,26},{10... | collective-permute-start | bytes 18440 | tf_op jit(solution)/shard_map/ppermute | solution.py:159
  55.9 4.9 %collective-permute-start.18 = (f32[32,48]{1,0:T(8,128)S(1)}, f32[32,48]{1,0:T(8,128)S(1)}, u32[]{:S(2)}, u32[]{:S(2)}) collective-permute-start(f32[32,48]{1,0:T(8,128)S(1)} %fusion.4), channel_id=1, source_target_pairs={{0,16},{8,24},{16,0},{24,8},{1,17},{9,25},{17,1},{25,9},{2,18},{10... | collective-permute-start | bytes 18440 | tf_op jit(solution)/shard_map/ppermute | solution.py:159

commit v4 on v3

--- a/solution.py
+++ b/solution.py
@@ -86,51 +86,79 @@
         outs[-1][...] = pick(hits(where, me[0], count), whole[...])
 
 
-def score_kernel(sources, mems, last, lane, me, mine, members, *refs):
-    ins, (keep, send, acc) = refs[:sources], refs[-3:]
+def score_kernel(keys, last, me, core, members, *refs):
+    keep, send, acc = refs[-3:]
+    ins = list(refs[: len(keys) + (last in keys)])
     slot_count, total, _ = members.shape
-    block = total // mems
-    count = acc.shape[1]
-
-    def put(src):
+    chips = keep.shape[1]
+    block = total // (2 * chips)
+
+    def put(ins):
         for s in range(slot_count):
-            acc[:, s * MOST : (s + 1) * MOST] = lax.dot_general(
-                members[s], src[s * MOST : (s + 1) * MOST, :], NT, preferred_element_type=jnp.float32
+            rows = [src[s * MOST : (s + 1) * MOST, :] for src in ins]
+            rows = jnp.concatenate(rows, axis=0) if len(rows) > 1 else rows[0]
+            product = lax.dot_general(members[s], rows, NT, preferred_element_type=jnp.float32)
+            acc[s] = product.T
+
+    def give(first, second):
+        for at, key in enumerate(keys):
+            for chip in range(chips):
+                for side, out in enumerate((first, second)):
+                    start = (chip * 2 + side) * block
+                    for s in range(slot_count):
+                        out[me[0] ^ key, chip, :, s * block : (s + 1) * block] = (
+                            acc[s, at * MOST : (at + 1) * MOST, start : start + block]
+                        )
+
+    if last in keys:
+        inner = is_inner(me, last)
+        pl.when(inner)(lambda: put(ins[:-1]))
+        pl.when(jnp.logical_not(inner))(lambda: put(ins[:-2] + ins[-1:]))
+    else:
+        put(ins)
+    pl.when(core[0] == 0)(lambda: give(keep, send))
+    pl.when(core[0] == 1)(lambda: give(send, keep))
+
+
+def gate_kernel(members, rows, out):
+    out[0:16, 0:128] = rows[0:16, 0:128]
+
+
+def half_kernel(key, other, me, core, members, rows, _, out, acc):
+    slot_count, chips = members.shape[0], out.shape[1]
+    block = members.shape[1] // (2 * chips)
+    starts = [pl.multiple_of((chip * 2 + (core[0] ^ other)) * block, block) for chip in range(chips)]
+    for s in range(slot_count):
+        half = jnp.concatenate([members[s, pl.ds(start, block), :] for start in starts], axis=0)
+        product = lax.dot_general(
+            half, rows[s * MOST : (s + 1) * MOST, :], NT, preferred_element_type=jnp.float32
+        )
+        acc[...] = product.T
+        for chip in range(chips):
+            out[me[0] ^ key, chip, :, s * block : (s + 1) * block] = (
+                acc[:, chip * block : (chip + 1) * block]
             )
 
-    if sources == 2:
-        inner = is_inner(me, last)
-
-        @pl.when(inner)
-        def _():
-            put(ins[0])
-
-        @pl.when(jnp.logical_not(inner))
-        def _():
-            put(ins[1])
-    else:
-        put(ins[0])
-    for p in range(mems // 2):
-        for core, out in ((0, keep), (1, send)):
-            at = (mine[0] ^ (p * 2 + core)) * block
-            out[p, :, lane : lane + count] = acc[pl.ds(pl.multiple_of(at, block), block), :]
-
-
-def final_kernel(count, scale, keys, me, mine, places, lives, *refs):
-    tables, out = refs[:-1], refs[-1]
+
+def final_kernel(slot_count, scale, mine, places, lives, parts, out):
+    groups, chips = parts.shape[:2]
     block, rows = out.shape[1], out.shape[2]
     member = iota((block, rows), 0) + mine[0] * block
+    tables = []
+    for group in range(groups):
+        total = parts[group, 0]
+        for chip in range(1, chips):
+            total = total + parts[group, chip]
+        for s in range(slot_count):
+            tables.append(total[:, s * block : (s + 1) * block])
+    table = jnp.concatenate(tables, axis=0)
     for r in range(2):
-        total = jnp.zeros((block, rows), jnp.float32)
-        where = places[r : r + 1]
-        for key, table in zip(keys, tables, strict=True):
-            wanted = iota((count, rows), 0) + (me[0] ^ key) * count
-            one = (where == wanted).astype(jnp.float32)
-            total = total + lax.dot_general(
-                table[...], one, NN,
-                precision=lax.Precision.HIGHEST, preferred_element_type=jnp.float32,
-            )
-        out[r] = jnp.where(member < lives[r : r + 1], total * scale, 0.0)
+        one = (places[r : r + 1] == iota((table.shape[0], rows), 0)).astype(jnp.float32)
+        score = lax.dot_general(
+            table, one, (((0,), (0,)), ((), ())),
+            precision=lax.Precision.HIGHEST, preferred_element_type=jnp.float32,
+        )
+        out[r] = jnp.where(member < lives[r : r + 1], score * scale, 0.0)
 
 
 def call(kernel, shapes, specs, scratch=(), flops=0, mib=4, alias=()):
@@ -150,16 +178,19 @@
     return pltpu.with_memory_space_constraint(value, pltpu.HBM)
 
 
-def make_local(groups, mems):
+def make_local(groups, chips):
     last = groups - 1
     half = groups // 2
     middle = (half - 1, half)
+    mems = 2 * chips
 
     def swap(value, key):
         return lax.ppermute(value, "grp", [(i, i ^ key) for i in range(groups)])
 
     def swap_mem(value, key):
-        return lax.ppermute(value, "mem", [(i, i ^ key) for i in range(mems)])
+        if key == 1:
+            return lax.ppermute(value, "core", [(0, 1), (1, 0)])
+        return lax.ppermute(value, "chip", [(i, i ^ (key // 2)) for i in range(chips)])
 
     def local(
         bin_sketch, rep_sketch, bin_profile, member_profile, bin_routes, owner_slot, cluster_sizes
@@ -169,9 +200,10 @@
         count = slot_count * MOST
         block = members // mems
         me = lax.axis_index("grp")
-        mine = lax.axis_index("mem")
-        me1, mine1 = me.reshape(1), mine.reshape(1)
+        core = lax.axis_index("core")
+        mine = lax.axis_index("chip") * 2 + core
         member_profile = pltpu.with_memory_space_constraint(member_profile, pltpu.VMEM)
+        me1, mine1, core1 = me.reshape(1), mine.reshape(1), core.reshape(1)
         bf, f32, i32 = jnp.bfloat16, jnp.float32, jnp.int32
         rows_out = ((count, width_here), bf)
 
@@ -195,13 +227,19 @@
         places_other = lax.ppermute(places, "grp", [(i, i ^ last) for i in middle])
 
         sketches = bin_sketch[None]
-        sketches = jnp.stack([bin_sketch] + [swap(bin_sketch, k) for k in range(1, groups)])
+        step = 1
+        while step < groups:
+            sketches = jnp.concatenate([sketches, swap(sketches, step)])
+            step *= 2
 
         got = {0: picked[0]}
         for k in near:
             got[k] = swap(picked[k], k)
         outer = [(i, i ^ last) for i in range(groups) if i not in middle]
-        direct = lax.ppermute(picked[last], "grp", outer)
+        (rows,) = call(
+            gate_kernel, [rows_out], [VM] * 2, mib=2, alias=[(1, 0)]
+        )(member_profile, picked[last])
+        direct = lax.ppermute(rows, "grp", outer)
         *onward, through = call(
             functools.partial(forward_kernel, far, last),
             [rows_out] * (len(far) + 1), [SM] + [VM] * (2 + len(far)),
@@ -217,37 +255,38 @@
             step *= 2
         sketches = sketches.reshape(-1, bin_sketch.shape[1])
 
-        def scores(keys):
-            shape = ((mems // 2, block, count * len(keys)), f32)
-            held = ()
-            for at, k in enumerate(keys):
-                rows = (through, direct) if k == last else (got[k],)
-                held = call(
-                    functools.partial(score_kernel, len(rows), mems, last, at * count),
-                    [shape] * 2, [SM] * 2 + [VM] * (1 + len(rows) + len(held)),
-                    scratch=[pltpu.VMEM((members, count), f32)], mib=2,
-                    flops=2 * members * width_here * count * 8,
-                    alias=[(3 + len(rows) + i, i) for i in range(len(held))],
-                )(me1, mine1, member_profile, *rows, *held)
-            return held
-
-        def reduce_mem(keep, send):
-            value = keep + swap_mem(send, 1)
-            while value.shape[0] > 1:
-                n = value.shape[0] // 2
-                value = value[:n] + swap_mem(value[n:], n * 2)
-            return value[0]
-
-        back = {}
-        early = [0] + near + [last]
-        summed = reduce_mem(*scores(early))
-        for at, k in enumerate(early):
-            part = summed[:, at * count : (at + 1) * count]
-            back[k] = swap(part, k) if k else part
-        if far:
-            summed = reduce_mem(*scores(far))
-            for at, k in enumerate(far):
-                back[k] = swap(summed[:, at * count : (at + 1) * count], k)
+        shape = ((groups, chips, MOST, 128), f32)
+        held = ()
+        got[last] = through
+        for keys in ([0] + near + [last],):
+            rows = [got[k] for k in keys] + ([direct] if last in keys else [])
+            held = call(
+                functools.partial(score_kernel, keys, last), [shape] * 2,
+                [SM] * 2 + [VM] * (1 + len(rows) + len(held)),
+                scratch=[pltpu.VMEM((slot_count, MOST * len(keys), members), f32)],
+                mib=2,
+                flops=2 * members * width_here * count * 8,
+                alias=[(3 + len(rows) + i, i) for i in range(len(held))],
+            )(me1, core1, member_profile, *rows, *held)
+        keep, send = held
+
+        def one_side(key, other, out):
+            (out,) = call(
+                functools.partial(half_kernel, key, other), [shape], [SM] * 2 + [VM] * 3,
+                scratch=[pltpu.VMEM((MOST, members // 2), f32)], mib=2,
+                flops=members * width_here * count * 8, alias=[(4, 0)],
+            )(me1, core1, member_profile, got[key], out)
+            return out
+
+        for k in far:
+            send = one_side(k, 1, send)
+        send = swap_mem(send, 1)
+        for k in far:
+            keep = one_side(k, 0, keep)
+        parts = keep + send
+        parts = parts.reshape(groups * chips, MOST, 128)
+        parts = lax.all_to_all(parts, ("grp", "chip"), 0, 0, tiled=True)
+        parts = parts.reshape(groups, chips, MOST, 128)
 
         product = lax.dot_general(sketches, rep_sketch, NT, preferred_element_type=f32)
         product = (product * bin_sketch.shape[1] ** (-0.5)).astype(bf)
@@ -258,31 +297,33 @@
         perm = source * each + within == iota((1, product.shape[0]), 1)
         coarse_scores = pick(perm, product)
 
-        keys = sorted(back)
         (fine,) = call(
-            functools.partial(final_kernel, count, FW ** (-0.5), keys),
-            [((2, block, rows_here), f32)], [SM] * 2 + [VM] * (2 + len(keys)),
-        )(me1, mine1, places, lives, *[back[k] for k in keys])
+            functools.partial(final_kernel, slot_count, FW ** (-0.5)),
+            [((2, block, rows_here), f32)], [SM] + [VM] * 3,
+        )(mine1, places, lives, parts)
         return (coarse_scores, fine.transpose(2, 0, 1))
 
     return local
 
 
 def solution(mesh):
-    local = make_local(mesh.shape["grp"], mesh.shape["mem"])
+    groups, chips = mesh.shape["grp"], mesh.shape["mem"] // 2
+    mesh = jax.sharding.Mesh(mesh.devices.reshape(groups, chips, 2), ("grp", "chip", "core"))
+    mem = ("chip", "core")
+    local = make_local(groups, chips)
 
     return jax.shard_map(
         local,
         mesh=mesh,
         in_specs=(
-            P(("grp", "mem"), None),
-            P(("grp", "mem"), None),
-            P("grp", "mem"),
-            P("grp", None, "mem"),
+            P(("grp", *mem), None),
+            P(("grp", *mem), None),
+            P("grp", mem),
+            P("grp", None, mem),
             P("grp", None),
             P(),
             P(),
         ),
-        out_specs=(P(None, ("grp", "mem")), P("grp", None, "mem")),
+        out_specs=(P(None, ("grp", *mem)), P("grp", None, mem)),
         check_vma=False,
     )

time: 62 us -> 80.1 us (1.29)
  waiting for transfers between devices: 16.3 us -> 32.4 us
  other arithmetic: 0.91 us -> 5.55 us
  starting transfers between devices: 29.4 us -> 26.6 us
  local copies, waits for them, and re-layouts: 2.89 us -> 5.58 us
  Pallas kernels: 10.1 us -> 7.47 us
    ppermute x7 -> x3, waiting for transfers between devices: 7.47 us -> 20.7 us  [swap(): return lax.ppermute(value, 'grp', [(i, i ^ key) for i in range(groups)])]
    ppermute x7 -> x3, starting transfers between devices: 15 us -> 6.22 us  [swap(): return lax.ppermute(value, 'grp', [(i, i ^ key) for i in range(groups)])]
    ppermute x10 -> x5, waiting for transfers between devices: 8.47 us -> 1.37 us  [the longest x2 1.24 us: swap_mem(): return lax.ppermute(value, 'core', [(0, 1), (1, 0)])]
    all_to_all x0 -> x1, waiting for transfers between devices: none -> 6.85 us  [local(): parts = lax.all_to_all(parts, ('grp', 'chip'), 0, 0, tiled=True)]
    all_to_all x0 -> x1, starting transfers between devices: none -> 4.38 us  [local(): parts = lax.all_to_all(parts, ('grp', 'chip'), 0, 0, tiled=True)]
    ppermute x1, starting transfers between devices: 2.62 us -> 6.94 us  [local(): got[k] = lax.ppermute(onward[at], 'grp', way)]
    another operation x4, other arithmetic: 0.84 us -> 4.15 us  [local(): sketches = jnp.stack([sketches, swap_mem(sketches, step)])]
    ppermute x1, waiting for transfers between devices: 0.33 us -> 3.5 us  [local(): got[k] = lax.ppermute(onward[at], 'grp', way)]
  transfers between devices with their start and end apart: 20 -> 12, of which waited for: 8 -> 7; matrix products, arithmetic and copies ran while one was open for 4% -> 8% of each run, Pallas kernels for 15% -> 8%
where the time goes in v4:
time: 80.1 us; the launch traced here: 79.7 us
  waiting for transfers between devices  32.4 us (40%)
  starting transfers between devices  26.6 us (33%)
  Pallas kernels  7.47 us (9%)
  local copies, waits for them, and re-layouts  5.58 us (7%)
  other arithmetic  5.55 us (7%)
  matrix products  1.23 us (2%)
    ppermute x3, waiting for transfers between devices, swap(): return lax.ppermute(value, 'grp', [(i, i ^ key) for i in range(groups)])  20.7 us
    ppermute x1, starting transfers between devices, local(): got[k] = lax.ppermute(onward[at], 'grp', way)  6.94 us
    all_to_all x1, waiting for transfers between devices, local(): parts = lax.all_to_all(parts, ('grp', 'chip'), 0, 0, tiled=True)  6.85 us
    ppermute x3, starting transfers between devices, swap(): return lax.ppermute(value, 'grp', [(i, i ^ key) for i in range(groups)])  6.22 us
    unnamed x10, local copies, waits for them, and re-layouts  5.58 us
    ppermute x1, starting transfers between devices, local(): direct = lax.ppermute(rows, 'grp', outer)  4.53 us
    all_to_all x1, starting transfers between devices, local(): parts = lax.all_to_all(parts, ('grp', 'chip'), 0, 0, tiled=True)  4.38 us
    another operation x4, other arithmetic, local(): sketches = jnp.stack([sketches, swap_mem(sketches, step)])  4.15 us
  transfers between devices with their start and end apart: 12, of which 7 were waited for; matrix products, arithmetic and copies ran while one was open for 8% of the time, Pallas kernels for 8%

profile of v4, /device:TPU:0, one launch (start us, length us, event | category | flops | bytes accessed | tf_op | source)
XLA Modules:
  0.0 79.7 jit_solution(15935587207543208355)
XLA Ops:
  0.6 3.1 %collective-permute-start = (bf16[1,8,1024]{2,1,0:T(8,128)(2,1)}, bf16[1,8,1024]{2,1,0:T(8,128)(2,1)S(1)}, u32[]{:S(2)}, u32[]{:S(2)}) collective-permute-start(bf16[1,8,1024]{2,1,0:T(8,128)(2,1)} %bitcast.22), channel_id=1, source_target_pairs={{0,8},{8,0},{16,24},{24,16},{1,9},{9,1},{17,25},{25,17},{2,10},{10... | collective-permute-start | bytes 49160 | tf_op jit(solution)/shard_map/ppermute | solution.py:188
  4.5 1.2 %collective-permute-done = bf16[1,8,1024]{2,1,0:T(8,128)(2,1)S(1)} collective-permute-done((bf16[1,8,1024]{2,1,0:T(8,128)(2,1)}, bf16[1,8,1024]{2,1,0:T(8,128)(2,1)S(1)}, u32[]{:S(2)}, u32[]{:S(2)}) %collective-permute-start) | collective-permute-done | bytes 16416 | tf_op jit(solution)/shard_map/ppermute | solution.py:188
  6.4 3.0 %collective-permute-start.1 = (bf16[2,8,1024]{2,1,0:T(8,128)(2,1)S(1)}, bf16[2,8,1024]{2,1,0:T(8,128)(2,1)S(1)}, u32[]{:S(2)}, u32[]{:S(2)}) collective-permute-start(bf16[2,8,1024]{2,1,0:T(8,128)(2,1)S(1)} %pad_maximum_fusion.4), channel_id=1, source_target_pairs={{0,16},{8,24},{16,0},{24,8},{1,17},{9,25},{17,1},{25,9},{2,18},{10... | collective-permute-start | bytes 98312 | tf_op jit(solution)/shard_map/ppermute | solution.py:188
  9.4 12.1 %collective-permute-done.1 = bf16[2,8,1024]{2,1,0:T(8,128)(2,1)S(1)} collective-permute-done((bf16[2,8,1024]{2,1,0:T(8,128)(2,1)S(1)}, bf16[2,8,1024]{2,1,0:T(8,128)(2,1)S(1)}, u32[]{:S(2)}, u32[]{:S(2)}) %collective-permute-start.1) | collective-permute-done | bytes 32800 | tf_op jit(solution)/shard_map/ppermute | solution.py:188
  21.5 0.7 fusion.8
  22.3 1.2 %collective-permute-done.2 = bf16[4,8,1024]{2,1,0:T(8,128)(2,1)S(1)} collective-permute-done((bf16[4,8,1024]{2,1,0:T(8,128)(2,1)S(1)}, bf16[4,8,1024]{2,1,0:T(8,128)(2,1)S(1)}, u32[]{:S(2)}, u32[]{:S(2)}) %collective-permute-start.2) | collective-permute-done | bytes 65568 | tf_op jit(solution)/shard_map/ppermute | solution.py:192
  24.2 1.5 %collective-permute-start.3 = (bf16[2,4,8,1024]{3,2,1,0:T(8,128)(2,1)}, bf16[2,4,8,1024]{3,2,1,0:T(8,128)(2,1)}, u32[]{:S(2)}, u32[]{:S(2)}) collective-permute-start(bf16[2,4,8,1024]{3,2,1,0:T(8,128)(2,1)} %get-tuple-element.25), channel_id=1, source_target_pairs={{0,2},{2,0},{4,6},{6,4},{1,3},{3,1},{5,7},{7,5},{8,10},{10,8},{12,... | collective-permute-start | bytes 393224 | tf_op jit(solution)/shard_map/ppermute | solution.py:193
  25.7 2.1 %shard_map.86 = (s32[2,64]{1,0:T(2,128)S(1)}, s32[2,64]{1,0:T(2,128)S(1)}, bf16[48,4096]{1,0:T(8,128)(2,1)}, bf16[48,4096]{1,0:T(8,128)(2,1)S(1)}, bf16[48,4096]...) custom-call(s32[1]{0:T(128)} %bitcast.9.me, s32[12]{0:T(128)} %slots_far.1, s32[12]{0:T(128)} %sizes_far.1, ...), custom_call_target="tpu_custom_call" | custom-call | bytes 262144 | tf_op jit(solution)/shard_map/pallas_call | solution.py:216
  27.8 2.8 %copy-done.1 = bf16[3,256,4096]{2,1,0:T(8,128)(2,1)S(1)} copy-done((bf16[3,256,4096]{2,1,0:T(8,128)(2,1)S(1)}, bf16[3,256,4096]{2,1,0:T(8,128)(2,1)}, u32[]{:S(2)}) %copy-start.1) | copy-done | bytes 6291480
  30.6 4.5 %collective-permute-start.9 = (bf16[48,4096]{1,0:T(8,128)(2,1)S(1)}, bf16[48,4096]{1,0:T(8,128)(2,1)S(1)}, u32[]{:S(2)}, u32[]{:S(2)}) collective-permute-start(bf16[48,4096]{1,0:T(8,128)(2,1)S(1)} %shard_map.88), channel_id=1, source_target_pairs={{0,24},{24,0},{1,25},{25,1},{2,26},{26,2},{3,27},{27,3},{4,28},{28... | collective-permute-start | bytes 1179656 | tf_op jit(solution)/shard_map/ppermute | solution.py:242
  35.9 6.9 %collective-permute-start.7 = (bf16[48,4096]{1,0:T(8,128)(2,1)S(1)}, bf16[48,4096]{1,0:T(8,128)(2,1)S(1)}, u32[]{:S(2)}, u32[]{:S(2)}) collective-permute-start(bf16[48,4096]{1,0:T(8,128)(2,1)S(1)} %get-tuple-element.15), channel_id=1, source_target_pairs={{0,16},{8,0},{16,24},{24,8},{1,17},{9,1},{17,25},{25,9},{2,18},{10... | collective-permute-start | bytes 1179656 | tf_op jit(solution)/shard_map/ppermute | solution.py:250
  42.9 1.7 %fusion.10 = (bf16[1,2,2,4,8,1024]{5,4,3,2,1,0:T(8,128)(2,1)}, bf16[2,2,4,8,1024]{4,3,2,1,0:T(8,128)(2,1)}) fusion(bf16[1,2,4,8,1024]{4,3,2,1,0:T(8,128)(2,1)} %bitcast.4, bf16[1,2,4,8,1024]{4,3,2,1,0:T(8,128)(2,1)S(1)} %get-tuple-element.24), kind=kLoop, calls=%fused_computation.29 | loop fusion | flops 131072 | bytes 786432 | tf_op jit(solution)/shard_map/stack | solution.py:254
  44.6 1.5 %collective-permute-start.4 = (bf16[2,2,4,8,1024]{4,3,2,1,0:T(8,128)(2,1)}, bf16[2,2,4,8,1024]{4,3,2,1,0:T(8,128)(2,1)}, u32[]{:S(2)}, u32[]{:S(2)}) collective-permute-start(bf16[2,2,4,8,1024]{4,3,2,1,0:T(8,128)(2,1)} %get-tuple-element.23), channel_id=1, source_target_pairs={{0,4},{2,6},{4,0},{6,2},{1,5},{3,7},{5,1},{7,3},{8,12},{10,14},{12... | collective-permute-start | bytes 786440 | tf_op jit(solution)/shard_map/ppermute | solution.py:193
  46.3 7.4 %collective-permute-done.8.refs_1_ = bf16[48,4096]{1,0:T(8,128)(2,1)S(1)} collective-permute-done((bf16[48,4096]{1,0:T(8,128)(2,1)}, bf16[48,4096]{1,0:T(8,128)(2,1)S(1)}, u32[]{:S(2)}, u32[]{:S(2)}) %collective-permute-start.8) | collective-permute-done | bytes 393248 | tf_op jit(solution)/shard_map/ppermute | solution.py:188
  53.7 2.8 %copy-done.2 = bf16[3,256,4096]{2,1,0:T(8,128)(2,1)S(1)} copy-done((bf16[3,256,4096]{2,1,0:T(8,128)(2,1)S(1)}, bf16[3,256,4096]{2,1,0:T(8,128)(2,1)}, u32[]{:S(2)}) %copy-start.2) | copy-done | bytes 6291480
  56.5 2.0 %shard_map.89 = (f32[4,4,16,128]{3,2,1,0:T(8,128)S(1)}, f32[4,4,16,128]{3,2,1,0:T(8,128)S(1)}) custom-call(s32[1]{0:T(128)} %bitcast.9.me, s32[1]{0:T(128)} %bitcast.11.core, bf16[3,256,4096]{2,1,0:T(8,128)(2,1)S(1)} %copy-done.2, bf16[48,4096]{1,0:T(8,128)(2,1)S(1)} %get-tuple-element.16.refs_0_, bf16[48,4096]{1,0:T(8,128)(2,1)S(1)} %collective-permute-done.8.refs_1_, ...), custom_call_target="tpu_custom_call" | custom-call | flops 805306368 | bytes 262144 | tf_op jit(solution)/shard_map/pallas_call | solution.py:263
  58.5 3.5 %collective-permute-done.7.rows = bf16[48,4096]{1,0:T(8,128)(2,1)S(1)} collective-permute-done((bf16[48,4096]{1,0:T(8,128)(2,1)S(1)}, bf16[48,4096]{1,0:T(8,128)(2,1)S(1)}, u32[]{:S(2)}, u32[]{:S(2)}) %collective-permute-start.7) | collective-permute-done | bytes 393248 | tf_op jit(solution)/shard_map/ppermute | solution.py:250
  62.0 1.1 %shard_map.91 = f32[4,4,16,128]{3,2,1,0:T(8,128)S(1)} custom-call(s32[1]{0:T(128)} %bitcast.9.me, s32[1]{0:T(128)} %bitcast.11.core, bf16[3,256,4096]{2,1,0:T(8,128)(2,1)S(1)} %copy-done.3, bf16[48,4096]{1,0:T(8,128)(2,1)S(1)} %collective-permute-done.7.rows, f32[4,4,16,128]{3,2,1,0:T(8,128)S(1)} %get-tuple-element.21._), custom_call_target="tpu_custom_call", output_to_operand_aliasing={{}: (4, {})} | custom-call | flops 402653184 | bytes 262144 | tf_op jit(solution)/shard_map/pallas_call | solution.py:274
  63.3 1.0 %pad_maximum_fusion = bf16[2,2,2,4,8,1024]{5,4,3,2,1,0:T(8,128)(2,1)S(1)} fusion(bf16[1,2,2,4,8,1024]{5,4,3,2,1,0:T(8,128)(2,1)} %bitcast.6, bf16[1,2,2,4,8,1024]{5,4,3,2,1,0:T(8,128)(2,1)S(1)} %copy-done.4), kind=kLoop, calls=%fused_computation.3 | loop fusion | flops 262144 | bytes 1048576 | tf_op jit(solution)/shard_map/stack | solution.py:254
  64.3 1.1 %shard_map.90 = f32[4,4,16,128]{3,2,1,0:T(8,128)S(1)} custom-call(s32[1]{0:T(128)} %bitcast.9.me, s32[1]{0:T(128)} %bitcast.11.core, bf16[3,256,4096]{2,1,0:T(8,128)(2,1)S(1)} %copy-done.3, bf16[48,4096]{1,0:T(8,128)(2,1)S(1)} %collective-permute-done.7.rows, f32[4,4,16,128]{3,2,1,0:T(8,128)S(1)} %get-tuple-element.20._), custom_call_target="tpu_custom_call", output_to_operand_aliasing={{}: (4, {})} | custom-call | flops 402653184 | bytes 262144 | tf_op jit(solution)/shard_map/pallas_call | solution.py:274
  66.1 4.4 %all-to-all-start = ((f32[16,16,128]{2,1,0:T(8,128)}), f32[16,16,128]{2,1,0:T(8,128)S(1)}, u32[]{:S(2)}, u32[]{:S(2)}) async-start(f32[16,16,128]{2,1,0:T(8,128)} %bitcast.12), calls=%async_computation | async-start | bytes 262144 | tf_op jit(solution)/shard_map/all_to_all | solution.py:288
  70.5 1.2 %convolution_convert_fusion = bf16[256,256]{1,0:T(8,128)(2,1)} fusion(bf16[256,1024]{1,0:T(8,128)(2,1)S(1)} %bitcast.21, bf16[256,1024]{1,0:T(8,128)(2,1)S(1)} %copy-done, s32[256]{0:T(256)S(1)} %fusion.5), kind=kOutput, calls=%fused_computation.2 | convolution fusion | flops 168165376 | bytes 1180672 | tf_op jit(solution)/shard_map/dot_general | solution.py:31
  71.7 6.8 %all-to-all-done = f32[16,16,128]{2,1,0:T(8,128)S(1)} async-done(((f32[16,16,128]{2,1,0:T(8,128)}), f32[16,16,128]{2,1,0:T(8,128)S(1)}, u32[]{:S(2)}, u32[]{:S(2)}) %all-to-all-start) | async-done | bytes 131104 | tf_op jit(solution)/shard_map/all_to_all | solution.py:288
  78.6 1.1 %shard_map.92 = f32[2,32,64]{2,1,0:T(8,128)} custom-call(s32[1]{0:T(128)} %bitcast.8.mine, s32[2,64]{1,0:T(2,128)S(1)} %get-tuple-element.12.places, s32[2,64]{1,0:T(2,128)S(1)} %get-tuple-element.13.lives, f32[4,4,16,128]{3,2,1,0:T(8,128)S(1)} %bitcast.20), custom_call_target="tpu_custom_call" | custom-call | bytes 262144 | tf_op jit(solution)/shard_map/pallas_call | solution.py:300
  (25 shorter events, 3.8 us)
Async XLA Ops:
  0.6 69.9 %copy-start = (bf16[256,1024]{1,0:T(8,128)(2,1)S(1)}, bf16[256,1024]{1,0:T(8,128)(2,1)}, u32[]{:S(2)}) copy-start(bf16[256,1024]{1,0:T(8,128)(2,1)} %param.8) | copy-start | bytes 1572868
  0.6 5.0 %collective-permute-start = (bf16[1,8,1024]{2,1,0:T(8,128)(2,1)}, bf16[1,8,1024]{2,1,0:T(8,128)(2,1)S(1)}, u32[]{:S(2)}, u32[]{:S(2)}) collective-permute-start(bf16[1,8,1024]{2,1,0:T(8,128)(2,1)} %bitcast.22), channel_id=1, source_target_pairs={{0,8},{8,0},{16,24},{24,16},{1,9},{9,1},{17,25},{25,17},{2,10},{10... | collective-permute-start | bytes 49160 | tf_op jit(solution)/shard_map/ppermute | solution.py:188
  3.8 32.1 %collective-permute-start.6 = (bf16[64,4096]{1,0:T(8,128)(2,1)}, bf16[64,4096]{1,0:T(8,128)(2,1)S(1)}, u32[]{:S(2)}, u32[]{:S(2)}) collective-permute-start(bf16[64,4096]{1,0:T(8,128)(2,1)} %rows_far.1), channel_id=1, source_target_pairs={{8,16},{16,8},{9,17},{17,9},{10,18},{18,10},{11,19},{19,11},{12,20... | collective-permute-start | bytes 1572872 | tf_op jit(solution)/shard_map/ppermute | solution.py:210
  6.4 15.1 %collective-permute-start.1 = (bf16[2,8,1024]{2,1,0:T(8,128)(2,1)S(1)}, bf16[2,8,1024]{2,1,0:T(8,128)(2,1)S(1)}, u32[]{:S(2)}, u32[]{:S(2)}) collective-permute-start(bf16[2,8,1024]{2,1,0:T(8,128)(2,1)S(1)} %pad_maximum_fusion.4), channel_id=1, source_target_pairs={{0,16},{8,24},{16,0},{24,8},{1,17},{9,25},{17,1},{25,9},{2,18},{10... | collective-permute-start | bytes 98312 | tf_op jit(solution)/shard_map/ppermute | solution.py:188
  22.2 1.3 %collective-permute-start.2 = (bf16[4,8,1024]{2,1,0:T(8,128)(2,1)S(1)}, bf16[4,8,1024]{2,1,0:T(8,128)(2,1)S(1)}, u32[]{:S(2)}, u32[]{:S(2)}) collective-permute-start(bf16[4,8,1024]{2,1,0:T(8,128)(2,1)S(1)} %get-tuple-element.27), channel_id=1, source_target_pairs={{0,1},{1,0},{2,3},{3,2},{4,5},{5,4},{6,7},{7,6},{8,9},{9,8},{10,11... | collective-permute-start | bytes 196616 | tf_op jit(solution)/shard_map/ppermute | solution.py:192
  24.2 18.6 %collective-permute-start.3 = (bf16[2,4,8,1024]{3,2,1,0:T(8,128)(2,1)}, bf16[2,4,8,1024]{3,2,1,0:T(8,128)(2,1)}, u32[]{:S(2)}, u32[]{:S(2)}) collective-permute-start(bf16[2,4,8,1024]{3,2,1,0:T(8,128)(2,1)} %get-tuple-element.25), channel_id=1, source_target_pairs={{0,2},{2,0},{4,6},{6,4},{1,3},{3,1},{5,7},{7,5},{8,10},{10,8},{12,... | collective-permute-start | bytes 393224 | tf_op jit(solution)/shard_map/ppermute | solution.py:193
  27.8 2.8 %copy-start.1 = (bf16[3,256,4096]{2,1,0:T(8,128)(2,1)S(1)}, bf16[3,256,4096]{2,1,0:T(8,128)(2,1)}, u32[]{:S(2)}) copy-start(bf16[3,256,4096]{2,1,0:T(8,128)(2,1)} %members.7) | copy-start | bytes 18874372
  30.6 15.7 %collective-permute-start.9 = (bf16[48,4096]{1,0:T(8,128)(2,1)S(1)}, bf16[48,4096]{1,0:T(8,128)(2,1)S(1)}, u32[]{:S(2)}, u32[]{:S(2)}) collective-permute-start(bf16[48,4096]{1,0:T(8,128)(2,1)S(1)} %shard_map.88), channel_id=1, source_target_pairs={{0,24},{24,0},{1,25},{25,1},{2,26},{26,2},{3,27},{27,3},{4,28},{28... | collective-permute-start | bytes 1179656 | tf_op jit(solution)/shard_map/ppermute | solution.py:242
  35.1 18.6 %collective-permute-start.8 = (bf16[48,4096]{1,0:T(8,128)(2,1)}, bf16[48,4096]{1,0:T(8,128)(2,1)S(1)}, u32[]{:S(2)}, u32[]{:S(2)}) collective-permute-start(bf16[48,4096]{1,0:T(8,128)(2,1)} %get-tuple-element.17), channel_id=1, source_target_pairs={{0,8},{8,0},{16,24},{24,16},{1,9},{9,1},{17,25},{25,17},{2,10},{10... | collective-permute-start | bytes 1179656 | tf_op jit(solution)/shard_map/ppermute | solution.py:188
  35.2 0.7 collective-permute-start.5
  35.9 26.1 %collective-permute-start.7 = (bf16[48,4096]{1,0:T(8,128)(2,1)S(1)}, bf16[48,4096]{1,0:T(8,128)(2,1)S(1)}, u32[]{:S(2)}, u32[]{:S(2)}) collective-permute-start(bf16[48,4096]{1,0:T(8,128)(2,1)S(1)} %get-tuple-element.15), channel_id=1, source_target_pairs={{0,16},{8,0},{16,24},{24,8},{1,17},{9,1},{17,25},{25,9},{2,18},{10... | collective-permute-start | bytes 1179656 | tf_op jit(solution)/shard_map/ppermute | solution.py:250
  44.6 18.6 %collective-permute-start.4 = (bf16[2,2,4,8,1024]{4,3,2,1,0:T(8,128)(2,1)}, bf16[2,2,4,8,1024]{4,3,2,1,0:T(8,128)(2,1)}, u32[]{:S(2)}, u32[]{:S(2)}) collective-permute-start(bf16[2,2,4,8,1024]{4,3,2,1,0:T(8,128)(2,1)} %get-tuple-element.23), channel_id=1, source_target_pairs={{0,4},{2,6},{4,0},{6,2},{1,5},{3,7},{5,1},{7,3},{8,12},{10,14},{12... | collective-permute-start | bytes 786440 | tf_op jit(solution)/shard_map/ppermute | solution.py:193
  53.7 2.8 %copy-start.2 = (bf16[3,256,4096]{2,1,0:T(8,128)(2,1)S(1)}, bf16[3,256,4096]{2,1,0:T(8,128)(2,1)}, u32[]{:S(2)}) copy-start(bf16[3,256,4096]{2,1,0:T(8,128)(2,1)} %members.7) | copy-start | bytes 18874372
  56.5 5.5 %copy-start.3 = (bf16[3,256,4096]{2,1,0:T(8,128)(2,1)S(1)}, bf16[3,256,4096]{2,1,0:T(8,128)(2,1)}, u32[]{:S(2)}) copy-start(bf16[3,256,4096]{2,1,0:T(8,128)(2,1)} %members.7) | copy-start | bytes 18874372
  56.5 6.8 %copy-start.4 = (bf16[1,2,2,4,8,1024]{5,4,3,2,1,0:T(8,128)(2,1)S(1)}, bf16[1,2,2,4,8,1024]{5,4,3,2,1,0:T(8,128)(2,1)}, u32[]{:S(2)}) copy-start(bf16[1,2,2,4,8,1024]{5,4,3,2,1,0:T(8,128)(2,1)} %get-tuple-element.22) | copy-start | bytes 786436
  63.2 2.3 %collective-permute-start.10 = (f32[4,4,16,128]{3,2,1,0:T(8,128)S(1)}, f32[4,4,16,128]{3,2,1,0:T(8,128)S(1)}, u32[]{:S(2)}, u32[]{:S(2)}) collective-permute-start(f32[4,4,16,128]{3,2,1,0:T(8,128)S(1)} %shard_map.91), channel_id=1, source_target_pairs={{0,1},{1,0},{2,3},{3,2},{4,5},{5,4},{6,7},{7,6},{8,9},{9,8},{10,11... | collective-permute-start | bytes 393224 | tf_op jit(solution)/shard_map/ppermute | solution.py:192
  66.1 12.5 %all-to-all-start = ((f32[16,16,128]{2,1,0:T(8,128)}), f32[16,16,128]{2,1,0:T(8,128)S(1)}, u32[]{:S(2)}, u32[]{:S(2)}) async-start(f32[16,16,128]{2,1,0:T(8,128)} %bitcast.12), calls=%async_computation | async-start | bytes 262144 | tf_op jit(solution)/shard_map/all_to_all | solution.py:288

commit v5 on v4

--- a/solution.py
+++ b/solution.py
@@ -32,8 +32,8 @@
 
 
 def head_kernel(
-    keys, me, slots_far, sizes_far, routes_far, rows_far,
-    places, lives, *refs,
+    keys, slot_count, me, slots_far, sizes_far, routes_far, rows_far,
+    places, lives, lines, slots_in, *refs,
 ):
     outs, (slots, sizes, routes, rows, sems) = refs[: len(keys)], refs[len(keys) :]
     pairs = ((slots_far, slots), (sizes_far, sizes), (routes_far, routes), (rows_far, rows))
@@ -47,11 +47,13 @@
     cluster = iota((total, width), 0)
     slot_of = jnp.zeros((total, width), jnp.int32)
     size_of = jnp.zeros((total, width), jnp.int32)
+    group_of = jnp.zeros((total, width), jnp.int32)
     for copy in copies[:3]:
         copy.wait()
     for c in range(total):
         slot_of = jnp.where(cluster == c, slots[c], slot_of)
         size_of = jnp.where(cluster == c, sizes[c], size_of)
+        group_of = jnp.where(cluster == c, slots[c] // slot_count, group_of)
     seen = jnp.zeros((total, 1), jnp.float32)
     for r in range(2):
         hit = routes[r : r + 1] == cluster
@@ -62,7 +64,10 @@
         rank = jnp.sum(jnp.where(hit, earlier + seen, 0.0), axis=0, keepdims=True)
         seen = seen + jnp.sum(one, axis=1, keepdims=True)
         slot = jnp.sum(jnp.where(hit, slot_of, 0), axis=0, keepdims=True)
+        group = jnp.sum(jnp.where(hit, group_of, 0), axis=0, keepdims=True)
         places[r : r + 1] = slot * MOST + rank.astype(jnp.int32)
+        lines[r : r + 1] = group * MOST + rank.astype(jnp.int32)
+        slots_in[r : r + 1] = slot - group * slot_count
         lives[r : r + 1] = jnp.sum(jnp.where(hit, size_of, 0), axis=0, keepdims=True)
     where = places[...]
     copies[3].wait()
@@ -122,6 +127,22 @@
 
 def gate_kernel(members, rows, out):
     out[0:16, 0:128] = rows[0:16, 0:128]
+
+
+def coarse_kernel(scale, me, mine, reps, *refs):
+    parts, out = refs[:-1], refs[-1]
+    cores, groups, each, width = parts[0].shape
+    mems = cores * len(parts)
+    lines = cores * groups
+    batch = max(1, 256 // (lines * each))
+    for first in range(0, len(parts), batch):
+        rows = [part[...].reshape(lines * each, width) for part in parts[first : first + batch]]
+        rows = jnp.concatenate(rows, axis=0) if len(rows) > 1 else rows[0]
+        score = lax.dot_general(rows, reps[...], NT, preferred_element_type=jnp.float32)
+        score = (score * scale).astype(out.dtype)
+        for at in range(score.shape[0] // each):
+            member = mine[0] ^ (first * cores + at // groups)
+            out[(me[0] ^ (at % groups)) * mems + member] = score[at * each : (at + 1) * each]
 
 
 def half_kernel(key, other, me, core, members, rows, _, out, acc):
@@ -140,25 +161,30 @@
             )
 
 
-def final_kernel(slot_count, scale, mine, places, lives, parts, out):
+def final_kernel(slot_count, scale, mine, lines, slots, lives, parts, out):
     groups, chips = parts.shape[:2]
     block, rows = out.shape[1], out.shape[2]
     member = iota((block, rows), 0) + mine[0] * block
-    tables = []
-    for group in range(groups):
-        total = parts[group, 0]
-        for chip in range(1, chips):
-            total = total + parts[group, chip]
+    total = parts[:, 0]
+    for chip in range(1, chips):
+        total = total + parts[:, chip]
+    total = total.reshape(groups * MOST, total.shape[2])
+    line = jnp.concatenate([lines[r : r + 1] for r in range(2)], axis=1)
+    one = (line == iota((groups * MOST, 2 * rows), 0)).astype(jnp.float32).astype(jnp.bfloat16)
+    score = jnp.zeros((total.shape[1], 2 * rows), jnp.float32)
+    for _ in range(3):
+        piece = total.astype(jnp.bfloat16)
+        total = total - piece.astype(jnp.float32)
+        score = score + lax.dot_general(
+            piece, one, (((0,), (0,)), ((), ())), preferred_element_type=jnp.float32
+        )
+    for r in range(2):
+        slot = slots[r : r + 1]
+        found = jnp.zeros((block, rows), jnp.float32)
         for s in range(slot_count):
-            tables.append(total[:, s * block : (s + 1) * block])
-    table = jnp.concatenate(tables, axis=0)
-    for r in range(2):
-        one = (places[r : r + 1] == iota((table.shape[0], rows), 0)).astype(jnp.float32)
-        score = lax.dot_general(
-            table, one, (((0,), (0,)), ((), ())),
-            precision=lax.Precision.HIGHEST, preferred_element_type=jnp.float32,
-        )
-        out[r] = jnp.where(member < lives[r : r + 1], score * scale, 0.0)
+            part = score[s * block : (s + 1) * block, r * rows : (r + 1) * rows]
+            found = jnp.where(slot == s, part, found)
+        out[r] = jnp.where(member < lives[r : r + 1], found * scale, 0.0)
 
 
 def call(kernel, shapes, specs, scratch=(), flops=0, mib=4, alias=()):
@@ -213,9 +239,9 @@
         far = list(range(half, last))
         keys = near + [last] + far + [0]
         total = owner_slot.shape[0]
-        places, lives, *picked = call(
-            functools.partial(head_kernel, keys),
-            [((2, rows_here), i32)] * 2 + [rows_out] * len(keys),
+        places, lives, lines, slots_in, *picked = call(
+            functools.partial(head_kernel, keys, slot_count),
+            [((2, rows_here), i32)] * 4 + [rows_out] * len(keys),
             [SM] + [FAR] * 4,
             scratch=[
                 pltpu.SMEM((total,), i32), pltpu.SMEM((total,), i32),
@@ -249,16 +275,23 @@
             way = [(i, i ^ last ^ k if i in middle else i ^ k) for i in range(groups)]
             got[k] = lax.ppermute(onward[at], "grp", way)
 
-        step = 1
-        while step < mems:
-            sketches = jnp.stack([sketches, swap_mem(sketches, step)])
-            step *= 2
-        sketches = sketches.reshape(-1, bin_sketch.shape[1])
+        sketches = jnp.stack([sketches, swap_mem(sketches, 1)]).reshape(2, groups, *bin_sketch.shape)
+        parts = [sketches]
+        for q in range(1, chips):
+            parts.append(swap_mem(sketches, 2 * q))
+        each = bin_sketch.shape[0]
+        (coarse,) = call(
+            functools.partial(coarse_kernel, bin_sketch.shape[1] ** (-0.5)),
+            [((groups * mems, each, rep_sketch.shape[0]), bf)],
+            [SM] * 2 + [VM] * (1 + chips), mib=40 if groups * mems > 256 else 4,
+            flops=2 * groups * mems * each * rep_sketch.size,
+        )(me1, mine1, rep_sketch, *parts)
+        coarse_scores = coarse.reshape(-1, rep_sketch.shape[0])
 
         shape = ((groups, chips, MOST, 128), f32)
         held = ()
         got[last] = through
-        for keys in ([0] + near + [last],):
+        for keys in ([0], near + [last]):
             rows = [got[k] for k in keys] + ([direct] if last in keys else [])
             held = call(
                 functools.partial(score_kernel, keys, last), [shape] * 2,
@@ -288,19 +321,10 @@
         parts = lax.all_to_all(parts, ("grp", "chip"), 0, 0, tiled=True)
         parts = parts.reshape(groups, chips, MOST, 128)
 
-        product = lax.dot_general(sketches, rep_sketch, NT, preferred_element_type=f32)
-        product = (product * bin_sketch.shape[1] ** (-0.5)).astype(bf)
-        each = bin_sketch.shape[0]
-        row = iota((product.shape[0], 1), 0) // each
-        source = (row % mems ^ mine) * groups + (row // mems ^ me)
-        within = iota((product.shape[0], 1), 0) % each
-        perm = source * each + within == iota((1, product.shape[0]), 1)
-        coarse_scores = pick(perm, product)
-
         (fine,) = call(
             functools.partial(final_kernel, slot_count, FW ** (-0.5)),
-            [((2, block, rows_here), f32)], [SM] + [VM] * 3,
-        )(mine1, places, lives, parts)
+            [((2, block, rows_here), f32)], [SM] + [VM] * 4,
+        )(mine1, lines, slots_in, lives, parts)
         return (coarse_scores, fine.transpose(2, 0, 1))
 
     return local

time: 80.1 us -> 64.9 us (0.81)
  waiting for transfers between devices: 32.4 us -> 13 us
  starting transfers between devices: 26.6 us -> 34.7 us
  other arithmetic: 5.55 us -> 0.7 us
  Pallas kernels: 7.47 us -> 9.78 us
  matrix products: 1.23 us -> 0 us
    ppermute x3, waiting for transfers between devices: 20.7 us -> 6.07 us  [swap(): return lax.ppermute(value, 'grp', [(i, i ^ key) for i in range(groups)])]
    ppermute x1, starting transfers between devices: 6.94 us -> 15.8 us  [local(): got[k] = lax.ppermute(onward[at], 'grp', way)]
    ppermute x2 -> x3, waiting for transfers between devices: 0.01 us -> 6.88 us  [swap_mem(): lax.ppermute(value, 'chip', [(i, i ^ key // 2) for i in range(chips)])]
    all_to_all x1, waiting for transfers between devices: 6.85 us -> 0.01 us  [local(): parts = lax.all_to_all(parts, ('grp', 'chip'), 0, 0, tiled=True)]
    ppermute x3, starting transfers between devices: 6.22 us -> 0.63 us  [swap(): return lax.ppermute(value, 'grp', [(i, i ^ key) for i in range(groups)])]
    another operation x4 -> x2, other arithmetic: 4.15 us -> 0.03 us  [local(): jnp.stack([sketches, swap_mem(sketches, 1)])]
    ppermute x1, waiting for transfers between devices: 3.5 us -> 0.01 us  [local(): got[k] = lax.ppermute(onward[at], 'grp', way)]
    ppermute x1, starting transfers between devices: 4.53 us -> 6.97 us  [local(): direct = lax.ppermute(rows, 'grp', outer)]
  transfers between devices with their start and end apart: 12 -> 13, of which waited for: 7 -> 4; matrix products, arithmetic and copies ran while one was open for 8% -> 1% of each run, Pallas kernels for 8% -> 14%
where the time goes in v5:
time: 64.9 us; the launch traced here: 64.6 us
  starting transfers between devices  34.7 us (53%)
  waiting for transfers between devices  13 us (20%)
  Pallas kernels  9.78 us (15%)
  local copies, waits for them, and re-layouts  5.58 us (9%)
  between operations  0.83 us (1%)
  other arithmetic  0.7 us (1%)
    ppermute x1, starting transfers between devices, local(): got[k] = lax.ppermute(onward[at], 'grp', way)  15.8 us
    ppermute x1, starting transfers between devices, local(): direct = lax.ppermute(rows, 'grp', outer)  6.97 us
    ppermute x3, waiting for transfers between devices, swap_mem(): lax.ppermute(value, 'chip', [(i, i ^ key // 2) for i in range(chips)])  6.88 us
    all_to_all x1, starting transfers between devices, local(): parts = lax.all_to_all(parts, ('grp', 'chip'), 0, 0, tiled=True)  6.26 us
    ppermute x3, waiting for transfers between devices, swap(): return lax.ppermute(value, 'grp', [(i, i ^ key) for i in range(groups)])  6.07 us
    unnamed x10, local copies, waits for them, and re-layouts  5.58 us
    pallas_call x2, Pallas kernels, local(): call(functools.partial(score_kernel, keys, last), [shape] * 2, [SM] * 2 +...  3.93 us
    ppermute x3, starting transfers between devices, swap_mem(): lax.ppermute(value, 'chip', [(i, i ^ key // 2) for i in range(chips)])  3.55 us
  transfers between devices with their start and end apart: 13, of which 4 were waited for; matrix products, arithmetic and copies ran while one was open for 1% of the time, Pallas kernels for 14%

profile of v5, /device:TPU:0, one launch (start us, length us, event | category | flops | bytes accessed | tf_op | source)
XLA Modules:
  0.0 64.6 jit_solution(2520524792886923295)
XLA Ops:
  0.6 0.7 %collective-permute-start.7 = (bf16[64,4096]{1,0:T(8,128)(2,1)}, bf16[64,4096]{1,0:T(8,128)(2,1)S(1)}, u32[]{:S(2)}, u32[]{:S(2)}) collective-permute-start(bf16[64,4096]{1,0:T(8,128)(2,1)} %rows_far.1), channel_id=1, source_target_pairs={{8,16},{16,8},{9,17},{17,9},{10,18},{18,10},{11,19},{19,11},{12,20... | collective-permute-start | bytes 1572872 | tf_op jit(solution)/shard_map/ppermute | solution.py:236
  1.3 1.6 %shard_map.87 = (s32[2,64]{1,0:T(2,128)S(1)}, s32[2,64]{1,0:T(2,128)S(1)}, s32[2,64]{1,0:T(2,128)S(1)}, s32[2,64]{1,0:T(2,128)S(1)}, bf16[48,4096]{1,0:T(8,128)(...) custom-call(s32[1]{0:T(128)} %bitcast.me, s32[12]{0:T(128)} %slots_far.1, ...), custom_call_target="tpu_custom_call" | custom-call | bytes 262144 | tf_op jit(solution)/shard_map/pallas_call | solution.py:242
  3.0 2.8 %copy-done = bf16[3,256,4096]{2,1,0:T(8,128)(2,1)S(1)} copy-done((bf16[3,256,4096]{2,1,0:T(8,128)(2,1)S(1)}, bf16[3,256,4096]{2,1,0:T(8,128)(2,1)}, u32[]{:S(2)}) %copy-start) | copy-done | bytes 6291480
  5.8 7.0 %collective-permute-start.10 = (bf16[48,4096]{1,0:T(8,128)(2,1)S(1)}, bf16[48,4096]{1,0:T(8,128)(2,1)S(1)}, u32[]{:S(2)}, u32[]{:S(2)}) collective-permute-start(bf16[48,4096]{1,0:T(8,128)(2,1)S(1)} %shard_map.89), channel_id=1, source_target_pairs={{0,24},{24,0},{1,25},{25,1},{2,26},{26,2},{3,27},{27,3},{4,28},{28... | collective-permute-start | bytes 1179656 | tf_op jit(solution)/shard_map/ppermute | solution.py:268
  12.8 0.1 collective-permute-start.9
  12.9 0.7 %collective-permute-start.6 = (s32[2,64]{1,0:T(2,128)S(1)}, s32[2,64]{1,0:T(2,128)S(1)}, u32[]{:S(2)}, u32[]{:S(2)}) collective-permute-start(s32[2,64]{1,0:T(2,128)S(1)} %get-tuple-element.19), channel_id=1, source_target_pairs={{8,16},{16,8},{9,17},{17,9},{10,18},{18,10},{11,19},{19,11},{12,20... | collective-permute-start | bytes 1544 | tf_op jit(solution)/shard_map/ppermute | solution.py:253
  13.6 15.8 %collective-permute-start.8 = (bf16[48,4096]{1,0:T(8,128)(2,1)S(1)}, bf16[48,4096]{1,0:T(8,128)(2,1)S(1)}, u32[]{:S(2)}, u32[]{:S(2)}) collective-permute-start(bf16[48,4096]{1,0:T(8,128)(2,1)S(1)} %get-tuple-element.21), channel_id=1, source_target_pairs={{0,16},{8,0},{16,24},{24,8},{1,17},{9,1},{17,25},{25,9},{2,18},{10... | collective-permute-start | bytes 1179656 | tf_op jit(solution)/shard_map/ppermute | solution.py:276
  29.4 2.8 %copy-done.1 = bf16[3,256,4096]{2,1,0:T(8,128)(2,1)S(1)} copy-done((bf16[3,256,4096]{2,1,0:T(8,128)(2,1)S(1)}, bf16[3,256,4096]{2,1,0:T(8,128)(2,1)}, u32[]{:S(2)}) %copy-start.1) | copy-done | bytes 6291480
  32.2 1.9 %shard_map.90 = (f32[4,4,16,128]{3,2,1,0:T(8,128)S(1)}, f32[4,4,16,128]{3,2,1,0:T(8,128)S(1)}) custom-call(s32[1]{0:T(128)} %bitcast.me, s32[1]{0:T(128)} %bitcast.7.core, bf16[3,256,4096]{2,1,0:T(8,128)(2,1)S(1)} %copy-done.1, bf16[48,4096]{1,0:T(8,128)(2,1)S(1)} %get-tuple-element.25.refs_0_), custom_call_target="tpu_custom_call" | custom-call | flops 805306368 | bytes 262144 | tf_op jit(solution)/shard_map/pallas_call | solution.py:296
  34.1 5.1 %collective-permute-done = bf16[1,8,1024]{2,1,0:T(8,128)(2,1)S(1)} collective-permute-done((bf16[1,8,1024]{2,1,0:T(8,128)(2,1)S(1)}, bf16[1,8,1024]{2,1,0:T(8,128)(2,1)S(1)}, u32[]{:S(2)}, u32[]{:S(2)}) %collective-permute-start) | collective-permute-done | bytes 16416 | tf_op jit(solution)/shard_map/ppermute | solution.py:214
  39.2 0.6 collective-permute-start.1
  39.7 2.0 %shard_map.91 = (f32[4,4,16,128]{3,2,1,0:T(8,128)S(1)}, f32[4,4,16,128]{3,2,1,0:T(8,128)S(1)}) custom-call(s32[1]{0:T(128)} %bitcast.me, s32[1]{0:T(128)} %bitcast.7.core, bf16[3,256,4096]{2,1,0:T(8,128)(2,1)S(1)} %copy-done.2, bf16[48,4096]{1,0:T(8,128)(2,1)S(1)} %collective-permute-done.9.refs_0_, ...), custom_call_target="tpu_custom_call", output_to_operand_aliasing={{0}: (6, {}), {1}: (7, {})} | custom-call | flops 805306368 | bytes 262144 | tf_op jit(solution)/shard_map/pallas_call | solution.py:296
  41.8 1.1 %shard_map.93 = f32[4,4,16,128]{3,2,1,0:T(8,128)S(1)} custom-call(s32[1]{0:T(128)} %bitcast.me, s32[1]{0:T(128)} %bitcast.7.core, bf16[3,256,4096]{2,1,0:T(8,128)(2,1)S(1)} %copy-done.2, bf16[48,4096]{1,0:T(8,128)(2,1)S(1)} %collective-permute-done.8.rows, f32[4,4,16,128]{3,2,1,0:T(8,128)S(1)} %get-tuple-element.29._), custom_call_target="tpu_custom_call", output_to_operand_aliasing={{}: (4, {})} | custom-call | flops 402653184 | bytes 262144 | tf_op jit(solution)/shard_map/pallas_call | solution.py:307
  43.0 1.0 %collective-permute-done.1 = bf16[2,8,1024]{2,1,0:T(8,128)(2,1)S(1)} collective-permute-done((bf16[2,8,1024]{2,1,0:T(8,128)(2,1)S(1)}, bf16[2,8,1024]{2,1,0:T(8,128)(2,1)S(1)}, u32[]{:S(2)}, u32[]{:S(2)}) %collective-permute-start.1) | collective-permute-done | bytes 32800 | tf_op jit(solution)/shard_map/ppermute | solution.py:214
  44.1 1.1 %shard_map.92 = f32[4,4,16,128]{3,2,1,0:T(8,128)S(1)} custom-call(s32[1]{0:T(128)} %bitcast.me, s32[1]{0:T(128)} %bitcast.7.core, bf16[3,256,4096]{2,1,0:T(8,128)(2,1)S(1)} %copy-done.2, bf16[48,4096]{1,0:T(8,128)(2,1)S(1)} %collective-permute-done.8.rows, f32[4,4,16,128]{3,2,1,0:T(8,128)S(1)} %get-tuple-element.28._), custom_call_target="tpu_custom_call", output_to_operand_aliasing={{}: (4, {})} | custom-call | flops 402653184 | bytes 262144 | tf_op jit(solution)/shard_map/pallas_call | solution.py:307
  45.3 0.7 %add.7 = f32[4,4,16,128]{3,2,1,0:T(8,128)} add(f32[4,4,16,128]{3,2,1,0:T(8,128)S(1)} %shard_map.92, f32[4,4,16,128]{3,2,1,0:T(8,128)S(1)} %collective-permute-done.11) | non-fusion elementwise | flops 32768 | bytes 393216 | tf_op jit(solution)/shard_map/add | solution.py:319
  45.9 6.3 %all-to-all-start = ((f32[16,16,128]{2,1,0:T(8,128)}), f32[16,16,128]{2,1,0:T(8,128)S(1)}, u32[]{:S(2)}, u32[]{:S(2)}) async-start(f32[16,16,128]{2,1,0:T(8,128)} %bitcast.8), calls=%async_computation | async-start | bytes 262144 | tf_op jit(solution)/shard_map/all_to_all | solution.py:321
  52.2 2.0 %collective-permute-start.3 = (bf16[2,4,8,1024]{3,2,1,0:T(8,128)(2,1)S(1)}, bf16[2,4,8,1024]{3,2,1,0:T(8,128)(2,1)S(1)}, u32[]{:S(2)}, u32[]{:S(2)}) collective-permute-start(bf16[2,4,8,1024]{3,2,1,0:T(8,128)(2,1)S(1)} %pad_maximum_fusion.refs_0_), channel_id=1, source_target_pairs={{0,2},{2,0},{4,6},{6,4},{1,3},{3,1},{5,7},{7,5},{8,10},{10,8},{12,... | collective-permute-start | bytes 393224 | tf_op jit(solution)/shard_map/ppermute | solution.py:219
  54.2 1.5 %collective-permute-start.4 = (bf16[2,4,8,1024]{3,2,1,0:T(8,128)(2,1)S(1)}, bf16[2,4,8,1024]{3,2,1,0:T(8,128)(2,1)S(1)}, u32[]{:S(2)}, u32[]{:S(2)}) collective-permute-start(bf16[2,4,8,1024]{3,2,1,0:T(8,128)(2,1)S(1)} %pad_maximum_fusion.refs_0_), channel_id=1, source_target_pairs={{0,4},{2,6},{4,0},{6,2},{1,5},{3,7},{5,1},{7,3},{8,12},{10,14},{12... | collective-permute-start | bytes 393224 | tf_op jit(solution)/shard_map/ppermute | solution.py:219
  55.7 0.1 collective-permute-start.5
  55.8 4.1 %collective-permute-done.3.refs_1_ = bf16[2,4,8,1024]{3,2,1,0:T(8,128)(2,1)S(1)} collective-permute-done((bf16[2,4,8,1024]{3,2,1,0:T(8,128)(2,1)S(1)}, bf16[2,4,8,1024]{3,2,1,0:T(8,128)(2,1)S(1)}, u32[]{:S(2)}, u32[]{:S(2)}) %collective-permute-start.3) | collective-permute-done | bytes 131104 | tf_op jit(solution)/shard_map/ppermute | solution.py:219
  59.9 2.8 %collective-permute-done.4.refs_2_ = bf16[2,4,8,1024]{3,2,1,0:T(8,128)(2,1)S(1)} collective-permute-done((bf16[2,4,8,1024]{3,2,1,0:T(8,128)(2,1)S(1)}, bf16[2,4,8,1024]{3,2,1,0:T(8,128)(2,1)S(1)}, u32[]{:S(2)}, u32[]{:S(2)}) %collective-permute-start.4) | collective-permute-done | bytes 131104 | tf_op jit(solution)/shard_map/ppermute | solution.py:219
  62.7 1.0 %shard_map.86 = bf16[32,8,256]{2,1,0:T(8,128)(2,1)} custom-call(s32[1]{0:T(128)} %bitcast.me, s32[1]{0:T(128)} %bitcast.1.mine, bf16[256,1024]{1,0:T(8,128)(2,1)S(1)} %copy-done.3, bf16[2,4,8,1024]{3,2,1,0:T(8,128)(2,1)S(1)} %pad_maximum_fusion.refs_0_, bf16[2,4,8,1024]{3,2,1,0:T(8,128)(2,1)S(1)} %collective-permute-done.3.refs_1_, ...), custom_call_target="tpu_custom_call" | custom-call | flops 134217728 | bytes 262144 | tf_op jit(solution)/shard_map/pallas_call | solution.py:283
  63.7 0.9 %shard_map.94 = f32[2,32,64]{2,1,0:T(8,128)} custom-call(s32[1]{0:T(128)} %bitcast.1.mine, s32[2,64]{1,0:T(2,128)S(1)} %get-tuple-element.16.lines, s32[2,64]{1,0:T(2,128)S(1)} %get-tuple-element.17.slots, s32[2,64]{1,0:T(2,128)S(1)} %get-tuple-element.18.lives, f32[4,4,16,128]{3,2,1,0:T(8,128)S(1)} %bitcast.12), custom_call_target="tpu_custom_call" | custom-call | bytes 262144 | tf_op jit(solution)/shard_map/pallas_call | solution.py:324
  (25 shorter events, 0.2 us)
Async XLA Ops:
  0.6 28.7 %copy-start.4 = (bf16[8,1024]{1,0:T(8,128)(2,1)S(1)}, bf16[8,1024]{1,0:T(8,128)(2,1)}, u32[]{:S(2)}) copy-start(bf16[8,1024]{1,0:T(8,128)(2,1)} %param.7) | copy-start | bytes 49156
  0.6 12.9 %collective-permute-start.7 = (bf16[64,4096]{1,0:T(8,128)(2,1)}, bf16[64,4096]{1,0:T(8,128)(2,1)S(1)}, u32[]{:S(2)}, u32[]{:S(2)}) collective-permute-start(bf16[64,4096]{1,0:T(8,128)(2,1)} %rows_far.1), channel_id=1, source_target_pairs={{8,16},{16,8},{9,17},{17,9},{10,18},{18,10},{11,19},{19,11},{12,20... | collective-permute-start | bytes 1572872 | tf_op jit(solution)/shard_map/ppermute | solution.py:236
  3.0 2.8 %copy-start = (bf16[3,256,4096]{2,1,0:T(8,128)(2,1)S(1)}, bf16[3,256,4096]{2,1,0:T(8,128)(2,1)}, u32[]{:S(2)}) copy-start(bf16[3,256,4096]{2,1,0:T(8,128)(2,1)} %members.9) | copy-start | bytes 18874372
  5.8 33.9 %collective-permute-start.10 = (bf16[48,4096]{1,0:T(8,128)(2,1)S(1)}, bf16[48,4096]{1,0:T(8,128)(2,1)S(1)}, u32[]{:S(2)}, u32[]{:S(2)}) collective-permute-start(bf16[48,4096]{1,0:T(8,128)(2,1)S(1)} %shard_map.89), channel_id=1, source_target_pairs={{0,24},{24,0},{1,25},{25,1},{2,26},{26,2},{3,27},{27,3},{4,28},{28... | collective-permute-start | bytes 1179656 | tf_op jit(solution)/shard_map/ppermute | solution.py:268
  12.8 27.0 %collective-permute-start.9 = (bf16[48,4096]{1,0:T(8,128)(2,1)S(1)}, bf16[48,4096]{1,0:T(8,128)(2,1)S(1)}, u32[]{:S(2)}, u32[]{:S(2)}) collective-permute-start(bf16[48,4096]{1,0:T(8,128)(2,1)S(1)} %get-tuple-element.22), channel_id=1, source_target_pairs={{0,8},{8,0},{16,24},{24,16},{1,9},{9,1},{17,25},{25,17},{2,10},{10... | collective-permute-start | bytes 1179656 | tf_op jit(solution)/shard_map/ppermute | solution.py:214
  12.9 0.7 %collective-permute-start.6 = (s32[2,64]{1,0:T(2,128)S(1)}, s32[2,64]{1,0:T(2,128)S(1)}, u32[]{:S(2)}, u32[]{:S(2)}) collective-permute-start(s32[2,64]{1,0:T(2,128)S(1)} %get-tuple-element.19), channel_id=1, source_target_pairs={{8,16},{16,8},{9,17},{17,9},{10,18},{18,10},{11,19},{19,11},{12,20... | collective-permute-start | bytes 1544 | tf_op jit(solution)/shard_map/ppermute | solution.py:253
  13.6 28.2 %collective-permute-start.8 = (bf16[48,4096]{1,0:T(8,128)(2,1)S(1)}, bf16[48,4096]{1,0:T(8,128)(2,1)S(1)}, u32[]{:S(2)}, u32[]{:S(2)}) collective-permute-start(bf16[48,4096]{1,0:T(8,128)(2,1)S(1)} %get-tuple-element.21), channel_id=1, source_target_pairs={{0,16},{8,0},{16,24},{24,8},{1,17},{9,1},{17,25},{25,9},{2,18},{10... | collective-permute-start | bytes 1179656 | tf_op jit(solution)/shard_map/ppermute | solution.py:276
  29.4 9.8 %collective-permute-start = (bf16[1,8,1024]{2,1,0:T(8,128)(2,1)S(1)}, bf16[1,8,1024]{2,1,0:T(8,128)(2,1)S(1)}, u32[]{:S(2)}, u32[]{:S(2)}) collective-permute-start(bf16[1,8,1024]{2,1,0:T(8,128)(2,1)S(1)} %bitcast.14), channel_id=1, source_target_pairs={{0,8},{8,0},{16,24},{24,16},{1,9},{9,1},{17,25},{25,17},{2,10},{10... | collective-permute-start | bytes 49160 | tf_op jit(solution)/shard_map/ppermute | solution.py:214
  29.4 2.8 %copy-start.1 = (bf16[3,256,4096]{2,1,0:T(8,128)(2,1)S(1)}, bf16[3,256,4096]{2,1,0:T(8,128)(2,1)}, u32[]{:S(2)}) copy-start(bf16[3,256,4096]{2,1,0:T(8,128)(2,1)} %members.9) | copy-start | bytes 18874372
  32.2 7.6 %copy-start.2 = (bf16[3,256,4096]{2,1,0:T(8,128)(2,1)S(1)}, bf16[3,256,4096]{2,1,0:T(8,128)(2,1)}, u32[]{:S(2)}) copy-start(bf16[3,256,4096]{2,1,0:T(8,128)(2,1)} %members.9) | copy-start | bytes 18874372
  39.2 4.8 %collective-permute-start.1 = (bf16[2,8,1024]{2,1,0:T(8,128)(2,1)S(1)}, bf16[2,8,1024]{2,1,0:T(8,128)(2,1)S(1)}, u32[]{:S(2)}, u32[]{:S(2)}) collective-permute-start(bf16[2,8,1024]{2,1,0:T(8,128)(2,1)S(1)} %pad_maximum_fusion.2), channel_id=1, source_target_pairs={{0,16},{8,24},{16,0},{24,8},{1,17},{9,25},{17,1},{25,9},{2,18},{10... | collective-permute-start | bytes 98312 | tf_op jit(solution)/shard_map/ppermute | solution.py:214
  41.8 20.9 %copy-start.3 = (bf16[256,1024]{1,0:T(8,128)(2,1)S(1)}, bf16[256,1024]{1,0:T(8,128)(2,1)}, u32[]{:S(2)}) copy-start(bf16[256,1024]{1,0:T(8,128)(2,1)} %reps.1) | copy-start | bytes 1572868
  42.9 2.3 %collective-permute-start.11 = (f32[4,4,16,128]{3,2,1,0:T(8,128)S(1)}, f32[4,4,16,128]{3,2,1,0:T(8,128)S(1)}, u32[]{:S(2)}, u32[]{:S(2)}) collective-permute-start(f32[4,4,16,128]{3,2,1,0:T(8,128)S(1)} %shard_map.93), channel_id=1, source_target_pairs={{0,1},{1,0},{2,3},{3,2},{4,5},{5,4},{6,7},{7,6},{8,9},{9,8},{10,11... | collective-permute-start | bytes 393224 | tf_op jit(solution)/shard_map/ppermute | solution.py:218
  44.0 8.2 %collective-permute-start.2 = (bf16[4,8,1024]{2,1,0:T(8,128)(2,1)S(1)}, bf16[4,8,1024]{2,1,0:T(8,128)(2,1)S(1)}, u32[]{:S(2)}, u32[]{:S(2)}) collective-permute-start(bf16[4,8,1024]{2,1,0:T(8,128)(2,1)S(1)} %get-tuple-element.31), channel_id=1, source_target_pairs={{0,1},{1,0},{2,3},{3,2},{4,5},{5,4},{6,7},{7,6},{8,9},{9,8},{10,11... | collective-permute-start | bytes 196616 | tf_op jit(solution)/shard_map/ppermute | solution.py:218
  45.9 17.7 %all-to-all-start = ((f32[16,16,128]{2,1,0:T(8,128)}), f32[16,16,128]{2,1,0:T(8,128)S(1)}, u32[]{:S(2)}, u32[]{:S(2)}) async-start(f32[16,16,128]{2,1,0:T(8,128)} %bitcast.8), calls=%async_computation | async-start | bytes 262144 | tf_op jit(solution)/shard_map/all_to_all | solution.py:321
  52.2 7.7 %collective-permute-start.3 = (bf16[2,4,8,1024]{3,2,1,0:T(8,128)(2,1)S(1)}, bf16[2,4,8,1024]{3,2,1,0:T(8,128)(2,1)S(1)}, u32[]{:S(2)}, u32[]{:S(2)}) collective-permute-start(bf16[2,4,8,1024]{3,2,1,0:T(8,128)(2,1)S(1)} %pad_maximum_fusion.refs_0_), channel_id=1, source_target_pairs={{0,2},{2,0},{4,6},{6,4},{1,3},{3,1},{5,7},{7,5},{8,10},{10,8},{12,... | collective-permute-start | bytes 393224 | tf_op jit(solution)/shard_map/ppermute | solution.py:219
  54.2 8.4 %collective-permute-start.4 = (bf16[2,4,8,1024]{3,2,1,0:T(8,128)(2,1)S(1)}, bf16[2,4,8,1024]{3,2,1,0:T(8,128)(2,1)S(1)}, u32[]{:S(2)}, u32[]{:S(2)}) collective-permute-start(bf16[2,4,8,1024]{3,2,1,0:T(8,128)(2,1)S(1)} %pad_maximum_fusion.refs_0_), channel_id=1, source_target_pairs={{0,4},{2,6},{4,0},{6,2},{1,5},{3,7},{5,1},{7,3},{8,12},{10,14},{12... | collective-permute-start | bytes 393224 | tf_op jit(solution)/shard_map/ppermute | solution.py:219
  55.7 7.0 %collective-permute-start.5 = (bf16[2,4,8,1024]{3,2,1,0:T(8,128)(2,1)S(1)}, bf16[2,4,8,1024]{3,2,1,0:T(8,128)(2,1)S(1)}, u32[]{:S(2)}, u32[]{:S(2)}) collective-permute-start(bf16[2,4,8,1024]{3,2,1,0:T(8,128)(2,1)S(1)} %pad_maximum_fusion.refs_0_), channel_id=1, source_target_pairs={{0,6},{2,4},{4,2},{6,0},{1,7},{3,5},{5,3},{7,1},{8,14},{10,12},{12... | collective-permute-start | bytes 393224 | tf_op jit(solution)/shard_map/ppermute | solution.py:219

commit v6 on v5

--- a/solution.py
+++ b/solution.py
@@ -125,10 +125,6 @@
     pl.when(core[0] == 1)(lambda: give(send, keep))
 
 
-def gate_kernel(members, rows, out):
-    out[0:16, 0:128] = rows[0:16, 0:128]
-
-
 def coarse_kernel(scale, me, mine, reps, *refs):
     parts, out = refs[:-1], refs[-1]
     cores, groups, each, width = parts[0].shape
@@ -262,10 +258,7 @@
         for k in near:
             got[k] = swap(picked[k], k)
         outer = [(i, i ^ last) for i in range(groups) if i not in middle]
-        (rows,) = call(
-            gate_kernel, [rows_out], [VM] * 2, mib=2, alias=[(1, 0)]
-        )(member_profile, picked[last])
-        direct = lax.ppermute(rows, "grp", outer)
+        direct = lax.ppermute(picked[last], "grp", outer)
         *onward, through = call(
             functools.partial(forward_kernel, far, last),
             [rows_out] * (len(far) + 1), [SM] + [VM] * (2 + len(far)),

time: 64.9 us -> 63.8 us (0.983)
  starting transfers between devices: 34.7 us -> 39.3 us
  waiting for transfers between devices: 13 us -> 10 us
  local copies, waits for them, and re-layouts: 5.58 us -> 2.8 us
    ppermute x3, waiting for transfers between devices: 6.07 us -> 3.1 us  [swap(): return lax.ppermute(value, 'grp', [(i, i ^ key) for i in range(groups)])]
    ppermute x1, starting transfers between devices: 15.8 us -> 18.6 us  [local(): got[k] = lax.ppermute(onward[at], 'grp', way)]
    unnamed x10 -> x8, local copies, waits for them, and re-layouts: 5.58 us -> 2.8 us
    ppermute x3, starting transfers between devices: 0.63 us -> 2.51 us  [swap(): return lax.ppermute(value, 'grp', [(i, i ^ key) for i in range(groups)])]
  transfers between devices with their start and end apart: 13 -> 13, of which waited for: 4 -> 3; matrix products, arithmetic and copies ran while one was open for 1% -> 1% of each run, Pallas kernels for 14% -> 14%
where the time goes in v6:
time: 63.8 us; the launch traced here: 63.5 us
  starting transfers between devices  39.3 us (62%)
  waiting for transfers between devices  10 us (16%)
  Pallas kernels  9.79 us (15%)
  local copies, waits for them, and re-layouts  2.8 us (4%)
  between operations  0.82 us (1%)
  other arithmetic  0.7 us (1%)
    ppermute x1, starting transfers between devices, local(): got[k] = lax.ppermute(onward[at], 'grp', way)  18.6 us
    ppermute x1, starting transfers between devices, local(): direct = lax.ppermute(picked[last], 'grp', outer)  6.99 us
    ppermute x3, waiting for transfers between devices, swap_mem(): lax.ppermute(value, 'chip', [(i, i ^ key // 2) for i in range(chips)])  6.89 us
    all_to_all x1, starting transfers between devices, local(): parts = lax.all_to_all(parts, ('grp', 'chip'), 0, 0, tiled=True)  5.73 us
    pallas_call x2, Pallas kernels, local(): call(functools.partial(score_kernel, keys, last), [shape] * 2, [SM] * 2 +...  3.93 us
    ppermute x3, starting transfers between devices, swap_mem(): lax.ppermute(value, 'chip', [(i, i ^ key // 2) for i in range(chips)])  3.55 us
    ppermute x3, waiting for transfers between devices, swap(): return lax.ppermute(value, 'grp', [(i, i ^ key) for i in range(groups)])  3.1 us
    unnamed x8, local copies, waits for them, and re-layouts  2.8 us
  transfers between devices with their start and end apart: 13, of which 3 were waited for; matrix products, arithmetic and copies ran while one was open for 1% of the time, Pallas kernels for 14%

profile of v6, /device:TPU:0, one launch (start us, length us, event | category | flops | bytes accessed | tf_op | source)
XLA Modules:
  0.0 63.5 jit_solution(15056167384941671632)
XLA Ops:
  0.6 0.7 %collective-permute-start.7 = (bf16[64,4096]{1,0:T(8,128)(2,1)}, bf16[64,4096]{1,0:T(8,128)(2,1)S(1)}, u32[]{:S(2)}, u32[]{:S(2)}) collective-permute-start(bf16[64,4096]{1,0:T(8,128)(2,1)} %rows_far.1), channel_id=1, source_target_pairs={{8,16},{16,8},{9,17},{17,9},{10,18},{18,10},{11,19},{19,11},{12,20... | collective-permute-start | bytes 1572872 | tf_op jit(solution)/shard_map/ppermute | solution.py:232
  1.4 1.6 %shard_map.87 = (s32[2,64]{1,0:T(2,128)S(1)}, s32[2,64]{1,0:T(2,128)S(1)}, s32[2,64]{1,0:T(2,128)S(1)}, s32[2,64]{1,0:T(2,128)S(1)}, bf16[48,4096]{1,0:T(8,128)(...) custom-call(s32[1]{0:T(128)} %bitcast.me, s32[12]{0:T(128)} %slots_far.1, ...), custom_call_target="tpu_custom_call" | custom-call | bytes 262144 | tf_op jit(solution)/shard_map/pallas_call | solution.py:238
  3.0 7.0 %collective-permute-start.10 = (bf16[48,4096]{1,0:T(8,128)(2,1)S(1)}, bf16[48,4096]{1,0:T(8,128)(2,1)S(1)}, u32[]{:S(2)}, u32[]{:S(2)}) collective-permute-start(bf16[48,4096]{1,0:T(8,128)(2,1)S(1)} %get-tuple-element.24), channel_id=1, source_target_pairs={{0,24},{24,0},{1,25},{25,1},{2,26},{26,2},{3,27},{27,3},{4,28},{28... | collective-permute-start | bytes 1179656 | tf_op jit(solution)/shard_map/ppermute | solution.py:261
  10.0 0.1 collective-permute-start.9
  10.1 0.7 %collective-permute-start.6 = (s32[2,64]{1,0:T(2,128)S(1)}, s32[2,64]{1,0:T(2,128)S(1)}, u32[]{:S(2)}, u32[]{:S(2)}) collective-permute-start(s32[2,64]{1,0:T(2,128)S(1)} %get-tuple-element.19), channel_id=1, source_target_pairs={{8,16},{16,8},{9,17},{17,9},{10,18},{18,10},{11,19},{19,11},{12,20... | collective-permute-start | bytes 1544 | tf_op jit(solution)/shard_map/ppermute | solution.py:249
  10.8 18.6 %collective-permute-start.8 = (bf16[48,4096]{1,0:T(8,128)(2,1)S(1)}, bf16[48,4096]{1,0:T(8,128)(2,1)S(1)}, u32[]{:S(2)}, u32[]{:S(2)}) collective-permute-start(bf16[48,4096]{1,0:T(8,128)(2,1)S(1)} %get-tuple-element.21), channel_id=1, source_target_pairs={{0,16},{8,0},{16,24},{24,8},{1,17},{9,1},{17,25},{25,9},{2,18},{10... | collective-permute-start | bytes 1179656 | tf_op jit(solution)/shard_map/ppermute | solution.py:269
  29.4 2.8 %copy-done = bf16[3,256,4096]{2,1,0:T(8,128)(2,1)S(1)} copy-done((bf16[3,256,4096]{2,1,0:T(8,128)(2,1)S(1)}, bf16[3,256,4096]{2,1,0:T(8,128)(2,1)}, u32[]{:S(2)}) %copy-start) | copy-done | bytes 6291480
  32.2 1.9 %shard_map.89 = (f32[4,4,16,128]{3,2,1,0:T(8,128)S(1)}, f32[4,4,16,128]{3,2,1,0:T(8,128)S(1)}) custom-call(s32[1]{0:T(128)} %bitcast.me, s32[1]{0:T(128)} %bitcast.7.core, bf16[3,256,4096]{2,1,0:T(8,128)(2,1)S(1)} %copy-done, bf16[48,4096]{1,0:T(8,128)(2,1)S(1)} %get-tuple-element.25.refs_0_), custom_call_target="tpu_custom_call" | custom-call | flops 805306368 | bytes 262144 | tf_op jit(solution)/shard_map/pallas_call | solution.py:289
  34.1 3.1 %collective-permute-done = bf16[1,8,1024]{2,1,0:T(8,128)(2,1)S(1)} collective-permute-done((bf16[1,8,1024]{2,1,0:T(8,128)(2,1)}, bf16[1,8,1024]{2,1,0:T(8,128)(2,1)S(1)}, u32[]{:S(2)}, u32[]{:S(2)}) %collective-permute-start) | collective-permute-done | bytes 16416 | tf_op jit(solution)/shard_map/ppermute | solution.py:210
  37.2 2.4 %collective-permute-start.1 = (bf16[2,8,1024]{2,1,0:T(8,128)(2,1)S(1)}, bf16[2,8,1024]{2,1,0:T(8,128)(2,1)S(1)}, u32[]{:S(2)}, u32[]{:S(2)}) collective-permute-start(bf16[2,8,1024]{2,1,0:T(8,128)(2,1)S(1)} %pad_maximum_fusion.2), channel_id=1, source_target_pairs={{0,16},{8,24},{16,0},{24,8},{1,17},{9,25},{17,1},{25,9},{2,18},{10... | collective-permute-start | bytes 98312 | tf_op jit(solution)/shard_map/ppermute | solution.py:210
  39.7 2.0 %shard_map.90 = (f32[4,4,16,128]{3,2,1,0:T(8,128)S(1)}, f32[4,4,16,128]{3,2,1,0:T(8,128)S(1)}) custom-call(s32[1]{0:T(128)} %bitcast.me, s32[1]{0:T(128)} %bitcast.7.core, bf16[3,256,4096]{2,1,0:T(8,128)(2,1)S(1)} %copy-done.1, bf16[48,4096]{1,0:T(8,128)(2,1)S(1)} %collective-permute-done.9.refs_0_, ...), custom_call_target="tpu_custom_call", output_to_operand_aliasing={{0}: (6, {}), {1}: (7, {})} | custom-call | flops 805306368 | bytes 262144 | tf_op jit(solution)/shard_map/pallas_call | solution.py:289
  41.7 1.1 %shard_map.92 = f32[4,4,16,128]{3,2,1,0:T(8,128)S(1)} custom-call(s32[1]{0:T(128)} %bitcast.me, s32[1]{0:T(128)} %bitcast.7.core, bf16[3,256,4096]{2,1,0:T(8,128)(2,1)S(1)} %copy-done.1, bf16[48,4096]{1,0:T(8,128)(2,1)S(1)} %collective-permute-done.8.rows, f32[4,4,16,128]{3,2,1,0:T(8,128)S(1)} %get-tuple-element.29._), custom_call_target="tpu_custom_call", output_to_operand_aliasing={{}: (4, {})} | custom-call | flops 402653184 | bytes 262144 | tf_op jit(solution)/shard_map/pallas_call | solution.py:300
  42.8 0.1 collective-permute-start.11
  43.0 0.5 collective-permute-start.2
  43.5 1.1 %shard_map.91 = f32[4,4,16,128]{3,2,1,0:T(8,128)S(1)} custom-call(s32[1]{0:T(128)} %bitcast.me, s32[1]{0:T(128)} %bitcast.7.core, bf16[3,256,4096]{2,1,0:T(8,128)(2,1)S(1)} %copy-done.1, bf16[48,4096]{1,0:T(8,128)(2,1)S(1)} %collective-permute-done.8.rows, f32[4,4,16,128]{3,2,1,0:T(8,128)S(1)} %get-tuple-element.28._), custom_call_target="tpu_custom_call", output_to_operand_aliasing={{}: (4, {})} | custom-call | flops 402653184 | bytes 262144 | tf_op jit(solution)/shard_map/pallas_call | solution.py:300
  44.7 0.7 %add.7 = f32[4,4,16,128]{3,2,1,0:T(8,128)} add(f32[4,4,16,128]{3,2,1,0:T(8,128)S(1)} %shard_map.91, f32[4,4,16,128]{3,2,1,0:T(8,128)S(1)} %collective-permute-done.11) | non-fusion elementwise | flops 32768 | bytes 393216 | tf_op jit(solution)/shard_map/add | solution.py:312
  45.3 5.7 %all-to-all-start = ((f32[16,16,128]{2,1,0:T(8,128)}), f32[16,16,128]{2,1,0:T(8,128)S(1)}, u32[]{:S(2)}, u32[]{:S(2)}) async-start(f32[16,16,128]{2,1,0:T(8,128)} %bitcast.8), calls=%async_computation | async-start | bytes 262144 | tf_op jit(solution)/shard_map/all_to_all | solution.py:314
  51.1 2.0 %collective-permute-start.3 = (bf16[2,4,8,1024]{3,2,1,0:T(8,128)(2,1)S(1)}, bf16[2,4,8,1024]{3,2,1,0:T(8,128)(2,1)S(1)}, u32[]{:S(2)}, u32[]{:S(2)}) collective-permute-start(bf16[2,4,8,1024]{3,2,1,0:T(8,128)(2,1)S(1)} %pad_maximum_fusion.refs_0_), channel_id=1, source_target_pairs={{0,2},{2,0},{4,6},{6,4},{1,3},{3,1},{5,7},{7,5},{8,10},{10,8},{12,... | collective-permute-start | bytes 393224 | tf_op jit(solution)/shard_map/ppermute | solution.py:215
  53.1 1.5 %collective-permute-start.4 = (bf16[2,4,8,1024]{3,2,1,0:T(8,128)(2,1)S(1)}, bf16[2,4,8,1024]{3,2,1,0:T(8,128)(2,1)S(1)}, u32[]{:S(2)}, u32[]{:S(2)}) collective-permute-start(bf16[2,4,8,1024]{3,2,1,0:T(8,128)(2,1)S(1)} %pad_maximum_fusion.refs_0_), channel_id=1, source_target_pairs={{0,4},{2,6},{4,0},{6,2},{1,5},{3,7},{5,1},{7,3},{8,12},{10,14},{12... | collective-permute-start | bytes 393224 | tf_op jit(solution)/shard_map/ppermute | solution.py:215
  54.6 0.1 collective-permute-start.5
  54.7 4.1 %collective-permute-done.3.refs_1_ = bf16[2,4,8,1024]{3,2,1,0:T(8,128)(2,1)S(1)} collective-permute-done((bf16[2,4,8,1024]{3,2,1,0:T(8,128)(2,1)S(1)}, bf16[2,4,8,1024]{3,2,1,0:T(8,128)(2,1)S(1)}, u32[]{:S(2)}, u32[]{:S(2)}) %collective-permute-start.3) | collective-permute-done | bytes 131104 | tf_op jit(solution)/shard_map/ppermute | solution.py:215
  58.8 2.8 %collective-permute-done.4.refs_2_ = bf16[2,4,8,1024]{3,2,1,0:T(8,128)(2,1)S(1)} collective-permute-done((bf16[2,4,8,1024]{3,2,1,0:T(8,128)(2,1)S(1)}, bf16[2,4,8,1024]{3,2,1,0:T(8,128)(2,1)S(1)}, u32[]{:S(2)}, u32[]{:S(2)}) %collective-permute-start.4) | collective-permute-done | bytes 131104 | tf_op jit(solution)/shard_map/ppermute | solution.py:215
  61.5 1.0 %shard_map.86 = bf16[32,8,256]{2,1,0:T(8,128)(2,1)} custom-call(s32[1]{0:T(128)} %bitcast.me, s32[1]{0:T(128)} %bitcast.1.mine, bf16[256,1024]{1,0:T(8,128)(2,1)S(1)} %copy-done.2, bf16[2,4,8,1024]{3,2,1,0:T(8,128)(2,1)S(1)} %pad_maximum_fusion.refs_0_, bf16[2,4,8,1024]{3,2,1,0:T(8,128)(2,1)S(1)} %collective-permute-done.3.refs_1_, ...), custom_call_target="tpu_custom_call" | custom-call | flops 134217728 | bytes 262144 | tf_op jit(solution)/shard_map/pallas_call | solution.py:276
  62.6 0.9 %shard_map.93 = f32[2,32,64]{2,1,0:T(8,128)} custom-call(s32[1]{0:T(128)} %bitcast.1.mine, s32[2,64]{1,0:T(2,128)S(1)} %get-tuple-element.16.lines, s32[2,64]{1,0:T(2,128)S(1)} %get-tuple-element.17.slots, s32[2,64]{1,0:T(2,128)S(1)} %get-tuple-element.18.lives, f32[4,4,16,128]{3,2,1,0:T(8,128)S(1)} %bitcast.12), custom_call_target="tpu_custom_call" | custom-call | bytes 262144 | tf_op jit(solution)/shard_map/pallas_call | solution.py:317
  (22 shorter events, 0.1 us)
Async XLA Ops:
  0.6 36.6 %copy-start.3 = (bf16[8,1024]{1,0:T(8,128)(2,1)S(1)}, bf16[8,1024]{1,0:T(8,128)(2,1)}, u32[]{:S(2)}) copy-start(bf16[8,1024]{1,0:T(8,128)(2,1)} %param.7) | copy-start | bytes 49156
  0.6 10.1 %collective-permute-start.7 = (bf16[64,4096]{1,0:T(8,128)(2,1)}, bf16[64,4096]{1,0:T(8,128)(2,1)S(1)}, u32[]{:S(2)}, u32[]{:S(2)}) collective-permute-start(bf16[64,4096]{1,0:T(8,128)(2,1)} %rows_far.1), channel_id=1, source_target_pairs={{8,16},{16,8},{9,17},{17,9},{10,18},{18,10},{11,19},{19,11},{12,20... | collective-permute-start | bytes 1572872 | tf_op jit(solution)/shard_map/ppermute | solution.py:232
  3.0 36.6 %collective-permute-start.10 = (bf16[48,4096]{1,0:T(8,128)(2,1)S(1)}, bf16[48,4096]{1,0:T(8,128)(2,1)S(1)}, u32[]{:S(2)}, u32[]{:S(2)}) collective-permute-start(bf16[48,4096]{1,0:T(8,128)(2,1)S(1)} %get-tuple-element.24), channel_id=1, source_target_pairs={{0,24},{24,0},{1,25},{25,1},{2,26},{26,2},{3,27},{27,3},{4,28},{28... | collective-permute-start | bytes 1179656 | tf_op jit(solution)/shard_map/ppermute | solution.py:261
  10.0 29.7 %collective-permute-start.9 = (bf16[48,4096]{1,0:T(8,128)(2,1)S(1)}, bf16[48,4096]{1,0:T(8,128)(2,1)S(1)}, u32[]{:S(2)}, u32[]{:S(2)}) collective-permute-start(bf16[48,4096]{1,0:T(8,128)(2,1)S(1)} %get-tuple-element.22), channel_id=1, source_target_pairs={{0,8},{8,0},{16,24},{24,16},{1,9},{9,1},{17,25},{25,17},{2,10},{10... | collective-permute-start | bytes 1179656 | tf_op jit(solution)/shard_map/ppermute | solution.py:210
  10.1 0.7 %collective-permute-start.6 = (s32[2,64]{1,0:T(2,128)S(1)}, s32[2,64]{1,0:T(2,128)S(1)}, u32[]{:S(2)}, u32[]{:S(2)}) collective-permute-start(s32[2,64]{1,0:T(2,128)S(1)} %get-tuple-element.19), channel_id=1, source_target_pairs={{8,16},{16,8},{9,17},{17,9},{10,18},{18,10},{11,19},{19,11},{12,20... | collective-permute-start | bytes 1544 | tf_op jit(solution)/shard_map/ppermute | solution.py:249
  10.8 30.9 %collective-permute-start.8 = (bf16[48,4096]{1,0:T(8,128)(2,1)S(1)}, bf16[48,4096]{1,0:T(8,128)(2,1)S(1)}, u32[]{:S(2)}, u32[]{:S(2)}) collective-permute-start(bf16[48,4096]{1,0:T(8,128)(2,1)S(1)} %get-tuple-element.21), channel_id=1, source_target_pairs={{0,16},{8,0},{16,24},{24,8},{1,17},{9,1},{17,25},{25,9},{2,18},{10... | collective-permute-start | bytes 1179656 | tf_op jit(solution)/shard_map/ppermute | solution.py:269
  29.4 7.8 %collective-permute-start = (bf16[1,8,1024]{2,1,0:T(8,128)(2,1)}, bf16[1,8,1024]{2,1,0:T(8,128)(2,1)S(1)}, u32[]{:S(2)}, u32[]{:S(2)}) collective-permute-start(bf16[1,8,1024]{2,1,0:T(8,128)(2,1)} %bitcast.14), channel_id=1, source_target_pairs={{0,8},{8,0},{16,24},{24,16},{1,9},{9,1},{17,25},{25,17},{2,10},{10... | collective-permute-start | bytes 49160 | tf_op jit(solution)/shard_map/ppermute | solution.py:210
  29.4 2.8 %copy-start = (bf16[3,256,4096]{2,1,0:T(8,128)(2,1)S(1)}, bf16[3,256,4096]{2,1,0:T(8,128)(2,1)}, u32[]{:S(2)}) copy-start(bf16[3,256,4096]{2,1,0:T(8,128)(2,1)} %members.7) | copy-start | bytes 18874372
  32.2 7.5 %copy-start.1 = (bf16[3,256,4096]{2,1,0:T(8,128)(2,1)S(1)}, bf16[3,256,4096]{2,1,0:T(8,128)(2,1)}, u32[]{:S(2)}) copy-start(bf16[3,256,4096]{2,1,0:T(8,128)(2,1)} %members.7) | copy-start | bytes 18874372
  37.2 5.7 %collective-permute-start.1 = (bf16[2,8,1024]{2,1,0:T(8,128)(2,1)S(1)}, bf16[2,8,1024]{2,1,0:T(8,128)(2,1)S(1)}, u32[]{:S(2)}, u32[]{:S(2)}) collective-permute-start(bf16[2,8,1024]{2,1,0:T(8,128)(2,1)S(1)} %pad_maximum_fusion.2), channel_id=1, source_target_pairs={{0,16},{8,24},{16,0},{24,8},{1,17},{9,25},{17,1},{25,9},{2,18},{10... | collective-permute-start | bytes 98312 | tf_op jit(solution)/shard_map/ppermute | solution.py:210
  41.7 19.9 %copy-start.2 = (bf16[256,1024]{1,0:T(8,128)(2,1)S(1)}, bf16[256,1024]{1,0:T(8,128)(2,1)}, u32[]{:S(2)}) copy-start(bf16[256,1024]{1,0:T(8,128)(2,1)} %reps.1) | copy-start | bytes 1572868
  42.8 1.8 %collective-permute-start.11 = (f32[4,4,16,128]{3,2,1,0:T(8,128)S(1)}, f32[4,4,16,128]{3,2,1,0:T(8,128)S(1)}, u32[]{:S(2)}, u32[]{:S(2)}) collective-permute-start(f32[4,4,16,128]{3,2,1,0:T(8,128)S(1)} %shard_map.92), channel_id=1, source_target_pairs={{0,1},{1,0},{2,3},{3,2},{4,5},{5,4},{6,7},{7,6},{8,9},{9,8},{10,11... | collective-permute-start | bytes 393224 | tf_op jit(solution)/shard_map/ppermute | solution.py:214
  43.0 8.1 %collective-permute-start.2 = (bf16[4,8,1024]{2,1,0:T(8,128)(2,1)S(1)}, bf16[4,8,1024]{2,1,0:T(8,128)(2,1)S(1)}, u32[]{:S(2)}, u32[]{:S(2)}) collective-permute-start(bf16[4,8,1024]{2,1,0:T(8,128)(2,1)S(1)} %get-tuple-element.31), channel_id=1, source_target_pairs={{0,1},{1,0},{2,3},{3,2},{4,5},{5,4},{6,7},{7,6},{8,9},{9,8},{10,11... | collective-permute-start | bytes 196616 | tf_op jit(solution)/shard_map/ppermute | solution.py:214
  45.3 17.2 %all-to-all-start = ((f32[16,16,128]{2,1,0:T(8,128)}), f32[16,16,128]{2,1,0:T(8,128)S(1)}, u32[]{:S(2)}, u32[]{:S(2)}) async-start(f32[16,16,128]{2,1,0:T(8,128)} %bitcast.8), calls=%async_computation | async-start | bytes 262144 | tf_op jit(solution)/shard_map/all_to_all | solution.py:314
  51.1 7.7 %collective-permute-start.3 = (bf16[2,4,8,1024]{3,2,1,0:T(8,128)(2,1)S(1)}, bf16[2,4,8,1024]{3,2,1,0:T(8,128)(2,1)S(1)}, u32[]{:S(2)}, u32[]{:S(2)}) collective-permute-start(bf16[2,4,8,1024]{3,2,1,0:T(8,128)(2,1)S(1)} %pad_maximum_fusion.refs_0_), channel_id=1, source_target_pairs={{0,2},{2,0},{4,6},{6,4},{1,3},{3,1},{5,7},{7,5},{8,10},{10,8},{12,... | collective-permute-start | bytes 393224 | tf_op jit(solution)/shard_map/ppermute | solution.py:215
  53.1 8.5 %collective-permute-start.4 = (bf16[2,4,8,1024]{3,2,1,0:T(8,128)(2,1)S(1)}, bf16[2,4,8,1024]{3,2,1,0:T(8,128)(2,1)S(1)}, u32[]{:S(2)}, u32[]{:S(2)}) collective-permute-start(bf16[2,4,8,1024]{3,2,1,0:T(8,128)(2,1)S(1)} %pad_maximum_fusion.refs_0_), channel_id=1, source_target_pairs={{0,4},{2,6},{4,0},{6,2},{1,5},{3,7},{5,1},{7,3},{8,12},{10,14},{12... | collective-permute-start | bytes 393224 | tf_op jit(solution)/shard_map/ppermute | solution.py:215
  54.6 7.0 %collective-permute-start.5 = (bf16[2,4,8,1024]{3,2,1,0:T(8,128)(2,1)S(1)}, bf16[2,4,8,1024]{3,2,1,0:T(8,128)(2,1)S(1)}, u32[]{:S(2)}, u32[]{:S(2)}) collective-permute-start(bf16[2,4,8,1024]{3,2,1,0:T(8,128)(2,1)S(1)} %pad_maximum_fusion.refs_0_), channel_id=1, source_target_pairs={{0,6},{2,4},{4,2},{6,0},{1,7},{3,5},{5,3},{7,1},{8,14},{10,12},{12... | collective-permute-start | bytes 393224 | tf_op jit(solution)/shard_map/ppermute | solution.py:215

commit v7 on v6

--- a/solution.py
+++ b/solution.py
@@ -141,19 +141,18 @@
             out[(me[0] ^ (at % groups)) * mems + member] = score[at * each : (at + 1) * each]
 
 
-def half_kernel(key, other, me, core, members, rows, _, out, acc):
+def half_kernel(key, other, me, core, members, rows, _, out):
     slot_count, chips = members.shape[0], out.shape[1]
     block = members.shape[1] // (2 * chips)
     starts = [pl.multiple_of((chip * 2 + (core[0] ^ other)) * block, block) for chip in range(chips)]
     for s in range(slot_count):
         half = jnp.concatenate([members[s, pl.ds(start, block), :] for start in starts], axis=0)
         product = lax.dot_general(
-            half, rows[s * MOST : (s + 1) * MOST, :], NT, preferred_element_type=jnp.float32
+            rows[s * MOST : (s + 1) * MOST, :], half, NT, preferred_element_type=jnp.float32
         )
-        acc[...] = product.T
         for chip in range(chips):
             out[me[0] ^ key, chip, :, s * block : (s + 1) * block] = (
-                acc[:, chip * block : (chip + 1) * block]
+                product[:, chip * block : (chip + 1) * block]
             )
 
 
@@ -299,7 +298,7 @@
         def one_side(key, other, out):
             (out,) = call(
                 functools.partial(half_kernel, key, other), [shape], [SM] * 2 + [VM] * 3,
-                scratch=[pltpu.VMEM((MOST, members // 2), f32)], mib=2,
+                mib=2,
                 flops=members * width_here * count * 8, alias=[(4, 0)],
             )(me1, core1, member_profile, got[key], out)
             return out

time: 63.8 us -> 63.5 us (level)
  no operation moved by 1% of the time
where the time goes in v7:
time: 63.5 us; the launch traced here: 63.2 us
  starting transfers between devices  39.3 us (62%)
  waiting for transfers between devices  10 us (16%)
  Pallas kernels  9.52 us (15%)
  local copies, waits for them, and re-layouts  2.8 us (4%)
  between operations  0.82 us (1%)
  other arithmetic  0.7 us (1%)
    ppermute x1, starting transfers between devices, local(): got[k] = lax.ppermute(onward[at], 'grp', way)  18.6 us
    ppermute x1, starting transfers between devices, local(): direct = lax.ppermute(picked[last], 'grp', outer)  6.99 us
    ppermute x3, waiting for transfers between devices, swap_mem(): lax.ppermute(value, 'chip', [(i, i ^ key // 2) for i in range(chips)])  6.88 us
    all_to_all x1, starting transfers between devices, local(): parts = lax.all_to_all(parts, ('grp', 'chip'), 0, 0, tiled=True)  5.73 us
    pallas_call x2, Pallas kernels, local(): call(functools.partial(score_kernel, keys, last), [shape] * 2, [SM] * 2 +...  3.93 us
    ppermute x3, starting transfers between devices, swap_mem(): lax.ppermute(value, 'chip', [(i, i ^ key // 2) for i in range(chips)])  3.55 us
    ppermute x3, waiting for transfers between devices, swap(): return lax.ppermute(value, 'grp', [(i, i ^ key) for i in range(groups)])  3.1 us
    unnamed x8, local copies, waits for them, and re-layouts  2.8 us
  transfers between devices with their start and end apart: 13, of which 3 were waited for; matrix products, arithmetic and copies ran while one was open for 1% of the time, Pallas kernels for 14%

profile of v7, /device:TPU:0, one launch (start us, length us, event | category | flops | bytes accessed | tf_op | source)
XLA Modules:
  0.0 63.2 jit_solution(9799603313754837907)
XLA Ops:
  0.6 0.7 %collective-permute-start.7 = (bf16[64,4096]{1,0:T(8,128)(2,1)}, bf16[64,4096]{1,0:T(8,128)(2,1)S(1)}, u32[]{:S(2)}, u32[]{:S(2)}) collective-permute-start(bf16[64,4096]{1,0:T(8,128)(2,1)} %rows_far.1), channel_id=1, source_target_pairs={{8,16},{16,8},{9,17},{17,9},{10,18},{18,10},{11,19},{19,11},{12,20... | collective-permute-start | bytes 1572872 | tf_op jit(solution)/shard_map/ppermute | solution.py:231
  1.4 1.6 %shard_map.87 = (s32[2,64]{1,0:T(2,128)S(1)}, s32[2,64]{1,0:T(2,128)S(1)}, s32[2,64]{1,0:T(2,128)S(1)}, s32[2,64]{1,0:T(2,128)S(1)}, bf16[48,4096]{1,0:T(8,128)(...) custom-call(s32[1]{0:T(128)} %bitcast.me, s32[12]{0:T(128)} %slots_far.1, ...), custom_call_target="tpu_custom_call" | custom-call | bytes 262144 | tf_op jit(solution)/shard_map/pallas_call | solution.py:237
  3.0 7.0 %collective-permute-start.10 = (bf16[48,4096]{1,0:T(8,128)(2,1)S(1)}, bf16[48,4096]{1,0:T(8,128)(2,1)S(1)}, u32[]{:S(2)}, u32[]{:S(2)}) collective-permute-start(bf16[48,4096]{1,0:T(8,128)(2,1)S(1)} %get-tuple-element.24), channel_id=1, source_target_pairs={{0,24},{24,0},{1,25},{25,1},{2,26},{26,2},{3,27},{27,3},{4,28},{28... | collective-permute-start | bytes 1179656 | tf_op jit(solution)/shard_map/ppermute | solution.py:260
  10.0 0.1 collective-permute-start.9
  10.1 0.7 %collective-permute-start.6 = (s32[2,64]{1,0:T(2,128)S(1)}, s32[2,64]{1,0:T(2,128)S(1)}, u32[]{:S(2)}, u32[]{:S(2)}) collective-permute-start(s32[2,64]{1,0:T(2,128)S(1)} %get-tuple-element.19), channel_id=1, source_target_pairs={{8,16},{16,8},{9,17},{17,9},{10,18},{18,10},{11,19},{19,11},{12,20... | collective-permute-start | bytes 1544 | tf_op jit(solution)/shard_map/ppermute | solution.py:248
  10.8 18.6 %collective-permute-start.8 = (bf16[48,4096]{1,0:T(8,128)(2,1)S(1)}, bf16[48,4096]{1,0:T(8,128)(2,1)S(1)}, u32[]{:S(2)}, u32[]{:S(2)}) collective-permute-start(bf16[48,4096]{1,0:T(8,128)(2,1)S(1)} %get-tuple-element.21), channel_id=1, source_target_pairs={{0,16},{8,0},{16,24},{24,8},{1,17},{9,1},{17,25},{25,9},{2,18},{10... | collective-permute-start | bytes 1179656 | tf_op jit(solution)/shard_map/ppermute | solution.py:268
  29.4 2.8 %copy-done = bf16[3,256,4096]{2,1,0:T(8,128)(2,1)S(1)} copy-done((bf16[3,256,4096]{2,1,0:T(8,128)(2,1)S(1)}, bf16[3,256,4096]{2,1,0:T(8,128)(2,1)}, u32[]{:S(2)}) %copy-start) | copy-done | bytes 6291480
  32.2 1.9 %shard_map.89 = (f32[4,4,16,128]{3,2,1,0:T(8,128)S(1)}, f32[4,4,16,128]{3,2,1,0:T(8,128)S(1)}) custom-call(s32[1]{0:T(128)} %bitcast.me, s32[1]{0:T(128)} %bitcast.7.core, bf16[3,256,4096]{2,1,0:T(8,128)(2,1)S(1)} %copy-done, bf16[48,4096]{1,0:T(8,128)(2,1)S(1)} %get-tuple-element.25.refs_0_), custom_call_target="tpu_custom_call" | custom-call | flops 805306368 | bytes 262144 | tf_op jit(solution)/shard_map/pallas_call | solution.py:288
  34.1 3.1 %collective-permute-done = bf16[1,8,1024]{2,1,0:T(8,128)(2,1)S(1)} collective-permute-done((bf16[1,8,1024]{2,1,0:T(8,128)(2,1)}, bf16[1,8,1024]{2,1,0:T(8,128)(2,1)S(1)}, u32[]{:S(2)}, u32[]{:S(2)}) %collective-permute-start) | collective-permute-done | bytes 16416 | tf_op jit(solution)/shard_map/ppermute | solution.py:209
  37.2 2.4 %collective-permute-start.1 = (bf16[2,8,1024]{2,1,0:T(8,128)(2,1)S(1)}, bf16[2,8,1024]{2,1,0:T(8,128)(2,1)S(1)}, u32[]{:S(2)}, u32[]{:S(2)}) collective-permute-start(bf16[2,8,1024]{2,1,0:T(8,128)(2,1)S(1)} %pad_maximum_fusion.2), channel_id=1, source_target_pairs={{0,16},{8,24},{16,0},{24,8},{1,17},{9,25},{17,1},{25,9},{2,18},{10... | collective-permute-start | bytes 98312 | tf_op jit(solution)/shard_map/ppermute | solution.py:209
  39.7 2.0 %shard_map.90 = (f32[4,4,16,128]{3,2,1,0:T(8,128)S(1)}, f32[4,4,16,128]{3,2,1,0:T(8,128)S(1)}) custom-call(s32[1]{0:T(128)} %bitcast.me, s32[1]{0:T(128)} %bitcast.7.core, bf16[3,256,4096]{2,1,0:T(8,128)(2,1)S(1)} %copy-done.1, bf16[48,4096]{1,0:T(8,128)(2,1)S(1)} %collective-permute-done.9.refs_0_, ...), custom_call_target="tpu_custom_call", output_to_operand_aliasing={{0}: (6, {}), {1}: (7, {})} | custom-call | flops 805306368 | bytes 262144 | tf_op jit(solution)/shard_map/pallas_call | solution.py:288
  41.7 1.0 %shard_map.92 = f32[4,4,16,128]{3,2,1,0:T(8,128)S(1)} custom-call(s32[1]{0:T(128)} %bitcast.me, s32[1]{0:T(128)} %bitcast.7.core, bf16[3,256,4096]{2,1,0:T(8,128)(2,1)S(1)} %copy-done.1, bf16[48,4096]{1,0:T(8,128)(2,1)S(1)} %collective-permute-done.8.rows, f32[4,4,16,128]{3,2,1,0:T(8,128)S(1)} %get-tuple-element.29._), custom_call_target="tpu_custom_call", output_to_operand_aliasing={{}: (4, {})} | custom-call | flops 402653184 | bytes 262144 | tf_op jit(solution)/shard_map/pallas_call | solution.py:299
  42.7 0.1 collective-permute-start.11
  42.8 0.5 collective-permute-start.2
  43.4 1.0 %shard_map.91 = f32[4,4,16,128]{3,2,1,0:T(8,128)S(1)} custom-call(s32[1]{0:T(128)} %bitcast.me, s32[1]{0:T(128)} %bitcast.7.core, bf16[3,256,4096]{2,1,0:T(8,128)(2,1)S(1)} %copy-done.1, bf16[48,4096]{1,0:T(8,128)(2,1)S(1)} %collective-permute-done.8.rows, f32[4,4,16,128]{3,2,1,0:T(8,128)S(1)} %get-tuple-element.28._), custom_call_target="tpu_custom_call", output_to_operand_aliasing={{}: (4, {})} | custom-call | flops 402653184 | bytes 262144 | tf_op jit(solution)/shard_map/pallas_call | solution.py:299
  44.4 0.7 %add.7 = f32[4,4,16,128]{3,2,1,0:T(8,128)} add(f32[4,4,16,128]{3,2,1,0:T(8,128)S(1)} %shard_map.91, f32[4,4,16,128]{3,2,1,0:T(8,128)S(1)} %collective-permute-done.11) | non-fusion elementwise | flops 32768 | bytes 393216 | tf_op jit(solution)/shard_map/add | solution.py:311
  45.1 5.7 %all-to-all-start = ((f32[16,16,128]{2,1,0:T(8,128)}), f32[16,16,128]{2,1,0:T(8,128)S(1)}, u32[]{:S(2)}, u32[]{:S(2)}) async-start(f32[16,16,128]{2,1,0:T(8,128)} %bitcast.8), calls=%async_computation | async-start | bytes 262144 | tf_op jit(solution)/shard_map/all_to_all | solution.py:313
  50.8 2.0 %collective-permute-start.3 = (bf16[2,4,8,1024]{3,2,1,0:T(8,128)(2,1)S(1)}, bf16[2,4,8,1024]{3,2,1,0:T(8,128)(2,1)S(1)}, u32[]{:S(2)}, u32[]{:S(2)}) collective-permute-start(bf16[2,4,8,1024]{3,2,1,0:T(8,128)(2,1)S(1)} %pad_maximum_fusion.refs_0_), channel_id=1, source_target_pairs={{0,2},{2,0},{4,6},{6,4},{1,3},{3,1},{5,7},{7,5},{8,10},{10,8},{12,... | collective-permute-start | bytes 393224 | tf_op jit(solution)/shard_map/ppermute | solution.py:214
  52.8 1.5 %collective-permute-start.4 = (bf16[2,4,8,1024]{3,2,1,0:T(8,128)(2,1)S(1)}, bf16[2,4,8,1024]{3,2,1,0:T(8,128)(2,1)S(1)}, u32[]{:S(2)}, u32[]{:S(2)}) collective-permute-start(bf16[2,4,8,1024]{3,2,1,0:T(8,128)(2,1)S(1)} %pad_maximum_fusion.refs_0_), channel_id=1, source_target_pairs={{0,4},{2,6},{4,0},{6,2},{1,5},{3,7},{5,1},{7,3},{8,12},{10,14},{12... | collective-permute-start | bytes 393224 | tf_op jit(solution)/shard_map/ppermute | solution.py:214
  54.3 0.1 collective-permute-start.5
  54.4 4.1 %collective-permute-done.3.refs_1_ = bf16[2,4,8,1024]{3,2,1,0:T(8,128)(2,1)S(1)} collective-permute-done((bf16[2,4,8,1024]{3,2,1,0:T(8,128)(2,1)S(1)}, bf16[2,4,8,1024]{3,2,1,0:T(8,128)(2,1)S(1)}, u32[]{:S(2)}, u32[]{:S(2)}) %collective-permute-start.3) | collective-permute-done | bytes 131104 | tf_op jit(solution)/shard_map/ppermute | solution.py:214
  58.5 2.8 %collective-permute-done.4.refs_2_ = bf16[2,4,8,1024]{3,2,1,0:T(8,128)(2,1)S(1)} collective-permute-done((bf16[2,4,8,1024]{3,2,1,0:T(8,128)(2,1)S(1)}, bf16[2,4,8,1024]{3,2,1,0:T(8,128)(2,1)S(1)}, u32[]{:S(2)}, u32[]{:S(2)}) %collective-permute-start.4) | collective-permute-done | bytes 131104 | tf_op jit(solution)/shard_map/ppermute | solution.py:214
  61.3 1.0 %shard_map.86 = bf16[32,8,256]{2,1,0:T(8,128)(2,1)} custom-call(s32[1]{0:T(128)} %bitcast.me, s32[1]{0:T(128)} %bitcast.1.mine, bf16[256,1024]{1,0:T(8,128)(2,1)S(1)} %copy-done.2, bf16[2,4,8,1024]{3,2,1,0:T(8,128)(2,1)S(1)} %pad_maximum_fusion.refs_0_, bf16[2,4,8,1024]{3,2,1,0:T(8,128)(2,1)S(1)} %collective-permute-done.3.refs_1_, ...), custom_call_target="tpu_custom_call" | custom-call | flops 134217728 | bytes 262144 | tf_op jit(solution)/shard_map/pallas_call | solution.py:275
  62.3 0.9 %shard_map.93 = f32[2,32,64]{2,1,0:T(8,128)} custom-call(s32[1]{0:T(128)} %bitcast.1.mine, s32[2,64]{1,0:T(2,128)S(1)} %get-tuple-element.16.lines, s32[2,64]{1,0:T(2,128)S(1)} %get-tuple-element.17.slots, s32[2,64]{1,0:T(2,128)S(1)} %get-tuple-element.18.lives, f32[4,4,16,128]{3,2,1,0:T(8,128)S(1)} %bitcast.12), custom_call_target="tpu_custom_call" | custom-call | bytes 262144 | tf_op jit(solution)/shard_map/pallas_call | solution.py:316
  (22 shorter events, 0.1 us)
Async XLA Ops:
  0.6 36.6 %copy-start.3 = (bf16[8,1024]{1,0:T(8,128)(2,1)S(1)}, bf16[8,1024]{1,0:T(8,128)(2,1)}, u32[]{:S(2)}) copy-start(bf16[8,1024]{1,0:T(8,128)(2,1)} %param.7) | copy-start | bytes 49156
  0.6 10.1 %collective-permute-start.7 = (bf16[64,4096]{1,0:T(8,128)(2,1)}, bf16[64,4096]{1,0:T(8,128)(2,1)S(1)}, u32[]{:S(2)}, u32[]{:S(2)}) collective-permute-start(bf16[64,4096]{1,0:T(8,128)(2,1)} %rows_far.1), channel_id=1, source_target_pairs={{8,16},{16,8},{9,17},{17,9},{10,18},{18,10},{11,19},{19,11},{12,20... | collective-permute-start | bytes 1572872 | tf_op jit(solution)/shard_map/ppermute | solution.py:231
  3.0 36.6 %collective-permute-start.10 = (bf16[48,4096]{1,0:T(8,128)(2,1)S(1)}, bf16[48,4096]{1,0:T(8,128)(2,1)S(1)}, u32[]{:S(2)}, u32[]{:S(2)}) collective-permute-start(bf16[48,4096]{1,0:T(8,128)(2,1)S(1)} %get-tuple-element.24), channel_id=1, source_target_pairs={{0,24},{24,0},{1,25},{25,1},{2,26},{26,2},{3,27},{27,3},{4,28},{28... | collective-permute-start | bytes 1179656 | tf_op jit(solution)/shard_map/ppermute | solution.py:260
  10.0 29.7 %collective-permute-start.9 = (bf16[48,4096]{1,0:T(8,128)(2,1)S(1)}, bf16[48,4096]{1,0:T(8,128)(2,1)S(1)}, u32[]{:S(2)}, u32[]{:S(2)}) collective-permute-start(bf16[48,4096]{1,0:T(8,128)(2,1)S(1)} %get-tuple-element.22), channel_id=1, source_target_pairs={{0,8},{8,0},{16,24},{24,16},{1,9},{9,1},{17,25},{25,17},{2,10},{10... | collective-permute-start | bytes 1179656 | tf_op jit(solution)/shard_map/ppermute | solution.py:209
  10.1 0.7 %collective-permute-start.6 = (s32[2,64]{1,0:T(2,128)S(1)}, s32[2,64]{1,0:T(2,128)S(1)}, u32[]{:S(2)}, u32[]{:S(2)}) collective-permute-start(s32[2,64]{1,0:T(2,128)S(1)} %get-tuple-element.19), channel_id=1, source_target_pairs={{8,16},{16,8},{9,17},{17,9},{10,18},{18,10},{11,19},{19,11},{12,20... | collective-permute-start | bytes 1544 | tf_op jit(solution)/shard_map/ppermute | solution.py:248
  10.8 30.9 %collective-permute-start.8 = (bf16[48,4096]{1,0:T(8,128)(2,1)S(1)}, bf16[48,4096]{1,0:T(8,128)(2,1)S(1)}, u32[]{:S(2)}, u32[]{:S(2)}) collective-permute-start(bf16[48,4096]{1,0:T(8,128)(2,1)S(1)} %get-tuple-element.21), channel_id=1, source_target_pairs={{0,16},{8,0},{16,24},{24,8},{1,17},{9,1},{17,25},{25,9},{2,18},{10... | collective-permute-start | bytes 1179656 | tf_op jit(solution)/shard_map/ppermute | solution.py:268
  29.4 7.8 %collective-permute-start = (bf16[1,8,1024]{2,1,0:T(8,128)(2,1)}, bf16[1,8,1024]{2,1,0:T(8,128)(2,1)S(1)}, u32[]{:S(2)}, u32[]{:S(2)}) collective-permute-start(bf16[1,8,1024]{2,1,0:T(8,128)(2,1)} %bitcast.14), channel_id=1, source_target_pairs={{0,8},{8,0},{16,24},{24,16},{1,9},{9,1},{17,25},{25,17},{2,10},{10... | collective-permute-start | bytes 49160 | tf_op jit(solution)/shard_map/ppermute | solution.py:209
  29.4 2.8 %copy-start = (bf16[3,256,4096]{2,1,0:T(8,128)(2,1)S(1)}, bf16[3,256,4096]{2,1,0:T(8,128)(2,1)}, u32[]{:S(2)}) copy-start(bf16[3,256,4096]{2,1,0:T(8,128)(2,1)} %members.7) | copy-start | bytes 18874372
  32.2 7.5 %copy-start.1 = (bf16[3,256,4096]{2,1,0:T(8,128)(2,1)S(1)}, bf16[3,256,4096]{2,1,0:T(8,128)(2,1)}, u32[]{:S(2)}) copy-start(bf16[3,256,4096]{2,1,0:T(8,128)(2,1)} %members.7) | copy-start | bytes 18874372
  37.2 5.6 %collective-permute-start.1 = (bf16[2,8,1024]{2,1,0:T(8,128)(2,1)S(1)}, bf16[2,8,1024]{2,1,0:T(8,128)(2,1)S(1)}, u32[]{:S(2)}, u32[]{:S(2)}) collective-permute-start(bf16[2,8,1024]{2,1,0:T(8,128)(2,1)S(1)} %pad_maximum_fusion.2), channel_id=1, source_target_pairs={{0,16},{8,24},{16,0},{24,8},{1,17},{9,25},{17,1},{25,9},{2,18},{10... | collective-permute-start | bytes 98312 | tf_op jit(solution)/shard_map/ppermute | solution.py:209
  41.7 19.6 %copy-start.2 = (bf16[256,1024]{1,0:T(8,128)(2,1)S(1)}, bf16[256,1024]{1,0:T(8,128)(2,1)}, u32[]{:S(2)}) copy-start(bf16[256,1024]{1,0:T(8,128)(2,1)} %reps.1) | copy-start | bytes 1572868
  42.7 1.7 %collective-permute-start.11 = (f32[4,4,16,128]{3,2,1,0:T(8,128)S(1)}, f32[4,4,16,128]{3,2,1,0:T(8,128)S(1)}, u32[]{:S(2)}, u32[]{:S(2)}) collective-permute-start(f32[4,4,16,128]{3,2,1,0:T(8,128)S(1)} %shard_map.92), channel_id=1, source_target_pairs={{0,1},{1,0},{2,3},{3,2},{4,5},{5,4},{6,7},{7,6},{8,9},{9,8},{10,11... | collective-permute-start | bytes 393224 | tf_op jit(solution)/shard_map/ppermute | solution.py:213
  42.8 8.0 %collective-permute-start.2 = (bf16[4,8,1024]{2,1,0:T(8,128)(2,1)S(1)}, bf16[4,8,1024]{2,1,0:T(8,128)(2,1)S(1)}, u32[]{:S(2)}, u32[]{:S(2)}) collective-permute-start(bf16[4,8,1024]{2,1,0:T(8,128)(2,1)S(1)} %get-tuple-element.31), channel_id=1, source_target_pairs={{0,1},{1,0},{2,3},{3,2},{4,5},{5,4},{6,7},{7,6},{8,9},{9,8},{10,11... | collective-permute-start | bytes 196616 | tf_op jit(solution)/shard_map/ppermute | solution.py:213
  45.1 17.2 %all-to-all-start = ((f32[16,16,128]{2,1,0:T(8,128)}), f32[16,16,128]{2,1,0:T(8,128)S(1)}, u32[]{:S(2)}, u32[]{:S(2)}) async-start(f32[16,16,128]{2,1,0:T(8,128)} %bitcast.8), calls=%async_computation | async-start | bytes 262144 | tf_op jit(solution)/shard_map/all_to_all | solution.py:313
  50.8 7.7 %collective-permute-start.3 = (bf16[2,4,8,1024]{3,2,1,0:T(8,128)(2,1)S(1)}, bf16[2,4,8,1024]{3,2,1,0:T(8,128)(2,1)S(1)}, u32[]{:S(2)}, u32[]{:S(2)}) collective-permute-start(bf16[2,4,8,1024]{3,2,1,0:T(8,128)(2,1)S(1)} %pad_maximum_fusion.refs_0_), channel_id=1, source_target_pairs={{0,2},{2,0},{4,6},{6,4},{1,3},{3,1},{5,7},{7,5},{8,10},{10,8},{12,... | collective-permute-start | bytes 393224 | tf_op jit(solution)/shard_map/ppermute | solution.py:214
  52.8 8.4 %collective-permute-start.4 = (bf16[2,4,8,1024]{3,2,1,0:T(8,128)(2,1)S(1)}, bf16[2,4,8,1024]{3,2,1,0:T(8,128)(2,1)S(1)}, u32[]{:S(2)}, u32[]{:S(2)}) collective-permute-start(bf16[2,4,8,1024]{3,2,1,0:T(8,128)(2,1)S(1)} %pad_maximum_fusion.refs_0_), channel_id=1, source_target_pairs={{0,4},{2,6},{4,0},{6,2},{1,5},{3,7},{5,1},{7,3},{8,12},{10,14},{12... | collective-permute-start | bytes 393224 | tf_op jit(solution)/shard_map/ppermute | solution.py:214
  54.3 7.0 %collective-permute-start.5 = (bf16[2,4,8,1024]{3,2,1,0:T(8,128)(2,1)S(1)}, bf16[2,4,8,1024]{3,2,1,0:T(8,128)(2,1)S(1)}, u32[]{:S(2)}, u32[]{:S(2)}) collective-permute-start(bf16[2,4,8,1024]{3,2,1,0:T(8,128)(2,1)S(1)} %pad_maximum_fusion.refs_0_), channel_id=1, source_target_pairs={{0,6},{2,4},{4,2},{6,0},{1,7},{3,5},{5,3},{7,1},{8,14},{10,12},{12... | collective-permute-start | bytes 393224 | tf_op jit(solution)/shard_map/ppermute | solution.py:214
